TPU v7x, 32 devices: a whole 2x2x4 slice. The times are simulated.
32 devices in a mesh: seq: 8 (over z, y), chan: 2 (over x), section: 2 (over core).
Axes of the slice: x: 2, y: 2, z: 4, core: 2. Of those that a mesh axis runs over, the one named last changes fastest.
Arguments:
- tokens: bfloat16 [2, 2048, 1024], P(None, 'seq', 'chan'), may hold values from -6 to 6
- in_proj: bfloat16 [2, 1024, 2, 1024], P('section', None, None, 'chan'), may hold values from -0.1875 to 0.1875
- filters: bfloat16 [2, 8, 2304], P('section', 'chan'), may hold values from -0.13183594 to 0.13183594
- out_proj: bfloat16 [2, 1024, 1024], P('section', None, 'chan'), may hold values from -0.1875 to 0.1875
- widths: int32 [2], replicated, may hold values from 1 to 4, as said below
Outputs:
- layer_outputs: bfloat16 [2, 2, 2048, 1024], P('section', None, 'seq', 'chan')
Inputs may be any that keep to these rules, and one draw needn't show every extreme that they name: `widths`: exactly one sequence has width 8 / 2.
All inputs are finite; a program needn't handle non-finite values.
Results may differ from a plain program's by a relative error of at most 0.0077.
Values may be sent and summed in bfloat16 or wider, within the bound.
No kernel may reach another device: no remote copies, remote signals or barrier semaphores. Data moves between devices by JAX's collectives and lax.ppermute only.
A program may use at most 64 MiB of HBM per device.

v0:
```python
import functools

import jax
import jax.numpy as jnp
from jax import lax
from jax.experimental import pallas as pl
from jax.experimental.pallas import tpu as pltpu
from jax.sharding import PartitionSpec as P


BAND = 8
REACH = BAND // 2
MB = 2


VMEM = pl.BlockSpec(memory_space=pltpu.VMEM)
SMEM = pl.BlockSpec(memory_space=pltpu.SMEM)


def call(kernel, outs, specs, flops, moved, grant=12, out_spec=VMEM):
    return pl.pallas_call(
        kernel,
        out_shape=outs,
        in_specs=specs,
        out_specs=jax.tree.map(lambda _: out_spec, outs),
        cost_estimate=pl.CostEstimate(flops=flops, bytes_accessed=moved, transcendentals=0),
        compiler_params=pltpu.CompilerParams(vmem_limit_bytes=grant << 20),
    )


def shape(*dims, dtype=jnp.bfloat16):
    return jax.ShapeDtypeStruct(dims, dtype)


def position():
    count = lax.axis_size("seq")
    place = lax.axis_index("seq")
    sequence = jnp.where(place >= count // 2, 1, 0)
    return sequence, lax.rem(place + lax.axis_index("section") * (count // 2), count)


def lag_of(slot, index):
    if lax.axis_size("seq") == BAND:
        return ((index - (index ^ slot) + REACH) & (BAND - 1)) - REACH
    return slot - REACH


def toeplitz_kernel(block, groups, layer, widths_ref, near_ref, far_ref, *refs):
    outs, flipped_ref = refs[:-1], refs[-1]
    heads, taps = near_ref.shape
    pieces = taps // block
    rows = lax.broadcasted_iota(jnp.int32, (block, block), 0)
    columns = lax.broadcasted_iota(jnp.int32, (block, block), 1)
    turn = (rows + columns == block - 1).astype(jnp.bfloat16)
    own = lax.axis_index("section") == layer
    sequence, index = position()
    width = widths_ref[sequence]
    for piece in range(pieces):
        at = slice(piece * block, (piece + 1) * block)
        taken = jnp.where(own, near_ref[:, at].astype(jnp.float32), far_ref[:, at].astype(jnp.float32))
        turned = jnp.dot(taken.astype(jnp.bfloat16), turn, preferred_element_type=jnp.float32)
        flipped_ref[:, taps - (piece + 1) * block : taps - piece * block] = turned
    for out_ref, slots in zip(outs, groups):
        for place, slot in enumerate(slots):
            lag = lag_of(slot, index)
            start = pl.multiple_of(block * (REACH - 1 - lag), block)
            window = flipped_ref[:, pl.ds(start, 2 * block)]
            band = (lag >= -width) & (lag < width)
            for head in range(heads):
                row = jnp.broadcast_to(window[head : head + 1, :], (block, 2 * block))
                turned = pltpu.roll(row, 1, 1, stride=1, stride_axis=0)[:, block:]
                kept = jnp.where(band, turned, 0.0)
                out_ref[head, :, place * block : (place + 1) * block] = kept.astype(jnp.bfloat16)


def toeplitz(layer, widths, near, far, block, groups):
    heads = near.shape[0]
    outs = tuple(shape(heads, block, len(slots) * block) for slots in groups)
    return pl.pallas_call(
        functools.partial(toeplitz_kernel, block, groups, layer),
        out_shape=outs,
        in_specs=[SMEM, VMEM, VMEM],
        out_specs=(VMEM,) * len(outs),
        scratch_shapes=[pltpu.VMEM(near.shape, jnp.float32)],
        name="toeplitz",
        cost_estimate=pl.CostEstimate(
            flops=heads * BAND * block * block * 40,
            bytes_accessed=heads * BAND * block * block * 2,
            transcendentals=0,
        ),
        compiler_params=pltpu.CompilerParams(vmem_limit_bytes=12 << 20),
    )(widths, near, far)


def mix_kernel(count, last, toeplitz_ref, *refs):
    sources, others, out_ref = refs[:count], refs[count:-1], refs[-1]
    heads = toeplitz_ref.shape[0]
    wide = out_ref.shape[1] // heads
    for head in range(heads):
        lanes = slice(head * wide, (head + 1) * wide)
        stacked = jnp.concatenate([source[:, lanes] for source in sources], axis=0)
        mixed = jnp.dot(toeplitz_ref[head], stacked, preferred_element_type=jnp.float32)
        if len(others) > last:
            mixed += others[-1][:, lanes]
        if last:
            gate = others[0][:, lanes].astype(jnp.float32)
            mixed = gate / (1.0 + jnp.exp(-gate)) * mixed
        out_ref[:, lanes] = mixed.astype(out_ref.dtype)


def mix(toeplitz_blocks, sources, total, gating):
    block, local = sources[0].shape
    last = gating is not None
    others = ([gating] if last else []) + ([total] if total is not None else [])
    return call(
        functools.partial(mix_kernel, len(sources), int(last)),
        shape(block, local, dtype=jnp.bfloat16 if last else jnp.float32),
        [VMEM] * (1 + len(sources) + len(others)),
        2 * len(sources) * block * block * local,
        toeplitz_blocks.size * 2 + (len(sources) + 4) * block * local * 2,
    )(toeplitz_blocks, *sources, *others)


def product(own_ref, peer_ref, weight_ref):
    depth = own_ref.shape[1]
    chan = lax.axis_index("chan")
    own_rows = weight_ref[pl.ds(pl.multiple_of(chan * depth, depth), depth), :]
    peer_rows = weight_ref[pl.ds(pl.multiple_of((1 - chan) * depth, depth), depth), :]
    total = jnp.dot(own_ref[...], own_rows, preferred_element_type=jnp.float32)
    return total + jnp.dot(peer_ref[...], peer_rows, preferred_element_type=jnp.float32)


def project_kernel(own_ref, peer_ref, weight_ref, *out_refs):
    total = product(own_ref, peer_ref, weight_ref)
    wide = total.shape[1] // len(out_refs)
    for at, out_ref in enumerate(out_refs):
        out_ref[...] = total[:, at * wide : (at + 1) * wide].astype(jnp.bfloat16)


def project(own, peer, weight, count):
    block, _ = own.shape
    return call(
        project_kernel,
        tuple(shape(block, weight.shape[1] // count) for _ in range(count)),
        [VMEM, VMEM, VMEM],
        2 * block * weight.size,
        2 * weight.size + 6 * own.size,
    )(own, peer, weight)


def step_kernel(own_ref, peer_ref, out_own_ref, out_peer_ref, *refs):
    in_ref, first_ref, signal_ref, gate_ref, all_ref = refs
    depth = own_ref.shape[1]
    chan = lax.axis_index("chan")
    at = pl.ds(pl.multiple_of(chan * depth, depth), depth)
    other = pl.ds(pl.multiple_of((1 - chan) * depth, depth), depth)
    all_ref[:, at] = own_ref[...]
    all_ref[:, other] = peer_ref[...]
    gated = all_ref[...]
    first = jnp.dot(gated, out_own_ref[...], preferred_element_type=jnp.float32).astype(jnp.bfloat16)
    second = jnp.dot(gated, out_peer_ref[...], preferred_element_type=jnp.float32).astype(jnp.bfloat16)
    first_ref[...] = first
    all_ref[:, at] = first
    all_ref[:, other] = second
    total = jnp.dot(all_ref[...], in_ref[...], preferred_element_type=jnp.float32)
    signal_ref[...] = total[:, :depth].astype(jnp.bfloat16)
    gate_ref[...] = total[:, depth:].astype(jnp.bfloat16)


def step(own, peer, out_own, out_peer, in_weight):
    block, depth = own.shape
    return pl.pallas_call(
        step_kernel,
        out_shape=(shape(block, depth),) * 3,
        in_specs=[VMEM] * 5,
        out_specs=(VMEM,) * 3,
        scratch_shapes=[pltpu.VMEM((block, 2 * depth), jnp.bfloat16)],
        name="step",
        cost_estimate=pl.CostEstimate(
            flops=16 * block * depth * depth, bytes_accessed=16 * depth * depth + 10 * own.size, transcendentals=0
        ),
        compiler_params=pltpu.CompilerParams(vmem_limit_bytes=12 << 20),
    )(own, peer, out_own, out_peer, in_weight)


def finish_kernel(own_ref, peer_ref, weight_ref, first_ref, first_home_ref, near_ref, out_ref):
    section = lax.axis_index("section")
    sequence, _ = position()

    @pl.when(section == 0)
    def _():
        out_ref[0, sequence] = first_ref[...]
        out_ref[0, 1 - sequence] = first_home_ref[...]

    @pl.when(section == 1)
    def _():
        out_ref[0, 1 - sequence] = product(own_ref, peer_ref, weight_ref).astype(jnp.bfloat16)
        out_ref[0, sequence] = near_ref[...]


def finish(own, peer, weight, first, first_home, near):
    block, local = first.shape
    return call(
        finish_kernel,
        shape(1, MB, block, local),
        [VMEM] * 6,
        4 * block * local * local,
        weight.size * 2 + 7 * own.size * 2,
        out_spec=pl.BlockSpec(),
    )(own, peer, weight, first, first_home, near)


def both_layers(tokens, in_proj, filters, out_proj, widths):
    count = lax.axis_size("seq")
    half = count // 2
    section = lax.axis_index("section")
    block = tokens.shape[1]
    sequence, _ = position()

    def swap(value, axis):
        return lax.ppermute(value, axis, [(0, 1), (1, 0)])

    def swap_in(value, at):
        return lax.ppermute(value, ("chan", "section"), [(at, 2 + at), (2 + at, at)])

    def across(value, from_section, to_section):
        pairs = [(2 * i + from_section, 2 * ((i + half) % count) + to_section) for i in range(count)]
        return lax.ppermute(value, ("seq", "section"), pairs)

    def pick(zero, one):
        return jnp.where(section == 0, zero, one)

    def where_held(which, held):
        low = held < half
        if which == 0:
            return (held, 0) if low else (held - half, 1)
        return (held + half, 1) if low else (held, 0)

    def ring(value, lag):
        pairs = []
        for which in range(MB):
            for held in range(count):
                source, target = where_held(which, held), where_held(which, (held + lag) % count)
                pairs.append((2 * source[0] + source[1], 2 * target[0] + target[1]))
        return lax.ppermute(value, ("seq", "section"), pairs)

    def halves(value):
        return value[: value.shape[0] // 2], value[value.shape[0] // 2 :]

    swapped = across(lax.dynamic_index_in_dim(tokens, 1 - sequence, 0, False), 1, 1)
    current = pick(lax.optimization_barrier(lax.dynamic_index_in_dim(tokens, sequence, 0, False)), swapped)
    peer = swap(current, "chan")

    in_near = in_proj[0].reshape(in_proj.shape[1], -1)
    in_far = swap(in_near, "section")
    taps = filters[0]
    far_taps = swap(taps, "section")
    out_near = out_proj[0]
    out_far = swap(out_near, "section")

    groups = ((0, REACH, 1, REACH + 1), (2, REACH + 2, REACH - 1, BAND - 1))
    blocks = []
    for layer in range(2):
        blocks.append(toeplitz(layer, widths, taps, far_taps, block, groups))

    def gathered(signal):
        if count != BAND:
            return [ring(signal, lag) if lag else signal for lag in range(-REACH, REACH)]
        near = [signal]
        for apart in range(1, REACH):
            near.append(lax.ppermute(signal, "seq", [(i, i ^ apart) for i in range(count)]))
        return near + [swap(value, "section") for value in near]

    def mixed(layer, sources, gating):
        total = None
        for group, members in enumerate(groups):
            last = group == len(groups) - 1
            chosen = [sources[slot] for slot in members]
            total = mix(blocks[layer][group], chosen, total, gating if last else None)
        return total

    in_first, in_last = pick(in_near, in_far), pick(in_far, in_near)
    signal, gating = project(current, peer, in_first, 2)
    sources = gathered(signal)

    upper, lower = halves(out_near)[0], halves(out_far)[1]
    sent, _ = lax.optimization_barrier((pick(upper, lower), signal))
    part = swap(sent, "chan")
    other = swap(part, "section")
    out_peer = pick(jnp.concatenate([part, other]), jnp.concatenate([other, part]))
    out_first, out_last = pick(out_near, out_far), pick(out_far, out_near)

    gated = mixed(0, sources, gating)
    gated_peer = swap(gated, "chan")
    first, signal, gating = step(gated, gated_peer, out_first, out_peer, in_last)
    gated = mixed(1, gathered(signal), gating)

    moved = across(gated, 1, 1)
    first_home = across(first, 1, 0)
    gated_peer = swap_in(gated, 0)
    (second,) = project(gated, gated_peer, out_last, 1)
    second_near = lax.ppermute(second, "section", [(0, 1)])
    moved_peer = swap_in(moved, 1)
    return finish(moved, moved_peer, out_last, first, first_home, second_near)


def solution(mesh):
    placed = (
        P(None, "seq", "chan"),
        P("section", None, None, "chan"),
        P("section", "chan", None),
        P("section", None, "chan"),
        P(),
    )
    return jax.shard_map(
        both_layers,
        mesh=mesh,
        in_specs=placed,
        out_specs=P("section", None, "seq", "chan"),
        check_vma=False,
    )
```

profile of v0, /device:TPU:1, one launch (start us, length us, event | category | flops | bytes accessed | tf_op | source)
XLA Modules:
  0.0 92.2 jit_solution(6270966502927876944)
XLA Ops:
  0.0 2.2 %copy.6 = bf16[128,8,2,512]{3,1,2,0:T(8,128)(2,1)S(1)} copy(bf16[128,8,2,512]{3,2,1,0:T(2,128)(2,1)} %bitcast.19) | data formatting | bytes 4194304
  2.2 0.1 collective-permute-start.3
  2.3 0.5 collective-permute-start.12
  2.8 1.8 %dynamic-slice_bitcast_fusion = (bf16[256,512]{1,0:T(8,128)(2,1)}, bf16[256,512]{1,0:T(8,128)(2,1)S(1)}) fusion(bf16[2,256,512]{2,1,0:T(8,128)(2,1)} %param.5, s32[]{:T(128)S(6)} %select_n.55, s32[]{:T(128)S(6)} %select_n.54), kind=kLoop, calls=%fused_computation.6 | loop fusion | bytes 1048584 | tf_op jit(solution)/shard_map/jit(dynamic_index_in_dim)/squeeze | solution.py:250
  4.6 5.3 %collective-permute-start.1 = (bf16[256,512]{1,0:T(8,128)(2,1)}, bf16[256,512]{1,0:T(8,128)(2,1)}, u32[]{:S(2)}, u32[]{:S(2)}) collective-permute-start(bf16[256,512]{1,0:T(8,128)(2,1)} %get-tuple-element.29), channel_id=1, source_target_pairs={{1,17},{5,21},{9,25},{13,29},{17,1},{21,5},{25,9},{29,13},{3,19},{... | collective-permute-start | bytes 786440 | tf_op jit(solution)/shard_map/ppermute | solution.py:228
  9.9 6.9 %collective-permute-done.1 = bf16[256,512]{1,0:T(8,128)(2,1)} collective-permute-done((bf16[256,512]{1,0:T(8,128)(2,1)}, bf16[256,512]{1,0:T(8,128)(2,1)}, u32[]{:S(2)}, u32[]{:S(2)}) %collective-permute-start.1) | collective-permute-done | bytes 262176 | tf_op jit(solution)/shard_map/ppermute | solution.py:228
  16.7 1.0 %broadcast_select_fusion.4.own_ref = bf16[256,512]{1,0:T(8,128)(2,1)S(1)} fusion(bf16[256,512]{1,0:T(8,128)(2,1)S(1)} %get-tuple-element.30, bf16[256,512]{1,0:T(8,128)(2,1)} %collective-permute-done.1, pred[]{:T(512)S(6)} %eq.2), kind=kLoop, calls=%fused_computation.8 | loop fusion | flops 131072 | bytes 786433 | tf_op jit(solution)/shard_map/jit(_where)/select_n | solution.py:231
  17.7 1.3 %collective-permute-start.2 = (bf16[256,512]{1,0:T(8,128)(2,1)S(1)}, bf16[256,512]{1,0:T(8,128)(2,1)S(1)}, u32[]{:S(2)}, u32[]{:S(2)}) collective-permute-start(bf16[256,512]{1,0:T(8,128)(2,1)S(1)} %broadcast_select_fusion.4.own_ref), channel_id=1, source_target_pairs={{0,2},{2,0},{1,3},{3,1},{4,6},{6,4},{5,7},{7,5},{8,10},{10,8},{9,1... | collective-permute-start | bytes 786440 | tf_op jit(solution)/shard_map/ppermute | solution.py:221
  19.1 1.1 %slice_select_fusion = bf16[512,512]{1,0:T(8,128)(2,1)S(1)} fusion(bf16[1024,512]{1,0:T(8,128)(2,1)} %collective-permute-done.12, bf16[1,1024,512]{2,1,0:T(8,128)(2,1)S(1)} %copy-done.2, pred[]{:T(512)S(6)} %eq.2), kind=kLoop, calls=%fused_computation.5 | loop fusion | flops 262144 | bytes 1572865 | tf_op jit(solution)/shard_map/jit(_where)/select_n | solution.py:231
  20.2 1.9 %broadcast_select_fusion = (bf16[1024,1024]{1,0:T(8,128)(2,1)S(1)}, bf16[1024,1024]{1,0:T(8,128)(2,1)S(1)}) fusion(bf16[1024,1024]{1,0:T(8,128)(2,1)} %collective-permute-done.3, bf16[1024,1024]{1,0:T(8,128)(2,1)S(1)} %bitcast.17, pred[]{:T(512)S(6)} %eq.2), kind=kLoop, calls=%fused_computation | loop fusion | flops 2097152 | bytes 8388609 | tf_op jit(solution)/shard_map/jit(_where)/select_n | solution.py:231
  22.0 0.0 copy-start
  22.0 0.0 copy-start.1
  22.1 3.7 %collective-permute-done.2.peer_ref = bf16[256,512]{1,0:T(8,128)(2,1)S(1)} collective-permute-done((bf16[256,512]{1,0:T(8,128)(2,1)S(1)}, bf16[256,512]{1,0:T(8,128)(2,1)S(1)}, u32[]{:S(2)}, u32[]{:S(2)}) %collective-permute-start.2) | collective-permute-done | bytes 262176 | tf_op jit(solution)/shard_map/ppermute | solution.py:221
  25.8 0.7 shard_map.55
  26.5 1.7 %collective-permute-start.13 = (bf16[512,512]{1,0:T(8,128)(2,1)S(1)}, bf16[512,512]{1,0:T(8,128)(2,1)S(1)}, u32[]{:S(2)}, u32[]{:S(2)}) collective-permute-start(bf16[512,512]{1,0:T(8,128)(2,1)S(1)} %slice_select_fusion), channel_id=1, source_target_pairs={{0,2},{2,0},{1,3},{3,1},{4,6},{6,4},{5,7},{7,5},{8,10},{10,8},{9,1... | collective-permute-start | bytes 1572872 | tf_op jit(solution)/shard_map/ppermute | solution.py:221
  28.2 1.2 %collective-permute-start.9 = (bf16[256,512]{1,0:T(8,128)(2,1)S(1)}, bf16[256,512]{1,0:T(8,128)(2,1)S(1)}, u32[]{:S(2)}, u32[]{:S(2)}) collective-permute-start(bf16[256,512]{1,0:T(8,128)(2,1)S(1)} %get-tuple-element.17.refs_0_), channel_id=1, source_target_pairs={{0,4},{4,0},{8,12},{12,8},{16,20},{20,16},{24,28},{28,24},{1,5},{5... | collective-permute-start | bytes 786440 | tf_op jit(solution)/shard_map/ppermute | solution.py:271
  29.4 0.7 collective-permute-start.4
  30.1 0.7 collective-permute-start.6
  30.8 1.2 %collective-permute-done.far_ref = bf16[4,2304]{1,0:T(4,128)(2,1)S(1)} collective-permute-done((bf16[4,2304]{1,0:T(4,128)(2,1)S(1)}, bf16[4,2304]{1,0:T(4,128)(2,1)S(1)}, u32[]{:S(2)}, u32[]{:S(2)}) %collective-permute-start) | collective-permute-done | bytes 18464 | tf_op jit(solution)/shard_map/ppermute | solution.py:221
  32.0 0.2 collective-permute-start.8
  32.2 1.2 %collective-permute-done.9.refs_2_ = bf16[256,512]{1,0:T(8,128)(2,1)S(1)} collective-permute-done((bf16[256,512]{1,0:T(8,128)(2,1)S(1)}, bf16[256,512]{1,0:T(8,128)(2,1)S(1)}, u32[]{:S(2)}, u32[]{:S(2)}) %collective-permute-start.9) | collective-permute-done | bytes 262176 | tf_op jit(solution)/shard_map/ppermute | solution.py:271
  33.4 0.0 collective-permute-start.10
  33.4 1.2 %collective-permute-done.4.refs_0_ = bf16[256,512]{1,0:T(8,128)(2,1)S(1)} collective-permute-done((bf16[256,512]{1,0:T(8,128)(2,1)S(1)}, bf16[256,512]{1,0:T(8,128)(2,1)S(1)}, u32[]{:S(2)}, u32[]{:S(2)}) %collective-permute-start.4) | collective-permute-done | bytes 262176 | tf_op jit(solution)/shard_map/ppermute | solution.py:271
  34.6 0.0 collective-permute-start.5
  34.6 2.7 %collective-permute-done.6.refs_2_ = bf16[256,512]{1,0:T(8,128)(2,1)S(1)} collective-permute-done((bf16[256,512]{1,0:T(8,128)(2,1)S(1)}, bf16[256,512]{1,0:T(8,128)(2,1)S(1)}, u32[]{:S(2)}, u32[]{:S(2)}) %collective-permute-start.6) | collective-permute-done | bytes 262176 | tf_op jit(solution)/shard_map/ppermute | solution.py:271
  37.4 0.0 collective-permute-start.7
  37.4 0.0 collective-permute-done.13
  37.4 0.5 collective-permute-start.14
  37.9 1.9 %toeplitz.3 = (bf16[4,256,1024]{2,1,0:T(8,128)(2,1)S(1)}, bf16[4,256,1024]{2,1,0:T(8,128)(2,1)S(1)}) custom-call(s32[2]{0:T(128)S(1)} %copy-done.1, bf16[4,2304]{1,0:T(4,128)(2,1)S(1)} %bitcast.14, bf16[4,2304]{1,0:T(4,128)(2,1)S(1)} %collective-permute-done.far_ref), custom_call_target="tpu_custom_call" | custom-call | flops 83886080 | bytes 4194304 | tf_op jit(solution)/shard_map/toeplitz/pallas_call | solution.py:79
  39.8 0.0 collective-permute-done.8.refs_1_
  39.8 0.7 shard_map.56.refs_5_
  40.5 0.0 collective-permute-done.7.refs_3_
  40.6 0.7 shard_map.57.own_ref
  41.3 0.1 collective-permute-start.11
  41.4 1.4 %broadcast_select_fusion.2 = (bf16[1024,512]{1,0:T(8,128)(2,1)S(1)}, bf16[1024,512]{1,0:T(8,128)(2,1)S(1)}) fusion(bf16[1024,512]{1,0:T(8,128)(2,1)} %collective-permute-done.12, pred[]{:T(512)S(6)} %eq.2, bf16[1,1024,512]{2,1,0:T(8,128)(2,1)S(1)} %copy-done.2), kind=kLoop, calls=%fused_computation.3 | loop fusion | flops 1048576 | bytes 4194305 | tf_op jit(solution)/shard_map/jit(_where)/select_n | solution.py:231
  42.8 0.0 collective-permute-done.14
  42.8 0.5 maximum_select_fusion.out_peer_ref
  43.3 5.9 %collective-permute-done.11.peer_ref = bf16[256,512]{1,0:T(8,128)(2,1)S(1)} collective-permute-done((bf16[256,512]{1,0:T(8,128)(2,1)S(1)}, bf16[256,512]{1,0:T(8,128)(2,1)S(1)}, u32[]{:S(2)}, u32[]{:S(2)}) %collective-permute-start.11) | collective-permute-done | bytes 262176 | tf_op jit(solution)/shard_map/ppermute | solution.py:221
  49.2 1.4 %step.1 = (bf16[256,512]{1,0:T(8,128)(2,1)S(1)}, bf16[256,512]{1,0:T(8,128)(2,1)S(1)}, bf16[256,512]{1,0:T(8,128)(2,1)S(1)}) custom-call(bf16[256,512]{1,0:T(8,128)(2,1)S(1)} %shard_map.57.own_ref, bf16[256,512]{1,0:T(8,128)(2,1)S(1)} %collective-permute-done.11.peer_ref, bf16[1024,512]{1,0:T(8,128)(2,1)S(1)} %get-tuple-element.28.out_own_ref, ...), custom_call_target="tpu_custom_call" | custom-call | flops 1073741824 | bytes 5505024 | tf_op jit(solution)/shard_map/step/pallas_call | solution.py:172
  50.6 1.3 %collective-permute-start.20 = (bf16[256,512]{1,0:T(8,128)(2,1)S(1)}, bf16[256,512]{1,0:T(8,128)(2,1)S(1)}, u32[]{:S(2)}, u32[]{:S(2)}) collective-permute-start(bf16[256,512]{1,0:T(8,128)(2,1)S(1)} %get-tuple-element.21.refs_0_), channel_id=1, source_target_pairs={{0,4},{4,0},{8,12},{12,8},{16,20},{20,16},{24,28},{28,24},{1,5},{5... | collective-permute-start | bytes 786440 | tf_op jit(solution)/shard_map/ppermute | solution.py:271
  51.9 0.7 collective-permute-start.15
  52.6 0.7 collective-permute-start.17
  53.3 1.7 %collective-permute-start.19 = (bf16[256,512]{1,0:T(8,128)(2,1)S(1)}, bf16[256,512]{1,0:T(8,128)(2,1)S(1)}, u32[]{:S(2)}, u32[]{:S(2)}) collective-permute-start(bf16[256,512]{1,0:T(8,128)(2,1)S(1)} %get-tuple-element.21.refs_0_), channel_id=1, source_target_pairs={{0,1},{1,0},{2,3},{3,2},{4,5},{5,4},{6,7},{7,6},{8,9},{9,8},{10,11... | collective-permute-start | bytes 786440 | tf_op jit(solution)/shard_map/ppermute | solution.py:221
  55.0 2.7 %collective-permute-done.20.refs_2_ = bf16[256,512]{1,0:T(8,128)(2,1)S(1)} collective-permute-done((bf16[256,512]{1,0:T(8,128)(2,1)S(1)}, bf16[256,512]{1,0:T(8,128)(2,1)S(1)}, u32[]{:S(2)}, u32[]{:S(2)}) %collective-permute-start.20) | collective-permute-done | bytes 262176 | tf_op jit(solution)/shard_map/ppermute | solution.py:271
  57.7 2.1 %collective-permute-start.21 = (bf16[256,512]{1,0:T(8,128)(2,1)S(1)}, bf16[256,512]{1,0:T(8,128)(2,1)S(1)}, u32[]{:S(2)}, u32[]{:S(2)}) collective-permute-start(bf16[256,512]{1,0:T(8,128)(2,1)S(1)} %collective-permute-done.20.refs_2_), channel_id=1, source_target_pairs={{0,1},{1,0},{2,3},{3,2},{4,5},{5,4},{6,7},{7,6},{8,9},{9,8},{10,11... | collective-permute-start | bytes 786440 | tf_op jit(solution)/shard_map/ppermute | solution.py:221
  59.8 2.4 %collective-permute-start.16 = (bf16[256,512]{1,0:T(8,128)(2,1)S(1)}, bf16[256,512]{1,0:T(8,128)(2,1)S(1)}, u32[]{:S(2)}, u32[]{:S(2)}) collective-permute-start(bf16[256,512]{1,0:T(8,128)(2,1)S(1)} %collective-permute-done.15.refs_0_), channel_id=1, source_target_pairs={{0,1},{1,0},{2,3},{3,2},{4,5},{5,4},{6,7},{7,6},{8,9},{9,8},{10,11... | collective-permute-start | bytes 786440 | tf_op jit(solution)/shard_map/ppermute | solution.py:221
  62.2 2.0 %collective-permute-done.17.refs_2_ = bf16[256,512]{1,0:T(8,128)(2,1)S(1)} collective-permute-done((bf16[256,512]{1,0:T(8,128)(2,1)S(1)}, bf16[256,512]{1,0:T(8,128)(2,1)S(1)}, u32[]{:S(2)}, u32[]{:S(2)}) %collective-permute-start.17) | collective-permute-done | bytes 262176 | tf_op jit(solution)/shard_map/ppermute | solution.py:271
  64.2 2.0 %collective-permute-start.18 = (bf16[256,512]{1,0:T(8,128)(2,1)S(1)}, bf16[256,512]{1,0:T(8,128)(2,1)S(1)}, u32[]{:S(2)}, u32[]{:S(2)}) collective-permute-start(bf16[256,512]{1,0:T(8,128)(2,1)S(1)} %collective-permute-done.17.refs_2_), channel_id=1, source_target_pairs={{0,1},{1,0},{2,3},{3,2},{4,5},{5,4},{6,7},{7,6},{8,9},{9,8},{10,11... | collective-permute-start | bytes 786440 | tf_op jit(solution)/shard_map/ppermute | solution.py:221
  66.2 1.9 %toeplitz.2 = (bf16[4,256,1024]{2,1,0:T(8,128)(2,1)S(1)}, bf16[4,256,1024]{2,1,0:T(8,128)(2,1)S(1)}) custom-call(s32[2]{0:T(128)S(1)} %copy-done.1, bf16[4,2304]{1,0:T(4,128)(2,1)S(1)} %bitcast.15, bf16[4,2304]{1,0:T(4,128)(2,1)S(1)} %collective-permute-done.far_ref), custom_call_target="tpu_custom_call" | custom-call | flops 83886080 | bytes 4194304 | tf_op jit(solution)/shard_map/toeplitz/pallas_call | solution.py:79
  68.1 0.0 collective-permute-done.19.refs_1_
  68.1 0.7 shard_map.58.refs_5_
  68.8 0.0 collective-permute-done.16.refs_1_
  68.8 0.0 collective-permute-done.18.refs_3_
  68.9 0.7 shard_map.59.own_ref
  69.6 0.7 collective-permute-start.25
  70.3 3.9 %collective-permute-start.22 = (bf16[256,512]{1,0:T(8,128)(2,1)S(1)}, bf16[256,512]{1,0:T(8,128)(2,1)S(1)}, u32[]{:S(2)}, u32[]{:S(2)}) collective-permute-start(bf16[256,512]{1,0:T(8,128)(2,1)S(1)} %shard_map.59.own_ref), channel_id=1, source_target_pairs={{1,17},{5,21},{9,25},{13,29},{17,1},{21,5},{25,9},{29,13},{3,19},{... | collective-permute-start | bytes 786440 | tf_op jit(solution)/shard_map/ppermute | solution.py:228
  74.2 2.4 %collective-permute-start.24 = (bf16[256,512]{1,0:T(8,128)(2,1)S(1)}, bf16[256,512]{1,0:T(8,128)(2,1)S(1)}, u32[]{:S(2)}, u32[]{:S(2)}) collective-permute-start(bf16[256,512]{1,0:T(8,128)(2,1)S(1)} %get-tuple-element.24.first_ref), channel_id=1, source_target_pairs={{1,16},{5,20},{9,24},{13,28},{17,0},{21,4},{25,8},{29,12},{3,18},{... | collective-permute-start | bytes 786440 | tf_op jit(solution)/shard_map/ppermute | solution.py:228
  76.6 0.4 shard_map.60
  77.0 1.3 %collective-permute-start.26 = (bf16[256,512]{1,0:T(8,128)(2,1)S(1)}, bf16[256,512]{1,0:T(8,128)(2,1)S(1)}, u32[]{:S(2)}, u32[]{:S(2)}) collective-permute-start(bf16[256,512]{1,0:T(8,128)(2,1)S(1)} %shard_map.60), channel_id=1, source_target_pairs={{0,1},{2,3},{4,5},{6,7},{8,9},{10,11},{12,13},{14,15},{16,17},{18,... | collective-permute-start | bytes 786440 | tf_op jit(solution)/shard_map/ppermute | solution.py:302
  78.3 5.6 %collective-permute-done.22.own_ref = bf16[256,512]{1,0:T(8,128)(2,1)S(1)} collective-permute-done((bf16[256,512]{1,0:T(8,128)(2,1)S(1)}, bf16[256,512]{1,0:T(8,128)(2,1)S(1)}, u32[]{:S(2)}, u32[]{:S(2)}) %collective-permute-start.22) | collective-permute-done | bytes 262176 | tf_op jit(solution)/shard_map/ppermute | solution.py:228
  83.9 2.0 %collective-permute-start.23 = (bf16[256,512]{1,0:T(8,128)(2,1)S(1)}, bf16[256,512]{1,0:T(8,128)(2,1)S(1)}, u32[]{:S(2)}, u32[]{:S(2)}) collective-permute-start(bf16[256,512]{1,0:T(8,128)(2,1)S(1)} %collective-permute-done.22.own_ref), channel_id=1, source_target_pairs={{1,3},{3,1},{5,7},{7,5},{9,11},{11,9},{13,15},{15,13},{17,19},{19,... | collective-permute-start | bytes 786440 | tf_op jit(solution)/shard_map/ppermute | solution.py:224
  85.9 0.0 collective-permute-done.24.first_home_ref
  85.9 5.1 %collective-permute-done.23.peer_ref = bf16[256,512]{1,0:T(8,128)(2,1)S(1)} collective-permute-done((bf16[256,512]{1,0:T(8,128)(2,1)S(1)}, bf16[256,512]{1,0:T(8,128)(2,1)S(1)}, u32[]{:S(2)}, u32[]{:S(2)}) %collective-permute-start.23) | collective-permute-done | bytes 262176 | tf_op jit(solution)/shard_map/ppermute | solution.py:224
  91.0 1.2 %shard_map.61 = bf16[1,2,256,512]{3,2,1,0:T(8,128)(2,1)} custom-call(bf16[256,512]{1,0:T(8,128)(2,1)S(1)} %collective-permute-done.22.own_ref, bf16[256,512]{1,0:T(8,128)(2,1)S(1)} %collective-permute-done.23.peer_ref, bf16[1024,512]{1,0:T(8,128)(2,1)S(1)} %get-tuple-element.27.weight_ref, bf16[256,512]{1,0:T(8,128)(2,1)S(1)} %get-tuple-element.24.first_ref, ...), custom_call_target="tpu_custom_call" | custom-call | flops 268435456 | bytes 2883584 | tf_op jit(solution)/shard_map/pallas_call | solution.py:203
  (13 shorter events, 0.0 us)
Async XLA Ops:
  0.0 2.3 %copy-start.2 = (bf16[1,1024,512]{2,1,0:T(8,128)(2,1)S(1)}, bf16[1,1024,512]{2,1,0:T(8,128)(2,1)}, u32[]{:S(2)}) copy-start(bf16[1,1024,512]{2,1,0:T(8,128)(2,1)} %param.8) | copy-start | bytes 3145732
  2.2 17.9 %collective-permute-start.3 = (bf16[1024,1024]{1,0:T(8,128)(2,1)S(1)}, bf16[1024,1024]{1,0:T(8,128)(2,1)}, u32[]{:S(2)}, u32[]{:S(2)}) collective-permute-start(bf16[1024,1024]{1,0:T(8,128)(2,1)S(1)} %bitcast.16), channel_id=1, source_target_pairs={{0,1},{1,0},{2,3},{3,2},{4,5},{5,4},{6,7},{7,6},{8,9},{9,8},{10,11... | collective-permute-start | bytes 6291464 | tf_op jit(solution)/shard_map/ppermute | solution.py:221
  2.3 16.7 %collective-permute-start.12 = (bf16[1024,512]{1,0:T(8,128)(2,1)S(1)}, bf16[1024,512]{1,0:T(8,128)(2,1)}, u32[]{:S(2)}, u32[]{:S(2)}) collective-permute-start(bf16[1024,512]{1,0:T(8,128)(2,1)S(1)} %bitcast.18), channel_id=1, source_target_pairs={{0,1},{1,0},{2,3},{3,2},{4,5},{5,4},{6,7},{7,6},{8,9},{9,8},{10,11... | collective-permute-start | bytes 3145736 | tf_op jit(solution)/shard_map/ppermute | solution.py:221
  4.6 12.2 %collective-permute-start.1 = (bf16[256,512]{1,0:T(8,128)(2,1)}, bf16[256,512]{1,0:T(8,128)(2,1)}, u32[]{:S(2)}, u32[]{:S(2)}) collective-permute-start(bf16[256,512]{1,0:T(8,128)(2,1)} %get-tuple-element.29), channel_id=1, source_target_pairs={{1,17},{5,21},{9,25},{13,29},{17,1},{21,5},{25,9},{29,13},{3,19},{... | collective-permute-start | bytes 786440 | tf_op jit(solution)/shard_map/ppermute | solution.py:228
  17.7 8.0 %collective-permute-start.2 = (bf16[256,512]{1,0:T(8,128)(2,1)S(1)}, bf16[256,512]{1,0:T(8,128)(2,1)S(1)}, u32[]{:S(2)}, u32[]{:S(2)}) collective-permute-start(bf16[256,512]{1,0:T(8,128)(2,1)S(1)} %broadcast_select_fusion.4.own_ref), channel_id=1, source_target_pairs={{0,2},{2,0},{1,3},{3,1},{4,6},{6,4},{5,7},{7,5},{8,10},{10,8},{9,1... | collective-permute-start | bytes 786440 | tf_op jit(solution)/shard_map/ppermute | solution.py:221
  22.0 8.8 %copy-start = (bf16[1,4,2304]{2,1,0:T(4,128)(2,1)S(1)}, bf16[1,4,2304]{2,1,0:T(4,128)(2,1)}, u32[]{:S(2)}) copy-start(bf16[1,4,2304]{2,1,0:T(4,128)(2,1)} %param.7) | copy-start | bytes 55300
  22.0 15.8 %copy-start.1 = (s32[2]{0:T(128)S(1)}, s32[2]{0:T(128)}, u32[]{:S(2)}) copy-start(s32[2]{0:T(128)} %widths_ref.3) | copy-start | bytes 28
  26.5 10.9 %collective-permute-start.13 = (bf16[512,512]{1,0:T(8,128)(2,1)S(1)}, bf16[512,512]{1,0:T(8,128)(2,1)S(1)}, u32[]{:S(2)}, u32[]{:S(2)}) collective-permute-start(bf16[512,512]{1,0:T(8,128)(2,1)S(1)} %slice_select_fusion), channel_id=1, source_target_pairs={{0,2},{2,0},{1,3},{3,1},{4,6},{6,4},{5,7},{7,5},{8,10},{10,8},{9,1... | collective-permute-start | bytes 1572872 | tf_op jit(solution)/shard_map/ppermute | solution.py:221
  28.2 5.2 %collective-permute-start.9 = (bf16[256,512]{1,0:T(8,128)(2,1)S(1)}, bf16[256,512]{1,0:T(8,128)(2,1)S(1)}, u32[]{:S(2)}, u32[]{:S(2)}) collective-permute-start(bf16[256,512]{1,0:T(8,128)(2,1)S(1)} %get-tuple-element.17.refs_0_), channel_id=1, source_target_pairs={{0,4},{4,0},{8,12},{12,8},{16,20},{20,16},{24,28},{28,24},{1,5},{5... | collective-permute-start | bytes 786440 | tf_op jit(solution)/shard_map/ppermute | solution.py:271
  29.4 5.2 %collective-permute-start.4 = (bf16[256,512]{1,0:T(8,128)(2,1)S(1)}, bf16[256,512]{1,0:T(8,128)(2,1)S(1)}, u32[]{:S(2)}, u32[]{:S(2)}) collective-permute-start(bf16[256,512]{1,0:T(8,128)(2,1)S(1)} %get-tuple-element.17.refs_0_), channel_id=1, source_target_pairs={{0,8},{4,12},{8,0},{12,4},{16,24},{20,28},{24,16},{28,20},{1,9},{5... | collective-permute-start | bytes 786440 | tf_op jit(solution)/shard_map/ppermute | solution.py:271
  30.1 7.3 %collective-permute-start.6 = (bf16[256,512]{1,0:T(8,128)(2,1)S(1)}, bf16[256,512]{1,0:T(8,128)(2,1)S(1)}, u32[]{:S(2)}, u32[]{:S(2)}) collective-permute-start(bf16[256,512]{1,0:T(8,128)(2,1)S(1)} %get-tuple-element.17.refs_0_), channel_id=1, source_target_pairs={{0,12},{4,8},{8,4},{12,0},{16,28},{20,24},{24,20},{28,16},{1,13},{... | collective-permute-start | bytes 786440 | tf_op jit(solution)/shard_map/ppermute | solution.py:271
  30.8 1.2 %collective-permute-start = (bf16[4,2304]{1,0:T(4,128)(2,1)S(1)}, bf16[4,2304]{1,0:T(4,128)(2,1)S(1)}, u32[]{:S(2)}, u32[]{:S(2)}) collective-permute-start(bf16[4,2304]{1,0:T(4,128)(2,1)S(1)} %bitcast.13), channel_id=1, source_target_pairs={{0,1},{1,0},{2,3},{3,2},{4,5},{5,4},{6,7},{7,6},{8,9},{9,8},{10,11... | collective-permute-start | bytes 55304 | tf_op jit(solution)/shard_map/ppermute | solution.py:221
  32.0 7.8 %collective-permute-start.8 = (bf16[256,512]{1,0:T(8,128)(2,1)S(1)}, bf16[256,512]{1,0:T(8,128)(2,1)S(1)}, u32[]{:S(2)}, u32[]{:S(2)}) collective-permute-start(bf16[256,512]{1,0:T(8,128)(2,1)S(1)} %get-tuple-element.17.refs_0_), channel_id=1, source_target_pairs={{0,1},{1,0},{2,3},{3,2},{4,5},{5,4},{6,7},{7,6},{8,9},{9,8},{10,11... | collective-permute-start | bytes 786440 | tf_op jit(solution)/shard_map/ppermute | solution.py:221
  33.4 6.4 %collective-permute-start.10 = (bf16[256,512]{1,0:T(8,128)(2,1)S(1)}, bf16[256,512]{1,0:T(8,128)(2,1)S(1)}, u32[]{:S(2)}, u32[]{:S(2)}) collective-permute-start(bf16[256,512]{1,0:T(8,128)(2,1)S(1)} %collective-permute-done.9.refs_2_), channel_id=1, source_target_pairs={{0,1},{1,0},{2,3},{3,2},{4,5},{5,4},{6,7},{7,6},{8,9},{9,8},{10,11... | collective-permute-start | bytes 786440 | tf_op jit(solution)/shard_map/ppermute | solution.py:221
  34.6 5.9 %collective-permute-start.5 = (bf16[256,512]{1,0:T(8,128)(2,1)S(1)}, bf16[256,512]{1,0:T(8,128)(2,1)S(1)}, u32[]{:S(2)}, u32[]{:S(2)}) collective-permute-start(bf16[256,512]{1,0:T(8,128)(2,1)S(1)} %collective-permute-done.4.refs_0_), channel_id=1, source_target_pairs={{0,1},{1,0},{2,3},{3,2},{4,5},{5,4},{6,7},{7,6},{8,9},{9,8},{10,11... | collective-permute-start | bytes 786440 | tf_op jit(solution)/shard_map/ppermute | solution.py:221
  37.4 3.2 %collective-permute-start.7 = (bf16[256,512]{1,0:T(8,128)(2,1)S(1)}, bf16[256,512]{1,0:T(8,128)(2,1)S(1)}, u32[]{:S(2)}, u32[]{:S(2)}) collective-permute-start(bf16[256,512]{1,0:T(8,128)(2,1)S(1)} %collective-permute-done.6.refs_2_), channel_id=1, source_target_pairs={{0,1},{1,0},{2,3},{3,2},{4,5},{5,4},{6,7},{7,6},{8,9},{9,8},{10,11... | collective-permute-start | bytes 786440 | tf_op jit(solution)/shard_map/ppermute | solution.py:221
  37.4 5.4 %collective-permute-start.14 = (bf16[512,512]{1,0:T(8,128)(2,1)S(1)}, bf16[512,512]{1,0:T(8,128)(2,1)S(1)}, u32[]{:S(2)}, u32[]{:S(2)}) collective-permute-start(bf16[512,512]{1,0:T(8,128)(2,1)S(1)} %collective-permute-done.13), channel_id=1, source_target_pairs={{0,1},{1,0},{2,3},{3,2},{4,5},{5,4},{6,7},{7,6},{8,9},{9,8},{10,11... | collective-permute-start | bytes 1572872 | tf_op jit(solution)/shard_map/ppermute | solution.py:221
  41.3 7.9 %collective-permute-start.11 = (bf16[256,512]{1,0:T(8,128)(2,1)S(1)}, bf16[256,512]{1,0:T(8,128)(2,1)S(1)}, u32[]{:S(2)}, u32[]{:S(2)}) collective-permute-start(bf16[256,512]{1,0:T(8,128)(2,1)S(1)} %shard_map.57.own_ref), channel_id=1, source_target_pairs={{0,2},{2,0},{1,3},{3,1},{4,6},{6,4},{5,7},{7,5},{8,10},{10,8},{9,1... | collective-permute-start | bytes 786440 | tf_op jit(solution)/shard_map/ppermute | solution.py:221
  50.6 7.1 %collective-permute-start.20 = (bf16[256,512]{1,0:T(8,128)(2,1)S(1)}, bf16[256,512]{1,0:T(8,128)(2,1)S(1)}, u32[]{:S(2)}, u32[]{:S(2)}) collective-permute-start(bf16[256,512]{1,0:T(8,128)(2,1)S(1)} %get-tuple-element.21.refs_0_), channel_id=1, source_target_pairs={{0,4},{4,0},{8,12},{12,8},{16,20},{20,16},{24,28},{28,24},{1,5},{5... | collective-permute-start | bytes 786440 | tf_op jit(solution)/shard_map/ppermute | solution.py:271
  51.9 7.9 %collective-permute-start.15 = (bf16[256,512]{1,0:T(8,128)(2,1)S(1)}, bf16[256,512]{1,0:T(8,128)(2,1)S(1)}, u32[]{:S(2)}, u32[]{:S(2)}) collective-permute-start(bf16[256,512]{1,0:T(8,128)(2,1)S(1)} %get-tuple-element.21.refs_0_), channel_id=1, source_target_pairs={{0,8},{4,12},{8,0},{12,4},{16,24},{20,28},{24,16},{28,20},{1,9},{5... | collective-permute-start | bytes 786440 | tf_op jit(solution)/shard_map/ppermute | solution.py:271
  52.6 11.6 %collective-permute-start.17 = (bf16[256,512]{1,0:T(8,128)(2,1)S(1)}, bf16[256,512]{1,0:T(8,128)(2,1)S(1)}, u32[]{:S(2)}, u32[]{:S(2)}) collective-permute-start(bf16[256,512]{1,0:T(8,128)(2,1)S(1)} %get-tuple-element.21.refs_0_), channel_id=1, source_target_pairs={{0,12},{4,8},{8,4},{12,0},{16,28},{20,24},{24,20},{28,16},{1,13},{... | collective-permute-start | bytes 786440 | tf_op jit(solution)/shard_map/ppermute | solution.py:271
  53.3 14.8 %collective-permute-start.19 = (bf16[256,512]{1,0:T(8,128)(2,1)S(1)}, bf16[256,512]{1,0:T(8,128)(2,1)S(1)}, u32[]{:S(2)}, u32[]{:S(2)}) collective-permute-start(bf16[256,512]{1,0:T(8,128)(2,1)S(1)} %get-tuple-element.21.refs_0_), channel_id=1, source_target_pairs={{0,1},{1,0},{2,3},{3,2},{4,5},{5,4},{6,7},{7,6},{8,9},{9,8},{10,11... | collective-permute-start | bytes 786440 | tf_op jit(solution)/shard_map/ppermute | solution.py:221
  57.7 10.5 %collective-permute-start.21 = (bf16[256,512]{1,0:T(8,128)(2,1)S(1)}, bf16[256,512]{1,0:T(8,128)(2,1)S(1)}, u32[]{:S(2)}, u32[]{:S(2)}) collective-permute-start(bf16[256,512]{1,0:T(8,128)(2,1)S(1)} %collective-permute-done.20.refs_2_), channel_id=1, source_target_pairs={{0,1},{1,0},{2,3},{3,2},{4,5},{5,4},{6,7},{7,6},{8,9},{9,8},{10,11... | collective-permute-start | bytes 786440 | tf_op jit(solution)/shard_map/ppermute | solution.py:221
  59.8 9.0 %collective-permute-start.16 = (bf16[256,512]{1,0:T(8,128)(2,1)S(1)}, bf16[256,512]{1,0:T(8,128)(2,1)S(1)}, u32[]{:S(2)}, u32[]{:S(2)}) collective-permute-start(bf16[256,512]{1,0:T(8,128)(2,1)S(1)} %collective-permute-done.15.refs_0_), channel_id=1, source_target_pairs={{0,1},{1,0},{2,3},{3,2},{4,5},{5,4},{6,7},{7,6},{8,9},{9,8},{10,11... | collective-permute-start | bytes 786440 | tf_op jit(solution)/shard_map/ppermute | solution.py:221
  64.2 4.7 %collective-permute-start.18 = (bf16[256,512]{1,0:T(8,128)(2,1)S(1)}, bf16[256,512]{1,0:T(8,128)(2,1)S(1)}, u32[]{:S(2)}, u32[]{:S(2)}) collective-permute-start(bf16[256,512]{1,0:T(8,128)(2,1)S(1)} %collective-permute-done.17.refs_2_), channel_id=1, source_target_pairs={{0,1},{1,0},{2,3},{3,2},{4,5},{5,4},{6,7},{7,6},{8,9},{9,8},{10,11... | collective-permute-start | bytes 786440 | tf_op jit(solution)/shard_map/ppermute | solution.py:221
  69.6 7.0 %collective-permute-start.25 = (bf16[256,512]{1,0:T(8,128)(2,1)S(1)}, bf16[256,512]{1,0:T(8,128)(2,1)S(1)}, u32[]{:S(2)}, u32[]{:S(2)}) collective-permute-start(bf16[256,512]{1,0:T(8,128)(2,1)S(1)} %shard_map.59.own_ref), channel_id=1, source_target_pairs={{0,2},{2,0},{4,6},{6,4},{8,10},{10,8},{12,14},{14,12},{16,18},{18,... | collective-permute-start | bytes 786440 | tf_op jit(solution)/shard_map/ppermute | solution.py:224
  70.3 13.6 %collective-permute-start.22 = (bf16[256,512]{1,0:T(8,128)(2,1)S(1)}, bf16[256,512]{1,0:T(8,128)(2,1)S(1)}, u32[]{:S(2)}, u32[]{:S(2)}) collective-permute-start(bf16[256,512]{1,0:T(8,128)(2,1)S(1)} %shard_map.59.own_ref), channel_id=1, source_target_pairs={{1,17},{5,21},{9,25},{13,29},{17,1},{21,5},{25,9},{29,13},{3,19},{... | collective-permute-start | bytes 786440 | tf_op jit(solution)/shard_map/ppermute | solution.py:228
  74.2 11.7 %collective-permute-start.24 = (bf16[256,512]{1,0:T(8,128)(2,1)S(1)}, bf16[256,512]{1,0:T(8,128)(2,1)S(1)}, u32[]{:S(2)}, u32[]{:S(2)}) collective-permute-start(bf16[256,512]{1,0:T(8,128)(2,1)S(1)} %get-tuple-element.24.first_ref), channel_id=1, source_target_pairs={{1,16},{5,20},{9,24},{13,28},{17,0},{21,4},{25,8},{29,12},{3,18},{... | collective-permute-start | bytes 786440 | tf_op jit(solution)/shard_map/ppermute | solution.py:228
  77.0 8.9 %collective-permute-start.26 = (bf16[256,512]{1,0:T(8,128)(2,1)S(1)}, bf16[256,512]{1,0:T(8,128)(2,1)S(1)}, u32[]{:S(2)}, u32[]{:S(2)}) collective-permute-start(bf16[256,512]{1,0:T(8,128)(2,1)S(1)} %shard_map.60), channel_id=1, source_target_pairs={{0,1},{2,3},{4,5},{6,7},{8,9},{10,11},{12,13},{14,15},{16,17},{18,... | collective-permute-start | bytes 786440 | tf_op jit(solution)/shard_map/ppermute | solution.py:302
  83.9 7.1 %collective-permute-start.23 = (bf16[256,512]{1,0:T(8,128)(2,1)S(1)}, bf16[256,512]{1,0:T(8,128)(2,1)S(1)}, u32[]{:S(2)}, u32[]{:S(2)}) collective-permute-start(bf16[256,512]{1,0:T(8,128)(2,1)S(1)} %collective-permute-done.22.own_ref), channel_id=1, source_target_pairs={{1,3},{3,1},{5,7},{7,5},{9,11},{11,9},{13,15},{15,13},{17,19},{19,... | collective-permute-start | bytes 786440 | tf_op jit(solution)/shard_map/ppermute | solution.py:224
where the time goes:
time: 92.6 us; the launch traced here: 92.2 us
  waiting for transfers between devices  38.2 us (41%)
  starting transfers between devices  33.5 us (36%)
  Pallas kernels  10.4 us (11%)
  other arithmetic  5.77 us (6%)
  local copies, waits for them, and re-layouts  4.02 us (4%)
    ppermute x15, starting transfers between devices, swap(): return lax.ppermute(value, axis, [(0, 1), (1, 0)])  12.7 us
    ppermute x3, waiting for transfers between devices, across(): return lax.ppermute(value, ('seq', 'section'), pairs)  12.4 us
    ppermute x3, starting transfers between devices, across(): return lax.ppermute(value, ('seq', 'section'), pairs)  11.6 us
    ppermute x15, waiting for transfers between devices, swap(): return lax.ppermute(value, axis, [(0, 1), (1, 0)])  10.9 us
    ppermute x6, waiting for transfers between devices, gathered(): lax.ppermute(signal, 'seq', [(i, i ^ apart) for i in range(count)])  9.81 us
    select_n x5, other arithmetic, pick(): return jnp.where(section == 0, zero, one)  5.77 us
    ppermute x6, starting transfers between devices, gathered(): lax.ppermute(signal, 'seq', [(i, i ^ apart) for i in range(count)])  5.36 us
    ppermute x2, waiting for transfers between devices, swap_in(): lax.ppermute(value, ('chan', 'section'), [(at, 2 + at), (2 + at, at)])  5.08 us
  transfers between devices with their start and end apart: 27, of which 11 were waited for; matrix products, arithmetic and copies ran while one was open for 8% of the time, Pallas kernels for 7%

commit v1 on v0

--- a/solution.py
+++ b/solution.py
@@ -11,6 +11,7 @@
 BAND = 8
 REACH = BAND // 2
 MB = 2
+PARTS = 2
 
 
 VMEM = pl.BlockSpec(memory_space=pltpu.VMEM)
@@ -92,60 +93,103 @@
     )(widths, near, far)
 
 
+def take_kernel(tokens_ref, *refs):
+    outs, sems = refs[:-1], refs[-1]
+    sequence, _ = position()
+    parts = len(outs) // 2
+    rows = outs[0].shape[0]
+    copies = []
+    for at, out_ref in enumerate(outs):
+        held = 1 - sequence if at < parts else sequence
+        source = tokens_ref.at[held, pl.ds((at % parts) * rows, rows), :]
+        copies.append(pltpu.make_async_copy(source, out_ref, sems.at[at]))
+        copies[-1].start()
+    for copy in copies:
+        copy.wait()
+
+
+def take(tokens, parts):
+    _, block, local = tokens.shape
+    outs = pl.pallas_call(
+        take_kernel,
+        out_shape=(shape(block // parts, local),) * (2 * parts),
+        in_specs=[pl.BlockSpec(memory_space=pl.ANY)],
+        out_specs=(VMEM,) * (2 * parts),
+        scratch_shapes=[pltpu.SemaphoreType.DMA((2 * parts,))],
+        name="take",
+        cost_estimate=pl.CostEstimate(flops=0, bytes_accessed=4 * tokens.size, transcendentals=0),
+        compiler_params=pltpu.CompilerParams(vmem_limit_bytes=4 << 20),
+    )(tokens)
+    return outs[:parts], outs[parts:]
+
+
 def mix_kernel(count, last, toeplitz_ref, *refs):
-    sources, others, out_ref = refs[:count], refs[count:-1], refs[-1]
+    sources, refs = refs[:count], refs[count:]
+    gate_ref, refs = (refs[0], refs[1:]) if last else (None, refs)
+    total_ref, outs = refs[0] if last else None, refs[1:] if last else refs
     heads = toeplitz_ref.shape[0]
-    wide = out_ref.shape[1] // heads
+    wide = outs[0].shape[1] // heads
     for head in range(heads):
         lanes = slice(head * wide, (head + 1) * wide)
         stacked = jnp.concatenate([source[:, lanes] for source in sources], axis=0)
         mixed = jnp.dot(toeplitz_ref[head], stacked, preferred_element_type=jnp.float32)
-        if len(others) > last:
-            mixed += others[-1][:, lanes]
         if last:
-            gate = others[0][:, lanes].astype(jnp.float32)
+            mixed += total_ref[:, lanes]
+            gate = gate_ref[:, lanes].astype(jnp.float32)
             mixed = gate / (1.0 + jnp.exp(-gate)) * mixed
-        out_ref[:, lanes] = mixed.astype(out_ref.dtype)
-
-
-def mix(toeplitz_blocks, sources, total, gating):
+        mixed = mixed.astype(outs[0].dtype)
+        outs[0][:, lanes] = mixed
+        for at, out_ref in enumerate(outs[1:]):
+            rows = out_ref.shape[0]
+            out_ref[:, lanes] = mixed[at * rows : (at + 1) * rows]
+
+
+def mix(toeplitz_blocks, sources, total, gating, parts):
     block, local = sources[0].shape
     last = gating is not None
-    others = ([gating] if last else []) + ([total] if total is not None else [])
+    others = [gating, total] if last else []
+    outs = (shape(block, local, dtype=jnp.bfloat16 if last else jnp.float32),)
+    if parts > 1:
+        outs += (shape(block // parts, local),) * parts
     return call(
-        functools.partial(mix_kernel, len(sources), int(last)),
-        shape(block, local, dtype=jnp.bfloat16 if last else jnp.float32),
+        functools.partial(mix_kernel, len(sources), last),
+        outs,
         [VMEM] * (1 + len(sources) + len(others)),
         2 * len(sources) * block * block * local,
         toeplitz_blocks.size * 2 + (len(sources) + 4) * block * local * 2,
     )(toeplitz_blocks, *sources, *others)
 
 
-def product(own_ref, peer_ref, weight_ref):
-    depth = own_ref.shape[1]
+def rows_of(refs):
+    return refs[0][...] if len(refs) == 1 else jnp.concatenate([ref[...] for ref in refs], axis=0)
+
+
+def product(own_refs, peer_refs, weight_ref):
+    depth = own_refs[0].shape[1]
     chan = lax.axis_index("chan")
     own_rows = weight_ref[pl.ds(pl.multiple_of(chan * depth, depth), depth), :]
     peer_rows = weight_ref[pl.ds(pl.multiple_of((1 - chan) * depth, depth), depth), :]
-    total = jnp.dot(own_ref[...], own_rows, preferred_element_type=jnp.float32)
-    return total + jnp.dot(peer_ref[...], peer_rows, preferred_element_type=jnp.float32)
-
-
-def project_kernel(own_ref, peer_ref, weight_ref, *out_refs):
-    total = product(own_ref, peer_ref, weight_ref)
+    total = jnp.dot(rows_of(own_refs), own_rows, preferred_element_type=jnp.float32)
+    return total + jnp.dot(rows_of(peer_refs), peer_rows, preferred_element_type=jnp.float32)
+
+
+def project_kernel(parts, weight_ref, *refs):
+    own_refs, peer_refs, out_refs = refs[:parts], refs[parts : 2 * parts], refs[2 * parts :]
+    total = product(own_refs, peer_refs, weight_ref)
     wide = total.shape[1] // len(out_refs)
     for at, out_ref in enumerate(out_refs):
         out_ref[...] = total[:, at * wide : (at + 1) * wide].astype(jnp.bfloat16)
 
 
 def project(own, peer, weight, count):
-    block, _ = own.shape
+    block = own[0].shape[0] * len(own)
     return call(
-        project_kernel,
+        functools.partial(project_kernel, len(own)),
         tuple(shape(block, weight.shape[1] // count) for _ in range(count)),
-        [VMEM, VMEM, VMEM],
+        [VMEM] * (1 + 2 * len(own)),
         2 * block * weight.size,
-        2 * weight.size + 6 * own.size,
-    )(own, peer, weight)
+        2 * weight.size + 4 * block * weight.shape[0],
+    )(weight, *own, *peer)
 
 
 def step_kernel(own_ref, peer_ref, out_own_ref, out_peer_ref, *refs):
@@ -183,7 +227,8 @@
     )(own, peer, out_own, out_peer, in_weight)
 
 
-def finish_kernel(own_ref, peer_ref, weight_ref, first_ref, first_home_ref, near_ref, out_ref):
+def finish_kernel(parts, weight_ref, first_ref, first_home_ref, near_ref, *refs):
+    own_refs, peer_refs, out_ref = refs[:parts], refs[parts:-1], refs[-1]
     section = lax.axis_index("section")
     sequence, _ = position()
 
@@ -194,20 +239,20 @@
 
     @pl.when(section == 1)
     def _():
-        out_ref[0, 1 - sequence] = product(own_ref, peer_ref, weight_ref).astype(jnp.bfloat16)
+        out_ref[0, 1 - sequence] = product(own_refs, peer_refs, weight_ref).astype(jnp.bfloat16)
         out_ref[0, sequence] = near_ref[...]
 
 
 def finish(own, peer, weight, first, first_home, near):
     block, local = first.shape
     return call(
-        finish_kernel,
+        functools.partial(finish_kernel, len(own)),
         shape(1, MB, block, local),
-        [VMEM] * 6,
-        4 * block * local * local,
-        weight.size * 2 + 7 * own.size * 2,
+        [VMEM] * (4 + 2 * len(own)),
+        2 * block * weight.size,
+        weight.size * 2 + 14 * first.size,
         out_spec=pl.BlockSpec(),
-    )(own, peer, weight, first, first_home, near)
+    )(weight, first, first_home, near, *own, *peer)
 
 
 def both_layers(tokens, in_proj, filters, out_proj, widths):
@@ -215,7 +260,7 @@
     half = count // 2
     section = lax.axis_index("section")
     block = tokens.shape[1]
-    sequence, _ = position()
+    _, _ = position()
 
     def swap(value, axis):
         return lax.ppermute(value, axis, [(0, 1), (1, 0)])
@@ -247,9 +292,16 @@
     def halves(value):
         return value[: value.shape[0] // 2], value[value.shape[0] // 2 :]
 
-    swapped = across(lax.dynamic_index_in_dim(tokens, 1 - sequence, 0, False), 1, 1)
-    current = pick(lax.optimization_barrier(lax.dynamic_index_in_dim(tokens, sequence, 0, False)), swapped)
-    peer = swap(current, "chan")
+    def each(move, values):
+        moved = []
+        for value in values:
+            moved.append(move(value))
+        return moved
+
+    other_tokens, own_tokens = take(tokens, PARTS)
+    swapped = each(lambda value: across(value, 1, 1), other_tokens)
+    current = [pick(own, moved) for own, moved in zip(own_tokens, swapped)]
+    peer = each(lambda value: swap(value, "chan"), current)
 
     in_near = in_proj[0].reshape(in_proj.shape[1], -1)
     in_far = swap(in_near, "section")
@@ -269,14 +321,14 @@
         near = [signal]
         for apart in range(1, REACH):
             near.append(lax.ppermute(signal, "seq", [(i, i ^ apart) for i in range(count)]))
-        return near + [swap(value, "section") for value in near]
-
-    def mixed(layer, sources, gating):
-        total = None
+        return near + each(lambda value: swap(value, "section"), near)
+
+    def mixed(layer, sources, gating, parts):
+        total = (None,)
         for group, members in enumerate(groups):
             last = group == len(groups) - 1
             chosen = [sources[slot] for slot in members]
-            total = mix(blocks[layer][group], chosen, total, gating if last else None)
+            total = mix(blocks[layer][group], chosen, total[0], gating if last else None, parts if last else 1)
         return total
 
     in_first, in_last = pick(in_near, in_far), pick(in_far, in_near)
@@ -290,17 +342,18 @@
     out_peer = pick(jnp.concatenate([part, other]), jnp.concatenate([other, part]))
     out_first, out_last = pick(out_near, out_far), pick(out_far, out_near)
 
-    gated = mixed(0, sources, gating)
+    (gated,) = mixed(0, sources, gating, 1)
     gated_peer = swap(gated, "chan")
     first, signal, gating = step(gated, gated_peer, out_first, out_peer, in_last)
-    gated = mixed(1, gathered(signal), gating)
-
-    moved = across(gated, 1, 1)
+    sources = gathered(signal)
     first_home = across(first, 1, 0)
+    gated, *parts = mixed(1, sources, gating, PARTS)
+
+    moved = each(lambda value: across(value, 1, 1), parts)
     gated_peer = swap_in(gated, 0)
-    (second,) = project(gated, gated_peer, out_last, 1)
+    (second,) = project([gated], [gated_peer], out_last, 1)
     second_near = lax.ppermute(second, "section", [(0, 1)])
-    moved_peer = swap_in(moved, 1)
+    moved_peer = each(lambda value: swap_in(value, 1), moved)
     return finish(moved, moved_peer, out_last, first, first_home, second_near)
 
 

time: 92.6 us -> 93.5 us (level)
  starting transfers between devices: 33.5 us -> 45.5 us
  waiting for transfers between devices: 38.2 us -> 28.6 us
  local copies, waits for them, and re-layouts: 4.02 us -> 2.22 us
    ppermute x3 -> x5, starting transfers between devices: 11.6 us -> 18.7 us  [across(): return lax.ppermute(value, ('seq', 'section'), pairs)]
    ppermute x3 -> x5, waiting for transfers between devices: 12.4 us -> 7.93 us  [across(): return lax.ppermute(value, ('seq', 'section'), pairs)]
    ppermute x2 -> x3, starting transfers between devices: 2.68 us -> 5.95 us  [swap_in(): lax.ppermute(value, ('chan', 'section'), [(at, 2 + at), (2 + at, at)])]
    ppermute x15 -> x16, waiting for transfers between devices: 10.9 us -> 7.78 us  [swap(): return lax.ppermute(value, axis, [(0, 1), (1, 0)])]
    squeeze x1 -> x0, local copies, waits for them, and re-layouts: 1.76 us -> none  [both_layers(): lax.dynamic_index_in_dim(tokens, 1 - sequence, 0, False)]
    ppermute x15 -> x16, starting transfers between devices: 12.7 us -> 14.2 us  [swap(): return lax.ppermute(value, axis, [(0, 1), (1, 0)])]
    ppermute x2 -> x3, waiting for transfers between devices: 5.08 us -> 3.54 us  [swap_in(): lax.ppermute(value, ('chan', 'section'), [(at, 2 + at), (2 + at, at)])]
    pallas_call x7 -> x8, Pallas kernels: 5.2 us -> 5.97 us  [the longest x4 2.89 us: mix(): call(functools.partial(mix_kernel, len(sources), last), outs, [VMEM] * (1...]
  transfers between devices with their start and end apart: 27 -> 31, of which waited for: 11 -> 12; matrix products, arithmetic and copies ran while one was open for 8% -> 6% of each run, Pallas kernels for 7% -> 8%
where the time goes in v1:
time: 93.5 us; the launch traced here: 93.1 us
  starting transfers between devices  45.5 us (49%)
  waiting for transfers between devices  28.6 us (31%)
  Pallas kernels  11.2 us (12%)
  other arithmetic  5.3 us (6%)
  local copies, waits for them, and re-layouts  2.22 us (2%)
    ppermute x5, starting transfers between devices, across(): return lax.ppermute(value, ('seq', 'section'), pairs)  18.7 us
    ppermute x16, starting transfers between devices, swap(): return lax.ppermute(value, axis, [(0, 1), (1, 0)])  14.2 us
    ppermute x6, waiting for transfers between devices, gathered(): lax.ppermute(signal, 'seq', [(i, i ^ apart) for i in range(count)])  9.33 us
    ppermute x5, waiting for transfers between devices, across(): return lax.ppermute(value, ('seq', 'section'), pairs)  7.93 us
    ppermute x16, waiting for transfers between devices, swap(): return lax.ppermute(value, axis, [(0, 1), (1, 0)])  7.78 us
    ppermute x3, starting transfers between devices, swap_in(): lax.ppermute(value, ('chan', 'section'), [(at, 2 + at), (2 + at, at)])  5.95 us
    ppermute x6, starting transfers between devices, gathered(): lax.ppermute(signal, 'seq', [(i, i ^ apart) for i in range(count)])  5.36 us
    select_n x6, other arithmetic, pick(): return jnp.where(section == 0, zero, one)  5.3 us
  transfers between devices with their start and end apart: 31, of which 12 were waited for; matrix products, arithmetic and copies ran while one was open for 6% of the time, Pallas kernels for 8%

profile of v1, /device:TPU:1, one launch (start us, length us, event | category | flops | bytes accessed | tf_op | source)
XLA Modules:
  0.0 93.1 jit_solution(15574956863069533638)
XLA Ops:
  0.0 2.2 %copy.6 = bf16[128,8,2,512]{3,1,2,0:T(8,128)(2,1)S(1)} copy(bf16[128,8,2,512]{3,2,1,0:T(2,128)(2,1)} %bitcast.14) | data formatting | bytes 4194304
  2.2 0.1 collective-permute-start.2
  2.3 0.5 collective-permute-start
  2.8 0.7 take.1
  3.5 5.3 %collective-permute-start.3 = (bf16[128,512]{1,0:T(8,128)(2,1)S(1)}, bf16[128,512]{1,0:T(8,128)(2,1)S(1)}, u32[]{:S(2)}, u32[]{:S(2)}) collective-permute-start(bf16[128,512]{1,0:T(8,128)(2,1)S(1)} %get-tuple-element.24), channel_id=1, source_target_pairs={{1,17},{5,21},{9,25},{13,29},{17,1},{21,5},{25,9},{29,13},{3,19},{... | collective-permute-start | bytes 393224 | tf_op jit(solution)/shard_map/ppermute | solution.py:273
  8.8 1.9 %collective-permute-start.4 = (bf16[128,512]{1,0:T(8,128)(2,1)S(1)}, bf16[128,512]{1,0:T(8,128)(2,1)S(1)}, u32[]{:S(2)}, u32[]{:S(2)}) collective-permute-start(bf16[128,512]{1,0:T(8,128)(2,1)S(1)} %get-tuple-element.26), channel_id=1, source_target_pairs={{1,17},{5,21},{9,25},{13,29},{17,1},{21,5},{25,9},{29,13},{3,19},{... | collective-permute-start | bytes 393224 | tf_op jit(solution)/shard_map/ppermute | solution.py:273
  10.7 1.8 %collective-permute-done.3 = bf16[128,512]{1,0:T(8,128)(2,1)S(1)} collective-permute-done((bf16[128,512]{1,0:T(8,128)(2,1)S(1)}, bf16[128,512]{1,0:T(8,128)(2,1)S(1)}, u32[]{:S(2)}, u32[]{:S(2)}) %collective-permute-start.3) | collective-permute-done | bytes 131104 | tf_op jit(solution)/shard_map/ppermute | solution.py:273
  12.6 1.3 %collective-permute-start.5 = (bf16[128,512]{1,0:T(8,128)(2,1)S(1)}, bf16[128,512]{1,0:T(8,128)(2,1)S(1)}, u32[]{:S(2)}, u32[]{:S(2)}) collective-permute-start(bf16[128,512]{1,0:T(8,128)(2,1)S(1)} %broadcast_select_fusion.5.refs_0_), channel_id=1, source_target_pairs={{0,2},{2,0},{1,3},{3,1},{4,6},{6,4},{5,7},{7,5},{8,10},{10,8},{9,1... | collective-permute-start | bytes 393224 | tf_op jit(solution)/shard_map/ppermute | solution.py:266
  13.9 2.9 %collective-permute-done.4 = bf16[128,512]{1,0:T(8,128)(2,1)S(1)} collective-permute-done((bf16[128,512]{1,0:T(8,128)(2,1)S(1)}, bf16[128,512]{1,0:T(8,128)(2,1)S(1)}, u32[]{:S(2)}, u32[]{:S(2)}) %collective-permute-start.4) | collective-permute-done | bytes 131104 | tf_op jit(solution)/shard_map/ppermute | solution.py:273
  16.8 1.3 %collective-permute-start.6 = (bf16[128,512]{1,0:T(8,128)(2,1)S(1)}, bf16[128,512]{1,0:T(8,128)(2,1)S(1)}, u32[]{:S(2)}, u32[]{:S(2)}) collective-permute-start(bf16[128,512]{1,0:T(8,128)(2,1)S(1)} %broadcast_select_fusion.4.refs_1_), channel_id=1, source_target_pairs={{0,2},{2,0},{1,3},{3,1},{4,6},{6,4},{5,7},{7,5},{8,10},{10,8},{9,1... | collective-permute-start | bytes 393224 | tf_op jit(solution)/shard_map/ppermute | solution.py:266
  18.1 1.3 %slice_select_fusion = bf16[512,512]{1,0:T(8,128)(2,1)S(1)} fusion(bf16[1024,512]{1,0:T(8,128)(2,1)} %collective-permute-done, bf16[1,1024,512]{2,1,0:T(8,128)(2,1)} %param.8, pred[]{:T(512)S(6)} %eq.2), kind=kLoop, calls=%fused_computation.5 | loop fusion | flops 262144 | bytes 1572865 | tf_op jit(solution)/shard_map/jit(_where)/select_n | solution.py:276
  19.4 1.9 %broadcast_select_fusion = (bf16[1024,1024]{1,0:T(8,128)(2,1)S(1)}, bf16[1024,1024]{1,0:T(8,128)(2,1)S(1)}) fusion(bf16[1024,1024]{1,0:T(8,128)(2,1)} %collective-permute-done.2, bf16[1024,1024]{1,0:T(8,128)(2,1)S(1)} %bitcast.13, pred[]{:T(512)S(6)} %eq.2), kind=kLoop, calls=%fused_computation | loop fusion | flops 2097152 | bytes 8388609 | tf_op jit(solution)/shard_map/jit(_where)/select_n | solution.py:276
  21.2 0.0 copy-start.1
  21.3 0.0 copy-start.2
  21.3 0.0 collective-permute-done.5.refs_2_
  21.3 1.1 %collective-permute-done.6.refs_3_ = bf16[128,512]{1,0:T(8,128)(2,1)S(1)} collective-permute-done((bf16[128,512]{1,0:T(8,128)(2,1)S(1)}, bf16[128,512]{1,0:T(8,128)(2,1)S(1)}, u32[]{:S(2)}, u32[]{:S(2)}) %collective-permute-start.6) | collective-permute-done | bytes 131104 | tf_op jit(solution)/shard_map/ppermute | solution.py:266
  22.4 0.7 shard_map.55
  23.1 1.3 %collective-permute-start.15 = (bf16[512,512]{1,0:T(8,128)(2,1)S(1)}, bf16[512,512]{1,0:T(8,128)(2,1)S(1)}, u32[]{:S(2)}, u32[]{:S(2)}) collective-permute-start(bf16[512,512]{1,0:T(8,128)(2,1)S(1)} %slice_select_fusion), channel_id=1, source_target_pairs={{0,2},{2,0},{1,3},{3,1},{4,6},{6,4},{5,7},{7,5},{8,10},{10,8},{9,1... | collective-permute-start | bytes 1572872 | tf_op jit(solution)/shard_map/ppermute | solution.py:266
  24.4 1.2 %collective-permute-start.12 = (bf16[256,512]{1,0:T(8,128)(2,1)S(1)}, bf16[256,512]{1,0:T(8,128)(2,1)S(1)}, u32[]{:S(2)}, u32[]{:S(2)}) collective-permute-start(bf16[256,512]{1,0:T(8,128)(2,1)S(1)} %get-tuple-element.27.refs_0_), channel_id=1, source_target_pairs={{0,4},{4,0},{8,12},{12,8},{16,20},{20,16},{24,28},{28,24},{1,5},{5... | collective-permute-start | bytes 786440 | tf_op jit(solution)/shard_map/ppermute | solution.py:323
  25.6 0.0 collective-permute-start.9
  25.6 1.4 %collective-permute-start.7 = (bf16[256,512]{1,0:T(8,128)(2,1)S(1)}, bf16[256,512]{1,0:T(8,128)(2,1)S(1)}, u32[]{:S(2)}, u32[]{:S(2)}) collective-permute-start(bf16[256,512]{1,0:T(8,128)(2,1)S(1)} %get-tuple-element.27.refs_0_), channel_id=1, source_target_pairs={{0,8},{4,12},{8,0},{12,4},{16,24},{20,28},{24,16},{28,20},{1,9},{5... | collective-permute-start | bytes 786440 | tf_op jit(solution)/shard_map/ppermute | solution.py:323
  27.0 1.2 %collective-permute-done.1.far_ref = bf16[4,2304]{1,0:T(4,128)(2,1)S(1)} collective-permute-done((bf16[4,2304]{1,0:T(4,128)(2,1)S(1)}, bf16[4,2304]{1,0:T(4,128)(2,1)S(1)}, u32[]{:S(2)}, u32[]{:S(2)}) %collective-permute-start.1) | collective-permute-done | bytes 18464 | tf_op jit(solution)/shard_map/ppermute | solution.py:266
  28.2 0.2 collective-permute-start.11
  28.4 4.0 %collective-permute-done.12.refs_2_ = bf16[256,512]{1,0:T(8,128)(2,1)S(1)} collective-permute-done((bf16[256,512]{1,0:T(8,128)(2,1)S(1)}, bf16[256,512]{1,0:T(8,128)(2,1)S(1)}, u32[]{:S(2)}, u32[]{:S(2)}) %collective-permute-start.12) | collective-permute-done | bytes 262176 | tf_op jit(solution)/shard_map/ppermute | solution.py:323
  32.4 0.5 collective-permute-start.10
  32.9 0.7 collective-permute-done.7.refs_0_
  33.7 0.0 collective-permute-start.8
  33.7 0.0 collective-permute-done.15
  33.7 0.5 collective-permute-start.16
  34.2 1.9 %toeplitz.2 = (bf16[4,256,1024]{2,1,0:T(8,128)(2,1)S(1)}, bf16[4,256,1024]{2,1,0:T(8,128)(2,1)S(1)}) custom-call(s32[2]{0:T(128)S(1)} %copy-done.2, bf16[4,2304]{1,0:T(4,128)(2,1)S(1)} %bitcast.10, bf16[4,2304]{1,0:T(4,128)(2,1)S(1)} %collective-permute-done.1.far_ref), custom_call_target="tpu_custom_call" | custom-call | flops 83886080 | bytes 4194304 | tf_op jit(solution)/shard_map/toeplitz/pallas_call | solution.py:80
  36.1 0.0 collective-permute-done.11.refs_1_
  36.1 0.0 collective-permute-done.13.refs_3_
  36.1 0.7 shard_map.56.refs_5_
  36.9 0.0 collective-permute-done.10.refs_3_
  36.9 0.7 shard_map.57.own_ref
  37.6 0.3 collective-permute-start.14
  37.9 1.7 %broadcast_select_fusion.2 = (bf16[1024,512]{1,0:T(8,128)(2,1)S(1)}, bf16[1024,512]{1,0:T(8,128)(2,1)S(1)}) fusion(bf16[1024,512]{1,0:T(8,128)(2,1)} %collective-permute-done, pred[]{:T(512)S(6)} %eq.2, bf16[1,1024,512]{2,1,0:T(8,128)(2,1)} %param.8), kind=kLoop, calls=%fused_computation.3 | loop fusion | flops 1048576 | bytes 4194305 | tf_op jit(solution)/shard_map/jit(_where)/select_n | solution.py:276
  39.6 0.5 maximum_select_fusion.out_peer_ref
  40.1 5.4 %collective-permute-done.14.peer_ref = bf16[256,512]{1,0:T(8,128)(2,1)S(1)} collective-permute-done((bf16[256,512]{1,0:T(8,128)(2,1)S(1)}, bf16[256,512]{1,0:T(8,128)(2,1)S(1)}, u32[]{:S(2)}, u32[]{:S(2)}) %collective-permute-start.14) | collective-permute-done | bytes 262176 | tf_op jit(solution)/shard_map/ppermute | solution.py:266
  45.5 1.4 %step.1 = (bf16[256,512]{1,0:T(8,128)(2,1)S(1)}, bf16[256,512]{1,0:T(8,128)(2,1)S(1)}, bf16[256,512]{1,0:T(8,128)(2,1)S(1)}) custom-call(bf16[256,512]{1,0:T(8,128)(2,1)S(1)} %shard_map.57.own_ref, bf16[256,512]{1,0:T(8,128)(2,1)S(1)} %collective-permute-done.14.peer_ref, bf16[1024,512]{1,0:T(8,128)(2,1)S(1)} %get-tuple-element.41.out_own_ref, ...), custom_call_target="tpu_custom_call" | custom-call | flops 1073741824 | bytes 5505024 | tf_op jit(solution)/shard_map/step/pallas_call | solution.py:216
  46.9 1.3 %collective-permute-start.23 = (bf16[256,512]{1,0:T(8,128)(2,1)S(1)}, bf16[256,512]{1,0:T(8,128)(2,1)S(1)}, u32[]{:S(2)}, u32[]{:S(2)}) collective-permute-start(bf16[256,512]{1,0:T(8,128)(2,1)S(1)} %get-tuple-element.33.refs_0_), channel_id=1, source_target_pairs={{0,4},{4,0},{8,12},{12,8},{16,20},{20,16},{24,28},{28,24},{1,5},{5... | collective-permute-start | bytes 786440 | tf_op jit(solution)/shard_map/ppermute | solution.py:323
  48.2 0.1 collective-permute-start.18
  48.3 1.3 %collective-permute-start.20 = (bf16[256,512]{1,0:T(8,128)(2,1)S(1)}, bf16[256,512]{1,0:T(8,128)(2,1)S(1)}, u32[]{:S(2)}, u32[]{:S(2)}) collective-permute-start(bf16[256,512]{1,0:T(8,128)(2,1)S(1)} %get-tuple-element.33.refs_0_), channel_id=1, source_target_pairs={{0,12},{4,8},{8,4},{12,0},{16,28},{20,24},{24,20},{28,16},{1,13},{... | collective-permute-start | bytes 786440 | tf_op jit(solution)/shard_map/ppermute | solution.py:323
  49.6 1.7 %collective-permute-start.22 = (bf16[256,512]{1,0:T(8,128)(2,1)S(1)}, bf16[256,512]{1,0:T(8,128)(2,1)S(1)}, u32[]{:S(2)}, u32[]{:S(2)}) collective-permute-start(bf16[256,512]{1,0:T(8,128)(2,1)S(1)} %get-tuple-element.33.refs_0_), channel_id=1, source_target_pairs={{0,1},{1,0},{2,3},{3,2},{4,5},{5,4},{6,7},{7,6},{8,9},{9,8},{10,11... | collective-permute-start | bytes 786440 | tf_op jit(solution)/shard_map/ppermute | solution.py:266
  51.3 2.6 %collective-permute-done.23.refs_2_ = bf16[256,512]{1,0:T(8,128)(2,1)S(1)} collective-permute-done((bf16[256,512]{1,0:T(8,128)(2,1)S(1)}, bf16[256,512]{1,0:T(8,128)(2,1)S(1)}, u32[]{:S(2)}, u32[]{:S(2)}) %collective-permute-start.23) | collective-permute-done | bytes 262176 | tf_op jit(solution)/shard_map/ppermute | solution.py:323
  54.0 2.2 %collective-permute-start.24 = (bf16[256,512]{1,0:T(8,128)(2,1)S(1)}, bf16[256,512]{1,0:T(8,128)(2,1)S(1)}, u32[]{:S(2)}, u32[]{:S(2)}) collective-permute-start(bf16[256,512]{1,0:T(8,128)(2,1)S(1)} %collective-permute-done.23.refs_2_), channel_id=1, source_target_pairs={{0,1},{1,0},{2,3},{3,2},{4,5},{5,4},{6,7},{7,6},{8,9},{9,8},{10,11... | collective-permute-start | bytes 786440 | tf_op jit(solution)/shard_map/ppermute | solution.py:266
  56.1 2.4 %collective-permute-start.19 = (bf16[256,512]{1,0:T(8,128)(2,1)S(1)}, bf16[256,512]{1,0:T(8,128)(2,1)S(1)}, u32[]{:S(2)}, u32[]{:S(2)}) collective-permute-start(bf16[256,512]{1,0:T(8,128)(2,1)S(1)} %collective-permute-done.18.refs_0_), channel_id=1, source_target_pairs={{0,1},{1,0},{2,3},{3,2},{4,5},{5,4},{6,7},{7,6},{8,9},{9,8},{10,11... | collective-permute-start | bytes 786440 | tf_op jit(solution)/shard_map/ppermute | solution.py:266
  58.6 1.9 %collective-permute-done.20.refs_2_ = bf16[256,512]{1,0:T(8,128)(2,1)S(1)} collective-permute-done((bf16[256,512]{1,0:T(8,128)(2,1)S(1)}, bf16[256,512]{1,0:T(8,128)(2,1)S(1)}, u32[]{:S(2)}, u32[]{:S(2)}) %collective-permute-start.20) | collective-permute-done | bytes 262176 | tf_op jit(solution)/shard_map/ppermute | solution.py:323
  60.5 2.0 %collective-permute-start.21 = (bf16[256,512]{1,0:T(8,128)(2,1)S(1)}, bf16[256,512]{1,0:T(8,128)(2,1)S(1)}, u32[]{:S(2)}, u32[]{:S(2)}) collective-permute-start(bf16[256,512]{1,0:T(8,128)(2,1)S(1)} %collective-permute-done.20.refs_2_), channel_id=1, source_target_pairs={{0,1},{1,0},{2,3},{3,2},{4,5},{5,4},{6,7},{7,6},{8,9},{9,8},{10,11... | collective-permute-start | bytes 786440 | tf_op jit(solution)/shard_map/ppermute | solution.py:266
  62.5 1.9 %toeplitz.3 = (bf16[4,256,1024]{2,1,0:T(8,128)(2,1)S(1)}, bf16[4,256,1024]{2,1,0:T(8,128)(2,1)S(1)}) custom-call(s32[2]{0:T(128)S(1)} %copy-done.2, bf16[4,2304]{1,0:T(4,128)(2,1)S(1)} %bitcast.11, bf16[4,2304]{1,0:T(4,128)(2,1)S(1)} %collective-permute-done.1.far_ref), custom_call_target="tpu_custom_call" | custom-call | flops 83886080 | bytes 4194304 | tf_op jit(solution)/shard_map/toeplitz/pallas_call | solution.py:80
  64.4 0.7 shard_map.58.refs_5_
  65.2 0.7 shard_map.59
  65.9 0.7 collective-permute-start.25
  66.6 5.3 %collective-permute-start.17 = (bf16[256,512]{1,0:T(8,128)(2,1)S(1)}, bf16[256,512]{1,0:T(8,128)(2,1)S(1)}, u32[]{:S(2)}, u32[]{:S(2)}) collective-permute-start(bf16[256,512]{1,0:T(8,128)(2,1)S(1)} %get-tuple-element.31.first_ref), channel_id=1, source_target_pairs={{1,16},{5,20},{9,24},{13,28},{17,0},{21,4},{25,8},{29,12},{3,18},{... | collective-permute-start | bytes 786440 | tf_op jit(solution)/shard_map/ppermute | solution.py:273
  71.9 2.5 %collective-permute-start.27 = (bf16[128,512]{1,0:T(8,128)(2,1)S(1)}, bf16[128,512]{1,0:T(8,128)(2,1)S(1)}, u32[]{:S(2)}, u32[]{:S(2)}) collective-permute-start(bf16[128,512]{1,0:T(8,128)(2,1)S(1)} %get-tuple-element.37), channel_id=1, source_target_pairs={{1,17},{5,21},{9,25},{13,29},{17,1},{21,5},{25,9},{29,13},{3,19},{... | collective-permute-start | bytes 393224 | tf_op jit(solution)/shard_map/ppermute | solution.py:273
  74.4 3.7 %collective-permute-start.28 = (bf16[128,512]{1,0:T(8,128)(2,1)S(1)}, bf16[128,512]{1,0:T(8,128)(2,1)S(1)}, u32[]{:S(2)}, u32[]{:S(2)}) collective-permute-start(bf16[128,512]{1,0:T(8,128)(2,1)S(1)} %get-tuple-element.38), channel_id=1, source_target_pairs={{1,17},{5,21},{9,25},{13,29},{17,1},{21,5},{25,9},{29,13},{3,19},{... | collective-permute-start | bytes 393224 | tf_op jit(solution)/shard_map/ppermute | solution.py:273
  78.1 0.4 shard_map.60
  78.6 1.3 %collective-permute-start.26 = (bf16[256,512]{1,0:T(8,128)(2,1)S(1)}, bf16[256,512]{1,0:T(8,128)(2,1)S(1)}, u32[]{:S(2)}, u32[]{:S(2)}) collective-permute-start(bf16[256,512]{1,0:T(8,128)(2,1)S(1)} %shard_map.60), channel_id=1, source_target_pairs={{0,1},{2,3},{4,5},{6,7},{8,9},{10,11},{12,13},{14,15},{16,17},{18,... | collective-permute-start | bytes 786440 | tf_op jit(solution)/shard_map/ppermute | solution.py:355
  79.9 3.2 %collective-permute-done.27.refs_0_ = bf16[128,512]{1,0:T(8,128)(2,1)S(1)} collective-permute-done((bf16[128,512]{1,0:T(8,128)(2,1)S(1)}, bf16[128,512]{1,0:T(8,128)(2,1)S(1)}, u32[]{:S(2)}, u32[]{:S(2)}) %collective-permute-start.27) | collective-permute-done | bytes 131104 | tf_op jit(solution)/shard_map/ppermute | solution.py:273
  83.0 3.1 %collective-permute-start.29 = (bf16[128,512]{1,0:T(8,128)(2,1)S(1)}, bf16[128,512]{1,0:T(8,128)(2,1)S(1)}, u32[]{:S(2)}, u32[]{:S(2)}) collective-permute-start(bf16[128,512]{1,0:T(8,128)(2,1)S(1)} %collective-permute-done.27.refs_0_), channel_id=1, source_target_pairs={{1,3},{3,1},{5,7},{7,5},{9,11},{11,9},{13,15},{15,13},{17,19},{19,... | collective-permute-start | bytes 393224 | tf_op jit(solution)/shard_map/ppermute | solution.py:269
  86.2 2.2 %collective-permute-start.30 = (bf16[128,512]{1,0:T(8,128)(2,1)S(1)}, bf16[128,512]{1,0:T(8,128)(2,1)S(1)}, u32[]{:S(2)}, u32[]{:S(2)}) collective-permute-start(bf16[128,512]{1,0:T(8,128)(2,1)S(1)} %collective-permute-done.28.refs_1_), channel_id=1, source_target_pairs={{1,3},{3,1},{5,7},{7,5},{9,11},{11,9},{13,15},{15,13},{17,19},{19,... | collective-permute-start | bytes 393224 | tf_op jit(solution)/shard_map/ppermute | solution.py:269
  88.4 0.4 collective-permute-done.29.refs_2_
  88.7 3.1 %collective-permute-done.30.refs_3_ = bf16[128,512]{1,0:T(8,128)(2,1)S(1)} collective-permute-done((bf16[128,512]{1,0:T(8,128)(2,1)S(1)}, bf16[128,512]{1,0:T(8,128)(2,1)S(1)}, u32[]{:S(2)}, u32[]{:S(2)}) %collective-permute-start.30) | collective-permute-done | bytes 131104 | tf_op jit(solution)/shard_map/ppermute | solution.py:269
  91.9 1.2 %shard_map.61 = bf16[1,2,256,512]{3,2,1,0:T(8,128)(2,1)} custom-call(bf16[1024,512]{1,0:T(8,128)(2,1)S(1)} %get-tuple-element.42.weight_ref, bf16[256,512]{1,0:T(8,128)(2,1)S(1)} %get-tuple-element.31.first_ref, bf16[256,512]{1,0:T(8,128)(2,1)S(1)} %collective-permute-done.17.first_home_ref, bf16[256,512]{1,0:T(8,128)(2,1)S(1)} %collective-permute-done.26.near_ref, ...), custom_call_target="tpu_custom_call" | custom-call | flops 268435456 | bytes 2883584 | tf_op jit(solution)/shard_map/pallas_call | solution.py:248
  (22 shorter events, 0.1 us)
Async XLA Ops:
  0.0 2.8 %copy-start = (bf16[2,256,512]{2,1,0:T(8,128)(2,1)S(1)}, bf16[2,256,512]{2,1,0:T(8,128)(2,1)}, u32[]{:S(2)}) copy-start(bf16[2,256,512]{2,1,0:T(8,128)(2,1)} %tokens_ref.1) | copy-start | bytes 1572868
  2.2 17.1 %collective-permute-start.2 = (bf16[1024,1024]{1,0:T(8,128)(2,1)S(1)}, bf16[1024,1024]{1,0:T(8,128)(2,1)}, u32[]{:S(2)}, u32[]{:S(2)}) collective-permute-start(bf16[1024,1024]{1,0:T(8,128)(2,1)S(1)} %bitcast.12), channel_id=1, source_target_pairs={{0,1},{1,0},{2,3},{3,2},{4,5},{5,4},{6,7},{7,6},{8,9},{9,8},{10,11... | collective-permute-start | bytes 6291464 | tf_op jit(solution)/shard_map/ppermute | solution.py:266
  2.3 15.8 %collective-permute-start = (bf16[1024,512]{1,0:T(8,128)(2,1)}, bf16[1024,512]{1,0:T(8,128)(2,1)}, u32[]{:S(2)}, u32[]{:S(2)}) collective-permute-start(bf16[1024,512]{1,0:T(8,128)(2,1)} %bitcast), channel_id=1, source_target_pairs={{0,1},{1,0},{2,3},{3,2},{4,5},{5,4},{6,7},{7,6},{8,9},{9,8},{10,11... | collective-permute-start | bytes 3145736 | tf_op jit(solution)/shard_map/ppermute | solution.py:266
  3.5 9.0 %collective-permute-start.3 = (bf16[128,512]{1,0:T(8,128)(2,1)S(1)}, bf16[128,512]{1,0:T(8,128)(2,1)S(1)}, u32[]{:S(2)}, u32[]{:S(2)}) collective-permute-start(bf16[128,512]{1,0:T(8,128)(2,1)S(1)} %get-tuple-element.24), channel_id=1, source_target_pairs={{1,17},{5,21},{9,25},{13,29},{17,1},{21,5},{25,9},{29,13},{3,19},{... | collective-permute-start | bytes 393224 | tf_op jit(solution)/shard_map/ppermute | solution.py:273
  8.8 8.0 %collective-permute-start.4 = (bf16[128,512]{1,0:T(8,128)(2,1)S(1)}, bf16[128,512]{1,0:T(8,128)(2,1)S(1)}, u32[]{:S(2)}, u32[]{:S(2)}) collective-permute-start(bf16[128,512]{1,0:T(8,128)(2,1)S(1)} %get-tuple-element.26), channel_id=1, source_target_pairs={{1,17},{5,21},{9,25},{13,29},{17,1},{21,5},{25,9},{29,13},{3,19},{... | collective-permute-start | bytes 393224 | tf_op jit(solution)/shard_map/ppermute | solution.py:273
  12.6 8.7 %collective-permute-start.5 = (bf16[128,512]{1,0:T(8,128)(2,1)S(1)}, bf16[128,512]{1,0:T(8,128)(2,1)S(1)}, u32[]{:S(2)}, u32[]{:S(2)}) collective-permute-start(bf16[128,512]{1,0:T(8,128)(2,1)S(1)} %broadcast_select_fusion.5.refs_0_), channel_id=1, source_target_pairs={{0,2},{2,0},{1,3},{3,1},{4,6},{6,4},{5,7},{7,5},{8,10},{10,8},{9,1... | collective-permute-start | bytes 393224 | tf_op jit(solution)/shard_map/ppermute | solution.py:266
  16.8 5.6 %collective-permute-start.6 = (bf16[128,512]{1,0:T(8,128)(2,1)S(1)}, bf16[128,512]{1,0:T(8,128)(2,1)S(1)}, u32[]{:S(2)}, u32[]{:S(2)}) collective-permute-start(bf16[128,512]{1,0:T(8,128)(2,1)S(1)} %broadcast_select_fusion.4.refs_1_), channel_id=1, source_target_pairs={{0,2},{2,0},{1,3},{3,1},{4,6},{6,4},{5,7},{7,5},{8,10},{10,8},{9,1... | collective-permute-start | bytes 393224 | tf_op jit(solution)/shard_map/ppermute | solution.py:266
  21.2 5.8 %copy-start.1 = (bf16[1,4,2304]{2,1,0:T(4,128)(2,1)S(1)}, bf16[1,4,2304]{2,1,0:T(4,128)(2,1)}, u32[]{:S(2)}) copy-start(bf16[1,4,2304]{2,1,0:T(4,128)(2,1)} %param.7) | copy-start | bytes 55300
  21.3 12.9 %copy-start.2 = (s32[2]{0:T(128)S(1)}, s32[2]{0:T(128)}, u32[]{:S(2)}) copy-start(s32[2]{0:T(128)} %widths_ref.3) | copy-start | bytes 28
  23.1 10.5 %collective-permute-start.15 = (bf16[512,512]{1,0:T(8,128)(2,1)S(1)}, bf16[512,512]{1,0:T(8,128)(2,1)S(1)}, u32[]{:S(2)}, u32[]{:S(2)}) collective-permute-start(bf16[512,512]{1,0:T(8,128)(2,1)S(1)} %slice_select_fusion), channel_id=1, source_target_pairs={{0,2},{2,0},{1,3},{3,1},{4,6},{6,4},{5,7},{7,5},{8,10},{10,8},{9,1... | collective-permute-start | bytes 1572872 | tf_op jit(solution)/shard_map/ppermute | solution.py:266
  24.4 8.0 %collective-permute-start.12 = (bf16[256,512]{1,0:T(8,128)(2,1)S(1)}, bf16[256,512]{1,0:T(8,128)(2,1)S(1)}, u32[]{:S(2)}, u32[]{:S(2)}) collective-permute-start(bf16[256,512]{1,0:T(8,128)(2,1)S(1)} %get-tuple-element.27.refs_0_), channel_id=1, source_target_pairs={{0,4},{4,0},{8,12},{12,8},{16,20},{20,16},{24,28},{28,24},{1,5},{5... | collective-permute-start | bytes 786440 | tf_op jit(solution)/shard_map/ppermute | solution.py:323
  25.6 6.8 %collective-permute-start.9 = (bf16[256,512]{1,0:T(8,128)(2,1)S(1)}, bf16[256,512]{1,0:T(8,128)(2,1)S(1)}, u32[]{:S(2)}, u32[]{:S(2)}) collective-permute-start(bf16[256,512]{1,0:T(8,128)(2,1)S(1)} %get-tuple-element.27.refs_0_), channel_id=1, source_target_pairs={{0,12},{4,8},{8,4},{12,0},{16,28},{20,24},{24,20},{28,16},{1,13},{... | collective-permute-start | bytes 786440 | tf_op jit(solution)/shard_map/ppermute | solution.py:323
  25.6 8.0 %collective-permute-start.7 = (bf16[256,512]{1,0:T(8,128)(2,1)S(1)}, bf16[256,512]{1,0:T(8,128)(2,1)S(1)}, u32[]{:S(2)}, u32[]{:S(2)}) collective-permute-start(bf16[256,512]{1,0:T(8,128)(2,1)S(1)} %get-tuple-element.27.refs_0_), channel_id=1, source_target_pairs={{0,8},{4,12},{8,0},{12,4},{16,24},{20,28},{24,16},{28,20},{1,9},{5... | collective-permute-start | bytes 786440 | tf_op jit(solution)/shard_map/ppermute | solution.py:323
  27.0 1.2 %collective-permute-start.1 = (bf16[4,2304]{1,0:T(4,128)(2,1)S(1)}, bf16[4,2304]{1,0:T(4,128)(2,1)S(1)}, u32[]{:S(2)}, u32[]{:S(2)}) collective-permute-start(bf16[4,2304]{1,0:T(4,128)(2,1)S(1)} %bitcast.9), channel_id=1, source_target_pairs={{0,1},{1,0},{2,3},{3,2},{4,5},{5,4},{6,7},{7,6},{8,9},{9,8},{10,11... | collective-permute-start | bytes 55304 | tf_op jit(solution)/shard_map/ppermute | solution.py:266
  28.2 7.9 %collective-permute-start.11 = (bf16[256,512]{1,0:T(8,128)(2,1)S(1)}, bf16[256,512]{1,0:T(8,128)(2,1)S(1)}, u32[]{:S(2)}, u32[]{:S(2)}) collective-permute-start(bf16[256,512]{1,0:T(8,128)(2,1)S(1)} %get-tuple-element.27.refs_0_), channel_id=1, source_target_pairs={{0,1},{1,0},{2,3},{3,2},{4,5},{5,4},{6,7},{7,6},{8,9},{9,8},{10,11... | collective-permute-start | bytes 786440 | tf_op jit(solution)/shard_map/ppermute | solution.py:266
  32.4 3.7 %collective-permute-start.13 = (bf16[256,512]{1,0:T(8,128)(2,1)S(1)}, bf16[256,512]{1,0:T(8,128)(2,1)S(1)}, u32[]{:S(2)}, u32[]{:S(2)}) collective-permute-start(bf16[256,512]{1,0:T(8,128)(2,1)S(1)} %collective-permute-done.12.refs_2_), channel_id=1, source_target_pairs={{0,1},{1,0},{2,3},{3,2},{4,5},{5,4},{6,7},{7,6},{8,9},{9,8},{10,11... | collective-permute-start | bytes 786440 | tf_op jit(solution)/shard_map/ppermute | solution.py:266
  32.4 4.4 %collective-permute-start.10 = (bf16[256,512]{1,0:T(8,128)(2,1)S(1)}, bf16[256,512]{1,0:T(8,128)(2,1)S(1)}, u32[]{:S(2)}, u32[]{:S(2)}) collective-permute-start(bf16[256,512]{1,0:T(8,128)(2,1)S(1)} %collective-permute-done.9.refs_2_), channel_id=1, source_target_pairs={{0,1},{1,0},{2,3},{3,2},{4,5},{5,4},{6,7},{7,6},{8,9},{9,8},{10,11... | collective-permute-start | bytes 786440 | tf_op jit(solution)/shard_map/ppermute | solution.py:266
  33.7 3.2 %collective-permute-start.8 = (bf16[256,512]{1,0:T(8,128)(2,1)S(1)}, bf16[256,512]{1,0:T(8,128)(2,1)S(1)}, u32[]{:S(2)}, u32[]{:S(2)}) collective-permute-start(bf16[256,512]{1,0:T(8,128)(2,1)S(1)} %collective-permute-done.7.refs_0_), channel_id=1, source_target_pairs={{0,1},{1,0},{2,3},{3,2},{4,5},{5,4},{6,7},{7,6},{8,9},{9,8},{10,11... | collective-permute-start | bytes 786440 | tf_op jit(solution)/shard_map/ppermute | solution.py:266
  33.7 6.0 %collective-permute-start.16 = (bf16[512,512]{1,0:T(8,128)(2,1)S(1)}, bf16[512,512]{1,0:T(8,128)(2,1)S(1)}, u32[]{:S(2)}, u32[]{:S(2)}) collective-permute-start(bf16[512,512]{1,0:T(8,128)(2,1)S(1)} %collective-permute-done.15), channel_id=1, source_target_pairs={{0,1},{1,0},{2,3},{3,2},{4,5},{5,4},{6,7},{7,6},{8,9},{9,8},{10,11... | collective-permute-start | bytes 1572872 | tf_op jit(solution)/shard_map/ppermute | solution.py:266
  37.6 7.9 %collective-permute-start.14 = (bf16[256,512]{1,0:T(8,128)(2,1)S(1)}, bf16[256,512]{1,0:T(8,128)(2,1)S(1)}, u32[]{:S(2)}, u32[]{:S(2)}) collective-permute-start(bf16[256,512]{1,0:T(8,128)(2,1)S(1)} %shard_map.57.own_ref), channel_id=1, source_target_pairs={{0,2},{2,0},{1,3},{3,1},{4,6},{6,4},{5,7},{7,5},{8,10},{10,8},{9,1... | collective-permute-start | bytes 786440 | tf_op jit(solution)/shard_map/ppermute | solution.py:266
  46.9 7.1 %collective-permute-start.23 = (bf16[256,512]{1,0:T(8,128)(2,1)S(1)}, bf16[256,512]{1,0:T(8,128)(2,1)S(1)}, u32[]{:S(2)}, u32[]{:S(2)}) collective-permute-start(bf16[256,512]{1,0:T(8,128)(2,1)S(1)} %get-tuple-element.33.refs_0_), channel_id=1, source_target_pairs={{0,4},{4,0},{8,12},{12,8},{16,20},{20,16},{24,28},{28,24},{1,5},{5... | collective-permute-start | bytes 786440 | tf_op jit(solution)/shard_map/ppermute | solution.py:323
  48.2 7.9 %collective-permute-start.18 = (bf16[256,512]{1,0:T(8,128)(2,1)S(1)}, bf16[256,512]{1,0:T(8,128)(2,1)S(1)}, u32[]{:S(2)}, u32[]{:S(2)}) collective-permute-start(bf16[256,512]{1,0:T(8,128)(2,1)S(1)} %get-tuple-element.33.refs_0_), channel_id=1, source_target_pairs={{0,8},{4,12},{8,0},{12,4},{16,24},{20,28},{24,16},{28,20},{1,9},{5... | collective-permute-start | bytes 786440 | tf_op jit(solution)/shard_map/ppermute | solution.py:323
  48.3 12.2 %collective-permute-start.20 = (bf16[256,512]{1,0:T(8,128)(2,1)S(1)}, bf16[256,512]{1,0:T(8,128)(2,1)S(1)}, u32[]{:S(2)}, u32[]{:S(2)}) collective-permute-start(bf16[256,512]{1,0:T(8,128)(2,1)S(1)} %get-tuple-element.33.refs_0_), channel_id=1, source_target_pairs={{0,12},{4,8},{8,4},{12,0},{16,28},{20,24},{24,20},{28,16},{1,13},{... | collective-permute-start | bytes 786440 | tf_op jit(solution)/shard_map/ppermute | solution.py:323
  49.6 14.8 %collective-permute-start.22 = (bf16[256,512]{1,0:T(8,128)(2,1)S(1)}, bf16[256,512]{1,0:T(8,128)(2,1)S(1)}, u32[]{:S(2)}, u32[]{:S(2)}) collective-permute-start(bf16[256,512]{1,0:T(8,128)(2,1)S(1)} %get-tuple-element.33.refs_0_), channel_id=1, source_target_pairs={{0,1},{1,0},{2,3},{3,2},{4,5},{5,4},{6,7},{7,6},{8,9},{9,8},{10,11... | collective-permute-start | bytes 786440 | tf_op jit(solution)/shard_map/ppermute | solution.py:266
  54.0 10.5 %collective-permute-start.24 = (bf16[256,512]{1,0:T(8,128)(2,1)S(1)}, bf16[256,512]{1,0:T(8,128)(2,1)S(1)}, u32[]{:S(2)}, u32[]{:S(2)}) collective-permute-start(bf16[256,512]{1,0:T(8,128)(2,1)S(1)} %collective-permute-done.23.refs_2_), channel_id=1, source_target_pairs={{0,1},{1,0},{2,3},{3,2},{4,5},{5,4},{6,7},{7,6},{8,9},{9,8},{10,11... | collective-permute-start | bytes 786440 | tf_op jit(solution)/shard_map/ppermute | solution.py:266
  56.1 9.0 %collective-permute-start.19 = (bf16[256,512]{1,0:T(8,128)(2,1)S(1)}, bf16[256,512]{1,0:T(8,128)(2,1)S(1)}, u32[]{:S(2)}, u32[]{:S(2)}) collective-permute-start(bf16[256,512]{1,0:T(8,128)(2,1)S(1)} %collective-permute-done.18.refs_0_), channel_id=1, source_target_pairs={{0,1},{1,0},{2,3},{3,2},{4,5},{5,4},{6,7},{7,6},{8,9},{9,8},{10,11... | collective-permute-start | bytes 786440 | tf_op jit(solution)/shard_map/ppermute | solution.py:266
  60.5 4.7 %collective-permute-start.21 = (bf16[256,512]{1,0:T(8,128)(2,1)S(1)}, bf16[256,512]{1,0:T(8,128)(2,1)S(1)}, u32[]{:S(2)}, u32[]{:S(2)}) collective-permute-start(bf16[256,512]{1,0:T(8,128)(2,1)S(1)} %collective-permute-done.20.refs_2_), channel_id=1, source_target_pairs={{0,1},{1,0},{2,3},{3,2},{4,5},{5,4},{6,7},{7,6},{8,9},{9,8},{10,11... | collective-permute-start | bytes 786440 | tf_op jit(solution)/shard_map/ppermute | solution.py:266
  65.9 12.2 %collective-permute-start.25 = (bf16[256,512]{1,0:T(8,128)(2,1)S(1)}, bf16[256,512]{1,0:T(8,128)(2,1)S(1)}, u32[]{:S(2)}, u32[]{:S(2)}) collective-permute-start(bf16[256,512]{1,0:T(8,128)(2,1)S(1)} %get-tuple-element.36.refs_0_), channel_id=1, source_target_pairs={{0,2},{2,0},{4,6},{6,4},{8,10},{10,8},{12,14},{14,12},{16,18},{18,... | collective-permute-start | bytes 786440 | tf_op jit(solution)/shard_map/ppermute | solution.py:269
  66.6 21.8 %collective-permute-start.17 = (bf16[256,512]{1,0:T(8,128)(2,1)S(1)}, bf16[256,512]{1,0:T(8,128)(2,1)S(1)}, u32[]{:S(2)}, u32[]{:S(2)}) collective-permute-start(bf16[256,512]{1,0:T(8,128)(2,1)S(1)} %get-tuple-element.31.first_ref), channel_id=1, source_target_pairs={{1,16},{5,20},{9,24},{13,28},{17,0},{21,4},{25,8},{29,12},{3,18},{... | collective-permute-start | bytes 786440 | tf_op jit(solution)/shard_map/ppermute | solution.py:273
  71.9 11.1 %collective-permute-start.27 = (bf16[128,512]{1,0:T(8,128)(2,1)S(1)}, bf16[128,512]{1,0:T(8,128)(2,1)S(1)}, u32[]{:S(2)}, u32[]{:S(2)}) collective-permute-start(bf16[128,512]{1,0:T(8,128)(2,1)S(1)} %get-tuple-element.37), channel_id=1, source_target_pairs={{1,17},{5,21},{9,25},{13,29},{17,1},{21,5},{25,9},{29,13},{3,19},{... | collective-permute-start | bytes 393224 | tf_op jit(solution)/shard_map/ppermute | solution.py:273
  74.4 11.7 %collective-permute-start.28 = (bf16[128,512]{1,0:T(8,128)(2,1)S(1)}, bf16[128,512]{1,0:T(8,128)(2,1)S(1)}, u32[]{:S(2)}, u32[]{:S(2)}) collective-permute-start(bf16[128,512]{1,0:T(8,128)(2,1)S(1)} %get-tuple-element.38), channel_id=1, source_target_pairs={{1,17},{5,21},{9,25},{13,29},{17,1},{21,5},{25,9},{29,13},{3,19},{... | collective-permute-start | bytes 393224 | tf_op jit(solution)/shard_map/ppermute | solution.py:273
  78.6 13.3 %collective-permute-start.26 = (bf16[256,512]{1,0:T(8,128)(2,1)S(1)}, bf16[256,512]{1,0:T(8,128)(2,1)S(1)}, u32[]{:S(2)}, u32[]{:S(2)}) collective-permute-start(bf16[256,512]{1,0:T(8,128)(2,1)S(1)} %shard_map.60), channel_id=1, source_target_pairs={{0,1},{2,3},{4,5},{6,7},{8,9},{10,11},{12,13},{14,15},{16,17},{18,... | collective-permute-start | bytes 786440 | tf_op jit(solution)/shard_map/ppermute | solution.py:355
  83.0 5.7 %collective-permute-start.29 = (bf16[128,512]{1,0:T(8,128)(2,1)S(1)}, bf16[128,512]{1,0:T(8,128)(2,1)S(1)}, u32[]{:S(2)}, u32[]{:S(2)}) collective-permute-start(bf16[128,512]{1,0:T(8,128)(2,1)S(1)} %collective-permute-done.27.refs_0_), channel_id=1, source_target_pairs={{1,3},{3,1},{5,7},{7,5},{9,11},{11,9},{13,15},{15,13},{17,19},{19,... | collective-permute-start | bytes 393224 | tf_op jit(solution)/shard_map/ppermute | solution.py:269
  86.2 5.7 %collective-permute-start.30 = (bf16[128,512]{1,0:T(8,128)(2,1)S(1)}, bf16[128,512]{1,0:T(8,128)(2,1)S(1)}, u32[]{:S(2)}, u32[]{:S(2)}) collective-permute-start(bf16[128,512]{1,0:T(8,128)(2,1)S(1)} %collective-permute-done.28.refs_1_), channel_id=1, source_target_pairs={{1,3},{3,1},{5,7},{7,5},{9,11},{11,9},{13,15},{15,13},{17,19},{19,... | collective-permute-start | bytes 393224 | tf_op jit(solution)/shard_map/ppermute | solution.py:269

commit v2 on v1

--- a/solution.py
+++ b/solution.py
@@ -11,7 +11,8 @@
 BAND = 8
 REACH = BAND // 2
 MB = 2
-PARTS = 2
+LEAVING, HOMING = 1, 1 / 2
+GROUPS = ((0, REACH, 1, REACH + 1, 2, REACH + 2), (3, REACH + 3))
 
 
 VMEM = pl.BlockSpec(memory_space=pltpu.VMEM)
@@ -31,6 +32,11 @@
 
 def shape(*dims, dtype=jnp.bfloat16):
     return jax.ShapeDtypeStruct(dims, dtype)
+
+
+def two_parts(block, share):
+    first = round(block * share / 16) * 16
+    return tuple(rows for rows in (first, block - first) if rows)
 
 
 def position():
@@ -96,12 +102,12 @@
 def take_kernel(tokens_ref, *refs):
     outs, sems = refs[:-1], refs[-1]
     sequence, _ = position()
-    parts = len(outs) // 2
-    rows = outs[0].shape[0]
-    copies = []
+    copies, start = [], 0
     for at, out_ref in enumerate(outs):
-        held = 1 - sequence if at < parts else sequence
-        source = tokens_ref.at[held, pl.ds((at % parts) * rows, rows), :]
+        held = 1 - sequence if at < len(outs) // 2 else sequence
+        rows = out_ref.shape[0]
+        source = tokens_ref.at[held, pl.ds(start, rows), :]
+        start = (start + rows) % tokens_ref.shape[1]
         copies.append(pltpu.make_async_copy(source, out_ref, sems.at[at]))
         copies[-1].start()
     for copy in copies:
@@ -109,18 +115,18 @@
 
 
 def take(tokens, parts):
-    _, block, local = tokens.shape
+    local = tokens.shape[2]
     outs = pl.pallas_call(
         take_kernel,
-        out_shape=(shape(block // parts, local),) * (2 * parts),
-        in_specs=[pl.BlockSpec(memory_space=pl.ANY)],
-        out_specs=(VMEM,) * (2 * parts),
-        scratch_shapes=[pltpu.SemaphoreType.DMA((2 * parts,))],
+        out_shape=tuple(shape(rows, local) for rows in parts) * 2,
+        in_specs=[pl.BlockSpec(memory_space=pltpu.HBM)],
+        out_specs=(VMEM,) * (2 * len(parts)),
+        scratch_shapes=[pltpu.SemaphoreType.DMA((2 * len(parts),))],
         name="take",
         cost_estimate=pl.CostEstimate(flops=0, bytes_accessed=4 * tokens.size, transcendentals=0),
         compiler_params=pltpu.CompilerParams(vmem_limit_bytes=4 << 20),
-    )(tokens)
-    return outs[:parts], outs[parts:]
+    )(pltpu.with_memory_space_constraint(tokens, pltpu.HBM))
+    return outs[: len(parts)], outs[len(parts) :]
 
 
 def mix_kernel(count, last, toeplitz_ref, *refs):
@@ -139,9 +145,10 @@
             mixed = gate / (1.0 + jnp.exp(-gate)) * mixed
         mixed = mixed.astype(outs[0].dtype)
         outs[0][:, lanes] = mixed
-        for at, out_ref in enumerate(outs[1:]):
-            rows = out_ref.shape[0]
-            out_ref[:, lanes] = mixed[at * rows : (at + 1) * rows]
+        start = 0
+        for out_ref in outs[1:]:
+            out_ref[:, lanes] = mixed[start : start + out_ref.shape[0]]
+            start += out_ref.shape[0]
 
 
 def mix(toeplitz_blocks, sources, total, gating, parts):
@@ -149,8 +156,7 @@
     last = gating is not None
     others = [gating, total] if last else []
     outs = (shape(block, local, dtype=jnp.bfloat16 if last else jnp.float32),)
-    if parts > 1:
-        outs += (shape(block // parts, local),) * parts
+    outs += tuple(shape(rows, local) for rows in parts)
     return call(
         functools.partial(mix_kernel, len(sources), last),
         outs,
@@ -182,7 +188,7 @@
 
 
 def project(own, peer, weight, count):
-    block = own[0].shape[0] * len(own)
+    block = sum(value.shape[0] for value in own)
     return call(
         functools.partial(project_kernel, len(own)),
         tuple(shape(block, weight.shape[1] // count) for _ in range(count)),
@@ -227,10 +233,10 @@
     )(own, peer, out_own, out_peer, in_weight)
 
 
-def finish_kernel(parts, weight_ref, first_ref, first_home_ref, near_ref, *refs):
-    own_refs, peer_refs, out_ref = refs[:parts], refs[parts:-1], refs[-1]
+def finish_kernel(weight_ref, first_ref, first_home_ref, near_ref, home_ref, own_ref, peer_ref, out_ref):
     section = lax.axis_index("section")
     sequence, _ = position()
+    rows = home_ref.shape[0]
 
     @pl.when(section == 0)
     def _():
@@ -239,20 +245,21 @@
 
     @pl.when(section == 1)
     def _():
-        out_ref[0, 1 - sequence] = product(own_refs, peer_refs, weight_ref).astype(jnp.bfloat16)
+        out_ref[0, 1 - sequence, :rows] = home_ref[...]
+        out_ref[0, 1 - sequence, rows:] = product([own_ref], [peer_ref], weight_ref).astype(jnp.bfloat16)
         out_ref[0, sequence] = near_ref[...]
 
 
-def finish(own, peer, weight, first, first_home, near):
+def finish(weight, first, first_home, near, home, own, peer):
     block, local = first.shape
     return call(
-        functools.partial(finish_kernel, len(own)),
+        finish_kernel,
         shape(1, MB, block, local),
-        [VMEM] * (4 + 2 * len(own)),
-        2 * block * weight.size,
-        weight.size * 2 + 14 * first.size,
+        [VMEM] * 7,
+        block * weight.size,
+        weight.size * 2 + 12 * first.size,
         out_spec=pl.BlockSpec(),
-    )(weight, first, first_home, near, *own, *peer)
+    )(weight, first, first_home, near, home, own, peer)
 
 
 def both_layers(tokens, in_proj, filters, out_proj, widths):
@@ -264,9 +271,6 @@
 
     def swap(value, axis):
         return lax.ppermute(value, axis, [(0, 1), (1, 0)])
-
-    def swap_in(value, at):
-        return lax.ppermute(value, ("chan", "section"), [(at, 2 + at), (2 + at, at)])
 
     def across(value, from_section, to_section):
         pairs = [(2 * i + from_section, 2 * ((i + half) % count) + to_section) for i in range(count)]
@@ -298,7 +302,7 @@
             moved.append(move(value))
         return moved
 
-    other_tokens, own_tokens = take(tokens, PARTS)
+    other_tokens, own_tokens = take(tokens, two_parts(block, LEAVING))
     swapped = each(lambda value: across(value, 1, 1), other_tokens)
     current = [pick(own, moved) for own, moved in zip(own_tokens, swapped)]
     peer = each(lambda value: swap(value, "chan"), current)
@@ -310,7 +314,7 @@
     out_near = out_proj[0]
     out_far = swap(out_near, "section")
 
-    groups = ((0, REACH, 1, REACH + 1), (2, REACH + 2, REACH - 1, BAND - 1))
+    groups = GROUPS
     blocks = []
     for layer in range(2):
         blocks.append(toeplitz(layer, widths, taps, far_taps, block, groups))
@@ -328,7 +332,7 @@
         for group, members in enumerate(groups):
             last = group == len(groups) - 1
             chosen = [sources[slot] for slot in members]
-            total = mix(blocks[layer][group], chosen, total[0], gating if last else None, parts if last else 1)
+            total = mix(blocks[layer][group], chosen, total[0], gating if last else None, parts if last else ())
         return total
 
     in_first, in_last = pick(in_near, in_far), pick(in_far, in_near)
@@ -342,19 +346,24 @@
     out_peer = pick(jnp.concatenate([part, other]), jnp.concatenate([other, part]))
     out_first, out_last = pick(out_near, out_far), pick(out_far, out_near)
 
-    (gated,) = mixed(0, sources, gating, 1)
+    (gated,) = mixed(0, sources, gating, ())
     gated_peer = swap(gated, "chan")
+    gated_home = across(gated, 1, 0)
     first, signal, gating = step(gated, gated_peer, out_first, out_peer, in_last)
     sources = gathered(signal)
-    first_home = across(first, 1, 0)
-    gated, *parts = mixed(1, sources, gating, PARTS)
-
-    moved = each(lambda value: across(value, 1, 1), parts)
-    gated_peer = swap_in(gated, 0)
-    (second,) = project([gated], [gated_peer], out_last, 1)
-    second_near = lax.ppermute(second, "section", [(0, 1)])
-    moved_peer = each(lambda value: swap_in(value, 1), moved)
-    return finish(moved, moved_peer, out_last, first, first_home, second_near)
+    home_peer = swap(gated_home, "chan")
+    (first_home,) = project([gated_home], [home_peer], out_first, 1)
+    gated, upper, lower = mixed(1, sources, gating, two_parts(block, HOMING))
+
+    upper_peer = swap(upper, "chan")
+    lower_home = across(lower, 1, 1)
+    near_peer = lax.ppermute(gated, ("chan", "section"), [(0, 3), (2, 1)])
+    near_own = lax.ppermute(gated, "section", [(0, 1)])
+    (second_upper,) = project([upper], [upper_peer], out_last, 1)
+    upper_home = across(second_upper, 1, 1)
+    (second_near,) = project([near_own], [near_peer], out_last, 1)
+    lower_home_peer = swap(lower_home, "chan")
+    return finish(out_last, first, first_home, second_near, upper_home, lower_home, lower_home_peer)
 
 
 def solution(mesh):

time: 93.5 us -> 90.2 us (0.965)
  the two profiles are of different devices: /device:TPU:1 before, /device:TPU:0 now
where the time goes in v2:
time: 90.2 us; the launch traced here: 89.8 us
  starting transfers between devices  43.3 us (48%)
  waiting for transfers between devices  27.1 us (30%)
  Pallas kernels  11.7 us (13%)
  other arithmetic  5.29 us (6%)
  local copies, waits for them, and re-layouts  2.16 us (2%)
    ppermute x18, starting transfers between devices, swap(): return lax.ppermute(value, axis, [(0, 1), (1, 0)])  28.4 us
    ppermute x18, waiting for transfers between devices, swap(): return lax.ppermute(value, axis, [(0, 1), (1, 0)])  18.1 us
    ppermute x6, waiting for transfers between devices, gathered(): lax.ppermute(signal, 'seq', [(i, i ^ apart) for i in range(count)])  8.91 us
    ppermute x6, starting transfers between devices, gathered(): lax.ppermute(signal, 'seq', [(i, i ^ apart) for i in range(count)])  7.04 us
    select_n x5, other arithmetic, pick(): return jnp.where(section == 0, zero, one)  5.29 us
    pallas_call x2, Pallas kernels, toeplitz(): pl.pallas_call(functools.partial(toeplitz_kernel, block, groups, layer),...  3.83 us
    ppermute x4, starting transfers between devices, across(): return lax.ppermute(value, ('seq', 'section'), pairs)  3.28 us
    pallas_call x4, Pallas kernels, mix(): call(functools.partial(mix_kernel, len(sources), last), outs, [VMEM] * (1...  2.79 us
  transfers between devices with their start and end apart: 30, of which 8 were waited for; matrix products, arithmetic and copies ran while one was open for 6% of the time, Pallas kernels for 10%

profile of v2, /device:TPU:0, one launch (start us, length us, event | category | flops | bytes accessed | tf_op | source)
XLA Modules:
  0.0 89.8 jit_solution(10351854261036306579)
XLA Ops:
  0.0 2.1 %copy.6 = bf16[128,8,2,512]{3,1,2,0:T(8,128)(2,1)S(1)} copy(bf16[128,8,2,512]{3,2,1,0:T(2,128)(2,1)} %bitcast.14) | data formatting | bytes 4194304
  2.2 0.6 collective-permute-start.2
  2.7 0.1 collective-permute-start
  2.8 1.0 %take.1 = (bf16[256,512]{1,0:T(8,128)(2,1)S(1)}, bf16[256,512]{1,0:T(8,128)(2,1)S(1)}) custom-call(bf16[2,256,512]{2,1,0:T(8,128)(2,1)} %tokens_ref.1), custom_call_target="tpu_custom_call" | custom-call | bytes 1048576 | tf_op jit(solution)/shard_map/take/pallas_call | solution.py:119
  3.8 0.7 collective-permute-start.3
  4.6 3.0 %collective-permute-start.4 = (bf16[256,512]{1,0:T(8,128)(2,1)S(1)}, bf16[256,512]{1,0:T(8,128)(2,1)S(1)}, u32[]{:S(2)}, u32[]{:S(2)}) collective-permute-start(bf16[256,512]{1,0:T(8,128)(2,1)S(1)} %broadcast_select_fusion.4.refs_0_), channel_id=1, source_target_pairs={{0,2},{2,0},{1,3},{3,1},{4,6},{6,4},{5,7},{7,5},{8,10},{10,8},{9,1... | collective-permute-start | bytes 786440 | tf_op jit(solution)/shard_map/ppermute | solution.py:273
  7.6 0.6 collective-permute-done
  8.1 1.3 %slice_select_fusion = bf16[512,512]{1,0:T(8,128)(2,1)S(1)} fusion(bf16[1024,512]{1,0:T(8,128)(2,1)} %collective-permute-done, bf16[1,1024,512]{2,1,0:T(8,128)(2,1)} %param.8, pred[]{:T(512)S(6)} %eq.2), kind=kLoop, calls=%fused_computation.5 | loop fusion | flops 262144 | bytes 1572865 | tf_op jit(solution)/shard_map/jit(_where)/select_n | solution.py:280
  9.4 1.9 %broadcast_select_fusion = (bf16[1024,1024]{1,0:T(8,128)(2,1)S(1)}, bf16[1024,1024]{1,0:T(8,128)(2,1)S(1)}) fusion(bf16[1024,1024]{1,0:T(8,128)(2,1)} %collective-permute-done.2, bf16[1024,1024]{1,0:T(8,128)(2,1)S(1)} %bitcast.13, pred[]{:T(512)S(6)} %eq.2), kind=kLoop, calls=%fused_computation | loop fusion | flops 2097152 | bytes 8388609 | tf_op jit(solution)/shard_map/jit(_where)/select_n | solution.py:280
  11.3 0.0 copy-start
  11.3 0.0 copy-start.1
  11.3 0.6 collective-permute-done.4.refs_1_
  11.9 0.7 shard_map.55
  12.6 2.3 %collective-permute-start.13 = (bf16[512,512]{1,0:T(8,128)(2,1)S(1)}, bf16[512,512]{1,0:T(8,128)(2,1)S(1)}, u32[]{:S(2)}, u32[]{:S(2)}) collective-permute-start(bf16[512,512]{1,0:T(8,128)(2,1)S(1)} %slice_select_fusion), channel_id=1, source_target_pairs={{0,2},{2,0},{1,3},{3,1},{4,6},{6,4},{5,7},{7,5},{8,10},{10,8},{9,1... | collective-permute-start | bytes 1572872 | tf_op jit(solution)/shard_map/ppermute | solution.py:273
  14.9 1.6 %collective-permute-start.10 = (bf16[256,512]{1,0:T(8,128)(2,1)S(1)}, bf16[256,512]{1,0:T(8,128)(2,1)S(1)}, u32[]{:S(2)}, u32[]{:S(2)}) collective-permute-start(bf16[256,512]{1,0:T(8,128)(2,1)S(1)} %get-tuple-element.23.refs_0_), channel_id=1, source_target_pairs={{0,8},{4,12},{8,0},{12,4},{16,24},{20,28},{24,16},{28,20},{1,9},{5... | collective-permute-start | bytes 786440 | tf_op jit(solution)/shard_map/ppermute | solution.py:327
  16.5 1.5 %collective-permute-start.8 = (bf16[256,512]{1,0:T(8,128)(2,1)S(1)}, bf16[256,512]{1,0:T(8,128)(2,1)S(1)}, u32[]{:S(2)}, u32[]{:S(2)}) collective-permute-start(bf16[256,512]{1,0:T(8,128)(2,1)S(1)} %get-tuple-element.23.refs_0_), channel_id=1, source_target_pairs={{0,4},{4,0},{8,12},{12,8},{16,20},{20,16},{24,28},{28,24},{1,5},{5... | collective-permute-start | bytes 786440 | tf_op jit(solution)/shard_map/ppermute | solution.py:327
  18.0 0.4 collective-permute-start.5
  18.4 10.8 %collective-permute-start.1 = (bf16[4,2304]{1,0:T(4,128)(2,1)S(1)}, bf16[4,2304]{1,0:T(4,128)(2,1)S(1)}, u32[]{:S(2)}, u32[]{:S(2)}) collective-permute-start(bf16[4,2304]{1,0:T(4,128)(2,1)S(1)} %bitcast.9), channel_id=1, source_target_pairs={{0,1},{1,0},{2,3},{3,2},{4,5},{5,4},{6,7},{7,6},{8,9},{9,8},{10,11... | collective-permute-start | bytes 55304 | tf_op jit(solution)/shard_map/ppermute | solution.py:273
  29.2 0.8 collective-permute-done.1.far_ref
  30.1 0.3 collective-permute-start.7
  30.4 0.0 collective-permute-done.10.refs_4_
  30.4 1.4 %collective-permute-start.11 = (bf16[256,512]{1,0:T(8,128)(2,1)S(1)}, bf16[256,512]{1,0:T(8,128)(2,1)S(1)}, u32[]{:S(2)}, u32[]{:S(2)}) collective-permute-start(bf16[256,512]{1,0:T(8,128)(2,1)S(1)} %collective-permute-done.10.refs_4_), channel_id=1, source_target_pairs={{0,1},{1,0},{2,3},{3,2},{4,5},{5,4},{6,7},{7,6},{8,9},{9,8},{10,11... | collective-permute-start | bytes 786440 | tf_op jit(solution)/shard_map/ppermute | solution.py:273
  31.8 0.0 collective-permute-done.8.refs_2_
  31.8 2.8 %collective-permute-start.9 = (bf16[256,512]{1,0:T(8,128)(2,1)S(1)}, bf16[256,512]{1,0:T(8,128)(2,1)S(1)}, u32[]{:S(2)}, u32[]{:S(2)}) collective-permute-start(bf16[256,512]{1,0:T(8,128)(2,1)S(1)} %collective-permute-done.8.refs_2_), channel_id=1, source_target_pairs={{0,1},{1,0},{2,3},{3,2},{4,5},{5,4},{6,7},{7,6},{8,9},{9,8},{10,11... | collective-permute-start | bytes 786440 | tf_op jit(solution)/shard_map/ppermute | solution.py:273
  34.6 0.0 collective-permute-done.5.refs_0_
  34.6 0.9 %collective-permute-start.6 = (bf16[256,512]{1,0:T(8,128)(2,1)S(1)}, bf16[256,512]{1,0:T(8,128)(2,1)S(1)}, u32[]{:S(2)}, u32[]{:S(2)}) collective-permute-start(bf16[256,512]{1,0:T(8,128)(2,1)S(1)} %collective-permute-done.5.refs_0_), channel_id=1, source_target_pairs={{0,1},{1,0},{2,3},{3,2},{4,5},{5,4},{6,7},{7,6},{8,9},{9,8},{10,11... | collective-permute-start | bytes 786440 | tf_op jit(solution)/shard_map/ppermute | solution.py:273
  35.6 0.0 collective-permute-done.13
  35.6 0.0 collective-permute-start.14
  35.6 1.9 %toeplitz.2 = (bf16[4,256,1536]{2,1,0:T(8,128)(2,1)S(1)}, bf16[4,256,512]{2,1,0:T(8,128)(2,1)S(1)}) custom-call(s32[2]{0:T(128)S(1)} %copy-done.1, bf16[4,2304]{1,0:T(4,128)(2,1)S(1)} %bitcast.10, bf16[4,2304]{1,0:T(4,128)(2,1)S(1)} %collective-permute-done.1.far_ref), custom_call_target="tpu_custom_call" | custom-call | flops 83886080 | bytes 4194304 | tf_op jit(solution)/shard_map/toeplitz/pallas_call | solution.py:86
  37.5 0.0 collective-permute-done.7.refs_1_
  37.5 1.0 %shard_map.56.refs_3_ = f32[256,512]{1,0:T(8,128)S(1)} custom-call(bf16[4,256,1536]{2,1,0:T(8,128)(2,1)S(1)} %get-tuple-element.25.toeplitz_ref, bf16[256,512]{1,0:T(8,128)(2,1)S(1)} %get-tuple-element.23.refs_0_, bf16[256,512]{1,0:T(8,128)(2,1)S(1)} %collective-permute-done.7.refs_1_, bf16[256,512]{1,0:T(8,128)(2,1)S(1)} %collective-permute-done.8.refs_2_, ...), custom_call_target="tpu_custom_call" | custom-call | flops 402653184 | bytes 5767168 | tf_op jit(solution)/shard_map/pallas_call | solution.py:160
  38.5 0.4 shard_map.57.own_ref
  38.9 0.6 collective-permute-start.12
  39.5 1.7 %broadcast_select_fusion.2 = (bf16[1024,512]{1,0:T(8,128)(2,1)S(1)}, bf16[1024,512]{1,0:T(8,128)(2,1)S(1)}) fusion(bf16[1024,512]{1,0:T(8,128)(2,1)} %collective-permute-done, pred[]{:T(512)S(6)} %eq.2, bf16[1,1024,512]{2,1,0:T(8,128)(2,1)} %param.8), kind=kLoop, calls=%fused_computation.3 | loop fusion | flops 1048576 | bytes 4194305 | tf_op jit(solution)/shard_map/jit(_where)/select_n | solution.py:280
  41.2 0.5 maximum_select_fusion.out_peer_ref
  41.7 6.0 %collective-permute-done.12.peer_ref = bf16[256,512]{1,0:T(8,128)(2,1)S(1)} collective-permute-done((bf16[256,512]{1,0:T(8,128)(2,1)S(1)}, bf16[256,512]{1,0:T(8,128)(2,1)S(1)}, u32[]{:S(2)}, u32[]{:S(2)}) %collective-permute-start.12) | collective-permute-done | bytes 262176 | tf_op jit(solution)/shard_map/ppermute | solution.py:273
  47.7 1.4 %step.1 = (bf16[256,512]{1,0:T(8,128)(2,1)S(1)}, bf16[256,512]{1,0:T(8,128)(2,1)S(1)}, bf16[256,512]{1,0:T(8,128)(2,1)S(1)}) custom-call(bf16[256,512]{1,0:T(8,128)(2,1)S(1)} %shard_map.57.own_ref, bf16[256,512]{1,0:T(8,128)(2,1)S(1)} %collective-permute-done.12.peer_ref, bf16[1024,512]{1,0:T(8,128)(2,1)S(1)} %get-tuple-element.37.out_own_ref.weight_ref, ...), custom_call_target="tpu_custom_call" | custom-call | flops 1073741824 | bytes 5505024 | tf_op jit(solution)/shard_map/step/pallas_call | solution.py:222
  49.1 1.4 %collective-permute-start.20 = (bf16[256,512]{1,0:T(8,128)(2,1)S(1)}, bf16[256,512]{1,0:T(8,128)(2,1)S(1)}, u32[]{:S(2)}, u32[]{:S(2)}) collective-permute-start(bf16[256,512]{1,0:T(8,128)(2,1)S(1)} %get-tuple-element.29.refs_0_), channel_id=1, source_target_pairs={{0,4},{4,0},{8,12},{12,8},{16,20},{20,16},{24,28},{28,24},{1,5},{5... | collective-permute-start | bytes 786440 | tf_op jit(solution)/shard_map/ppermute | solution.py:327
  50.5 1.1 %collective-permute-start.22 = (bf16[256,512]{1,0:T(8,128)(2,1)S(1)}, bf16[256,512]{1,0:T(8,128)(2,1)S(1)}, u32[]{:S(2)}, u32[]{:S(2)}) collective-permute-start(bf16[256,512]{1,0:T(8,128)(2,1)S(1)} %get-tuple-element.29.refs_0_), channel_id=1, source_target_pairs={{0,8},{4,12},{8,0},{12,4},{16,24},{20,28},{24,16},{28,20},{1,9},{5... | collective-permute-start | bytes 786440 | tf_op jit(solution)/shard_map/ppermute | solution.py:327
  51.6 1.1 %collective-permute-start.17 = (bf16[256,512]{1,0:T(8,128)(2,1)S(1)}, bf16[256,512]{1,0:T(8,128)(2,1)S(1)}, u32[]{:S(2)}, u32[]{:S(2)}) collective-permute-start(bf16[256,512]{1,0:T(8,128)(2,1)S(1)} %get-tuple-element.29.refs_0_), channel_id=1, source_target_pairs={{0,12},{4,8},{8,4},{12,0},{16,28},{20,24},{24,20},{28,16},{1,13},{... | collective-permute-start | bytes 786440 | tf_op jit(solution)/shard_map/ppermute | solution.py:327
  52.7 1.3 %collective-permute-start.15 = (bf16[256,512]{1,0:T(8,128)(2,1)S(1)}, bf16[256,512]{1,0:T(8,128)(2,1)S(1)}, u32[]{:S(2)}, u32[]{:S(2)}) collective-permute-start(bf16[256,512]{1,0:T(8,128)(2,1)S(1)} %shard_map.57.own_ref), channel_id=1, source_target_pairs={{1,16},{5,20},{9,24},{13,28},{17,0},{21,4},{25,8},{29,12},{3,18},{... | collective-permute-start | bytes 786440 | tf_op jit(solution)/shard_map/ppermute | solution.py:277
  53.9 3.7 %collective-permute-start.19 = (bf16[256,512]{1,0:T(8,128)(2,1)S(1)}, bf16[256,512]{1,0:T(8,128)(2,1)S(1)}, u32[]{:S(2)}, u32[]{:S(2)}) collective-permute-start(bf16[256,512]{1,0:T(8,128)(2,1)S(1)} %get-tuple-element.29.refs_0_), channel_id=1, source_target_pairs={{0,1},{1,0},{2,3},{3,2},{4,5},{5,4},{6,7},{7,6},{8,9},{9,8},{10,11... | collective-permute-start | bytes 786440 | tf_op jit(solution)/shard_map/ppermute | solution.py:273
  57.7 0.1 collective-permute-start.21
  57.7 4.7 %collective-permute-done.22.refs_4_ = bf16[256,512]{1,0:T(8,128)(2,1)S(1)} collective-permute-done((bf16[256,512]{1,0:T(8,128)(2,1)S(1)}, bf16[256,512]{1,0:T(8,128)(2,1)S(1)}, u32[]{:S(2)}, u32[]{:S(2)}) %collective-permute-start.22) | collective-permute-done | bytes 262176 | tf_op jit(solution)/shard_map/ppermute | solution.py:327
  62.5 4.1 %collective-permute-done.17.refs_0_ = bf16[256,512]{1,0:T(8,128)(2,1)S(1)} collective-permute-done((bf16[256,512]{1,0:T(8,128)(2,1)S(1)}, bf16[256,512]{1,0:T(8,128)(2,1)S(1)}, u32[]{:S(2)}, u32[]{:S(2)}) %collective-permute-start.17) | collective-permute-done | bytes 262176 | tf_op jit(solution)/shard_map/ppermute | solution.py:327
  66.6 0.0 collective-permute-start.18
  66.6 1.9 %toeplitz.3 = (bf16[4,256,1536]{2,1,0:T(8,128)(2,1)S(1)}, bf16[4,256,512]{2,1,0:T(8,128)(2,1)S(1)}) custom-call(s32[2]{0:T(128)S(1)} %copy-done.1, bf16[4,2304]{1,0:T(4,128)(2,1)S(1)} %bitcast.11, bf16[4,2304]{1,0:T(4,128)(2,1)S(1)} %collective-permute-done.1.far_ref), custom_call_target="tpu_custom_call" | custom-call | flops 83886080 | bytes 4194304 | tf_op jit(solution)/shard_map/toeplitz/pallas_call | solution.py:86
  68.6 0.0 collective-permute-done.15.refs_0_
  68.6 0.6 collective-permute-start.16
  69.2 0.0 collective-permute-done.19.refs_1_
  69.2 1.0 %shard_map.59.refs_3_ = f32[256,512]{1,0:T(8,128)S(1)} custom-call(bf16[4,256,1536]{2,1,0:T(8,128)(2,1)S(1)} %get-tuple-element.31.toeplitz_ref, bf16[256,512]{1,0:T(8,128)(2,1)S(1)} %get-tuple-element.29.refs_0_, bf16[256,512]{1,0:T(8,128)(2,1)S(1)} %collective-permute-done.19.refs_1_, bf16[256,512]{1,0:T(8,128)(2,1)S(1)} %collective-permute-done.20.refs_2_, ...), custom_call_target="tpu_custom_call" | custom-call | flops 402653184 | bytes 5767168 | tf_op jit(solution)/shard_map/pallas_call | solution.py:160
  70.2 0.4 shard_map.60
  70.6 2.1 %collective-permute-start.24 = (bf16[256,512]{1,0:T(8,128)(2,1)S(1)}, bf16[256,512]{1,0:T(8,128)(2,1)S(1)}, u32[]{:S(2)}, u32[]{:S(2)}) collective-permute-start(bf16[256,512]{1,0:T(8,128)(2,1)S(1)} %get-tuple-element.32), channel_id=1, source_target_pairs={{0,1},{2,3},{4,5},{6,7},{8,9},{10,11},{12,13},{14,15},{16,17},{18,... | collective-permute-start | bytes 786440 | tf_op jit(solution)/shard_map/ppermute | solution.py:361
  72.8 2.4 %collective-permute-start.25 = (bf16[256,512]{1,0:T(8,128)(2,1)S(1)}, bf16[256,512]{1,0:T(8,128)(2,1)S(1)}, u32[]{:S(2)}, u32[]{:S(2)}) collective-permute-start(bf16[256,512]{1,0:T(8,128)(2,1)S(1)} %get-tuple-element.32), channel_id=1, source_target_pairs={{0,3},{2,1},{4,7},{6,5},{8,11},{10,9},{12,15},{14,13},{16,19},{18,... | collective-permute-start | bytes 786440 | tf_op jit(solution)/shard_map/ppermute | solution.py:360
  75.2 0.6 collective-permute-start.26
  75.8 0.7 collective-permute-start.28
  76.4 6.6 %collective-permute-done.26.refs_1_ = bf16[128,512]{1,0:T(8,128)(2,1)S(1)} collective-permute-done((bf16[128,512]{1,0:T(8,128)(2,1)S(1)}, bf16[128,512]{1,0:T(8,128)(2,1)S(1)}, u32[]{:S(2)}, u32[]{:S(2)}) %collective-permute-start.26) | collective-permute-done | bytes 131104 | tf_op jit(solution)/shard_map/ppermute | solution.py:273
  83.0 0.3 shard_map.62
  83.3 0.7 collective-permute-start.27
  84.0 0.6 collective-permute-start.29
  84.6 0.4 shard_map.58.first_home_ref
  85.0 0.4 shard_map.61.near_ref
  85.5 3.5 %collective-permute-done.29.peer_ref = bf16[128,512]{1,0:T(8,128)(2,1)S(1)} collective-permute-done((bf16[128,512]{1,0:T(8,128)(2,1)S(1)}, bf16[128,512]{1,0:T(8,128)(2,1)S(1)}, u32[]{:S(2)}, u32[]{:S(2)}) %collective-permute-start.29) | collective-permute-done | bytes 131104 | tf_op jit(solution)/shard_map/ppermute | solution.py:273
  89.0 0.8 shard_map.63
  (19 shorter events, 0.1 us)
Async XLA Ops:
  2.2 7.2 %collective-permute-start.2 = (bf16[1024,1024]{1,0:T(8,128)(2,1)S(1)}, bf16[1024,1024]{1,0:T(8,128)(2,1)}, u32[]{:S(2)}, u32[]{:S(2)}) collective-permute-start(bf16[1024,1024]{1,0:T(8,128)(2,1)S(1)} %bitcast.12), channel_id=1, source_target_pairs={{0,1},{1,0},{2,3},{3,2},{4,5},{5,4},{6,7},{7,6},{8,9},{9,8},{10,11... | collective-permute-start | bytes 6291464 | tf_op jit(solution)/shard_map/ppermute | solution.py:273
  2.7 5.4 %collective-permute-start = (bf16[1024,512]{1,0:T(8,128)(2,1)}, bf16[1024,512]{1,0:T(8,128)(2,1)}, u32[]{:S(2)}, u32[]{:S(2)}) collective-permute-start(bf16[1024,512]{1,0:T(8,128)(2,1)} %bitcast), channel_id=1, source_target_pairs={{0,1},{1,0},{2,3},{3,2},{4,5},{5,4},{6,7},{7,6},{8,9},{9,8},{10,11... | collective-permute-start | bytes 3145736 | tf_op jit(solution)/shard_map/ppermute | solution.py:273
  3.8 0.7 collective-permute-start.3
  4.6 7.3 %collective-permute-start.4 = (bf16[256,512]{1,0:T(8,128)(2,1)S(1)}, bf16[256,512]{1,0:T(8,128)(2,1)S(1)}, u32[]{:S(2)}, u32[]{:S(2)}) collective-permute-start(bf16[256,512]{1,0:T(8,128)(2,1)S(1)} %broadcast_select_fusion.4.refs_0_), channel_id=1, source_target_pairs={{0,2},{2,0},{1,3},{3,1},{4,6},{6,4},{5,7},{7,5},{8,10},{10,8},{9,1... | collective-permute-start | bytes 786440 | tf_op jit(solution)/shard_map/ppermute | solution.py:273
  11.3 7.2 %copy-start = (bf16[1,4,2304]{2,1,0:T(4,128)(2,1)S(1)}, bf16[1,4,2304]{2,1,0:T(4,128)(2,1)}, u32[]{:S(2)}) copy-start(bf16[1,4,2304]{2,1,0:T(4,128)(2,1)} %param.7) | copy-start | bytes 55300
  11.3 24.3 %copy-start.1 = (s32[2]{0:T(128)S(1)}, s32[2]{0:T(128)}, u32[]{:S(2)}) copy-start(s32[2]{0:T(128)} %widths_ref.3) | copy-start | bytes 28
  12.6 22.9 %collective-permute-start.13 = (bf16[512,512]{1,0:T(8,128)(2,1)S(1)}, bf16[512,512]{1,0:T(8,128)(2,1)S(1)}, u32[]{:S(2)}, u32[]{:S(2)}) collective-permute-start(bf16[512,512]{1,0:T(8,128)(2,1)S(1)} %slice_select_fusion), channel_id=1, source_target_pairs={{0,2},{2,0},{1,3},{3,1},{4,6},{6,4},{5,7},{7,5},{8,10},{10,8},{9,1... | collective-permute-start | bytes 1572872 | tf_op jit(solution)/shard_map/ppermute | solution.py:273
  14.9 15.5 %collective-permute-start.10 = (bf16[256,512]{1,0:T(8,128)(2,1)S(1)}, bf16[256,512]{1,0:T(8,128)(2,1)S(1)}, u32[]{:S(2)}, u32[]{:S(2)}) collective-permute-start(bf16[256,512]{1,0:T(8,128)(2,1)S(1)} %get-tuple-element.23.refs_0_), channel_id=1, source_target_pairs={{0,8},{4,12},{8,0},{12,4},{16,24},{20,28},{24,16},{28,20},{1,9},{5... | collective-permute-start | bytes 786440 | tf_op jit(solution)/shard_map/ppermute | solution.py:327
  16.5 15.3 %collective-permute-start.8 = (bf16[256,512]{1,0:T(8,128)(2,1)S(1)}, bf16[256,512]{1,0:T(8,128)(2,1)S(1)}, u32[]{:S(2)}, u32[]{:S(2)}) collective-permute-start(bf16[256,512]{1,0:T(8,128)(2,1)S(1)} %get-tuple-element.23.refs_0_), channel_id=1, source_target_pairs={{0,4},{4,0},{8,12},{12,8},{16,20},{20,16},{24,28},{28,24},{1,5},{5... | collective-permute-start | bytes 786440 | tf_op jit(solution)/shard_map/ppermute | solution.py:327
  18.0 16.6 %collective-permute-start.5 = (bf16[256,512]{1,0:T(8,128)(2,1)S(1)}, bf16[256,512]{1,0:T(8,128)(2,1)S(1)}, u32[]{:S(2)}, u32[]{:S(2)}) collective-permute-start(bf16[256,512]{1,0:T(8,128)(2,1)S(1)} %get-tuple-element.23.refs_0_), channel_id=1, source_target_pairs={{0,12},{4,8},{8,4},{12,0},{16,28},{20,24},{24,20},{28,16},{1,13},{... | collective-permute-start | bytes 786440 | tf_op jit(solution)/shard_map/ppermute | solution.py:327
  18.4 11.6 %collective-permute-start.1 = (bf16[4,2304]{1,0:T(4,128)(2,1)S(1)}, bf16[4,2304]{1,0:T(4,128)(2,1)S(1)}, u32[]{:S(2)}, u32[]{:S(2)}) collective-permute-start(bf16[4,2304]{1,0:T(4,128)(2,1)S(1)} %bitcast.9), channel_id=1, source_target_pairs={{0,1},{1,0},{2,3},{3,2},{4,5},{5,4},{6,7},{7,6},{8,9},{9,8},{10,11... | collective-permute-start | bytes 55304 | tf_op jit(solution)/shard_map/ppermute | solution.py:273
  30.1 7.4 %collective-permute-start.7 = (bf16[256,512]{1,0:T(8,128)(2,1)S(1)}, bf16[256,512]{1,0:T(8,128)(2,1)S(1)}, u32[]{:S(2)}, u32[]{:S(2)}) collective-permute-start(bf16[256,512]{1,0:T(8,128)(2,1)S(1)} %get-tuple-element.23.refs_0_), channel_id=1, source_target_pairs={{0,1},{1,0},{2,3},{3,2},{4,5},{5,4},{6,7},{7,6},{8,9},{9,8},{10,11... | collective-permute-start | bytes 786440 | tf_op jit(solution)/shard_map/ppermute | solution.py:273
  30.4 7.1 %collective-permute-start.11 = (bf16[256,512]{1,0:T(8,128)(2,1)S(1)}, bf16[256,512]{1,0:T(8,128)(2,1)S(1)}, u32[]{:S(2)}, u32[]{:S(2)}) collective-permute-start(bf16[256,512]{1,0:T(8,128)(2,1)S(1)} %collective-permute-done.10.refs_4_), channel_id=1, source_target_pairs={{0,1},{1,0},{2,3},{3,2},{4,5},{5,4},{6,7},{7,6},{8,9},{9,8},{10,11... | collective-permute-start | bytes 786440 | tf_op jit(solution)/shard_map/ppermute | solution.py:273
  31.8 5.7 %collective-permute-start.9 = (bf16[256,512]{1,0:T(8,128)(2,1)S(1)}, bf16[256,512]{1,0:T(8,128)(2,1)S(1)}, u32[]{:S(2)}, u32[]{:S(2)}) collective-permute-start(bf16[256,512]{1,0:T(8,128)(2,1)S(1)} %collective-permute-done.8.refs_2_), channel_id=1, source_target_pairs={{0,1},{1,0},{2,3},{3,2},{4,5},{5,4},{6,7},{7,6},{8,9},{9,8},{10,11... | collective-permute-start | bytes 786440 | tf_op jit(solution)/shard_map/ppermute | solution.py:273
  34.6 3.9 %collective-permute-start.6 = (bf16[256,512]{1,0:T(8,128)(2,1)S(1)}, bf16[256,512]{1,0:T(8,128)(2,1)S(1)}, u32[]{:S(2)}, u32[]{:S(2)}) collective-permute-start(bf16[256,512]{1,0:T(8,128)(2,1)S(1)} %collective-permute-done.5.refs_0_), channel_id=1, source_target_pairs={{0,1},{1,0},{2,3},{3,2},{4,5},{5,4},{6,7},{7,6},{8,9},{9,8},{10,11... | collective-permute-start | bytes 786440 | tf_op jit(solution)/shard_map/ppermute | solution.py:273
  35.6 5.7 %collective-permute-start.14 = (bf16[512,512]{1,0:T(8,128)(2,1)S(1)}, bf16[512,512]{1,0:T(8,128)(2,1)S(1)}, u32[]{:S(2)}, u32[]{:S(2)}) collective-permute-start(bf16[512,512]{1,0:T(8,128)(2,1)S(1)} %collective-permute-done.13), channel_id=1, source_target_pairs={{0,1},{1,0},{2,3},{3,2},{4,5},{5,4},{6,7},{7,6},{8,9},{9,8},{10,11... | collective-permute-start | bytes 1572872 | tf_op jit(solution)/shard_map/ppermute | solution.py:273
  38.9 8.8 %collective-permute-start.12 = (bf16[256,512]{1,0:T(8,128)(2,1)S(1)}, bf16[256,512]{1,0:T(8,128)(2,1)S(1)}, u32[]{:S(2)}, u32[]{:S(2)}) collective-permute-start(bf16[256,512]{1,0:T(8,128)(2,1)S(1)} %shard_map.57.own_ref), channel_id=1, source_target_pairs={{0,2},{2,0},{1,3},{3,1},{4,6},{6,4},{5,7},{7,5},{8,10},{10,8},{9,1... | collective-permute-start | bytes 786440 | tf_op jit(solution)/shard_map/ppermute | solution.py:273
  49.1 8.6 %collective-permute-start.20 = (bf16[256,512]{1,0:T(8,128)(2,1)S(1)}, bf16[256,512]{1,0:T(8,128)(2,1)S(1)}, u32[]{:S(2)}, u32[]{:S(2)}) collective-permute-start(bf16[256,512]{1,0:T(8,128)(2,1)S(1)} %get-tuple-element.29.refs_0_), channel_id=1, source_target_pairs={{0,4},{4,0},{8,12},{12,8},{16,20},{20,16},{24,28},{28,24},{1,5},{5... | collective-permute-start | bytes 786440 | tf_op jit(solution)/shard_map/ppermute | solution.py:327
  50.5 12.0 %collective-permute-start.22 = (bf16[256,512]{1,0:T(8,128)(2,1)S(1)}, bf16[256,512]{1,0:T(8,128)(2,1)S(1)}, u32[]{:S(2)}, u32[]{:S(2)}) collective-permute-start(bf16[256,512]{1,0:T(8,128)(2,1)S(1)} %get-tuple-element.29.refs_0_), channel_id=1, source_target_pairs={{0,8},{4,12},{8,0},{12,4},{16,24},{20,28},{24,16},{28,20},{1,9},{5... | collective-permute-start | bytes 786440 | tf_op jit(solution)/shard_map/ppermute | solution.py:327
  51.6 15.1 %collective-permute-start.17 = (bf16[256,512]{1,0:T(8,128)(2,1)S(1)}, bf16[256,512]{1,0:T(8,128)(2,1)S(1)}, u32[]{:S(2)}, u32[]{:S(2)}) collective-permute-start(bf16[256,512]{1,0:T(8,128)(2,1)S(1)} %get-tuple-element.29.refs_0_), channel_id=1, source_target_pairs={{0,12},{4,8},{8,4},{12,0},{16,28},{20,24},{24,20},{28,16},{1,13},{... | collective-permute-start | bytes 786440 | tf_op jit(solution)/shard_map/ppermute | solution.py:327
  52.7 15.9 %collective-permute-start.15 = (bf16[256,512]{1,0:T(8,128)(2,1)S(1)}, bf16[256,512]{1,0:T(8,128)(2,1)S(1)}, u32[]{:S(2)}, u32[]{:S(2)}) collective-permute-start(bf16[256,512]{1,0:T(8,128)(2,1)S(1)} %shard_map.57.own_ref), channel_id=1, source_target_pairs={{1,16},{5,20},{9,24},{13,28},{17,0},{21,4},{25,8},{29,12},{3,18},{... | collective-permute-start | bytes 786440 | tf_op jit(solution)/shard_map/ppermute | solution.py:277
  53.9 15.2 %collective-permute-start.19 = (bf16[256,512]{1,0:T(8,128)(2,1)S(1)}, bf16[256,512]{1,0:T(8,128)(2,1)S(1)}, u32[]{:S(2)}, u32[]{:S(2)}) collective-permute-start(bf16[256,512]{1,0:T(8,128)(2,1)S(1)} %get-tuple-element.29.refs_0_), channel_id=1, source_target_pairs={{0,1},{1,0},{2,3},{3,2},{4,5},{5,4},{6,7},{7,6},{8,9},{9,8},{10,11... | collective-permute-start | bytes 786440 | tf_op jit(solution)/shard_map/ppermute | solution.py:273
  57.7 11.5 %collective-permute-start.21 = (bf16[256,512]{1,0:T(8,128)(2,1)S(1)}, bf16[256,512]{1,0:T(8,128)(2,1)S(1)}, u32[]{:S(2)}, u32[]{:S(2)}) collective-permute-start(bf16[256,512]{1,0:T(8,128)(2,1)S(1)} %collective-permute-done.20.refs_2_), channel_id=1, source_target_pairs={{0,1},{1,0},{2,3},{3,2},{4,5},{5,4},{6,7},{7,6},{8,9},{9,8},{10,11... | collective-permute-start | bytes 786440 | tf_op jit(solution)/shard_map/ppermute | solution.py:273
  62.5 6.7 %collective-permute-start.23 = (bf16[256,512]{1,0:T(8,128)(2,1)S(1)}, bf16[256,512]{1,0:T(8,128)(2,1)S(1)}, u32[]{:S(2)}, u32[]{:S(2)}) collective-permute-start(bf16[256,512]{1,0:T(8,128)(2,1)S(1)} %collective-permute-done.22.refs_4_), channel_id=1, source_target_pairs={{0,1},{1,0},{2,3},{3,2},{4,5},{5,4},{6,7},{7,6},{8,9},{9,8},{10,11... | collective-permute-start | bytes 786440 | tf_op jit(solution)/shard_map/ppermute | solution.py:273
  66.6 3.5 %collective-permute-start.18 = (bf16[256,512]{1,0:T(8,128)(2,1)S(1)}, bf16[256,512]{1,0:T(8,128)(2,1)S(1)}, u32[]{:S(2)}, u32[]{:S(2)}) collective-permute-start(bf16[256,512]{1,0:T(8,128)(2,1)S(1)} %collective-permute-done.17.refs_0_), channel_id=1, source_target_pairs={{0,1},{1,0},{2,3},{3,2},{4,5},{5,4},{6,7},{7,6},{8,9},{9,8},{10,11... | collective-permute-start | bytes 786440 | tf_op jit(solution)/shard_map/ppermute | solution.py:273
  68.6 16.0 %collective-permute-start.16 = (bf16[256,512]{1,0:T(8,128)(2,1)S(1)}, bf16[256,512]{1,0:T(8,128)(2,1)S(1)}, u32[]{:S(2)}, u32[]{:S(2)}) collective-permute-start(bf16[256,512]{1,0:T(8,128)(2,1)S(1)} %collective-permute-done.15.refs_0_), channel_id=1, source_target_pairs={{0,2},{2,0},{1,3},{3,1},{4,6},{6,4},{5,7},{7,5},{8,10},{10,8},{9,1... | collective-permute-start | bytes 786440 | tf_op jit(solution)/shard_map/ppermute | solution.py:273
  70.6 14.4 %collective-permute-start.24 = (bf16[256,512]{1,0:T(8,128)(2,1)S(1)}, bf16[256,512]{1,0:T(8,128)(2,1)S(1)}, u32[]{:S(2)}, u32[]{:S(2)}) collective-permute-start(bf16[256,512]{1,0:T(8,128)(2,1)S(1)} %get-tuple-element.32), channel_id=1, source_target_pairs={{0,1},{2,3},{4,5},{6,7},{8,9},{10,11},{12,13},{14,15},{16,17},{18,... | collective-permute-start | bytes 786440 | tf_op jit(solution)/shard_map/ppermute | solution.py:361
  72.8 12.3 %collective-permute-start.25 = (bf16[256,512]{1,0:T(8,128)(2,1)S(1)}, bf16[256,512]{1,0:T(8,128)(2,1)S(1)}, u32[]{:S(2)}, u32[]{:S(2)}) collective-permute-start(bf16[256,512]{1,0:T(8,128)(2,1)S(1)} %get-tuple-element.32), channel_id=1, source_target_pairs={{0,3},{2,1},{4,7},{6,5},{8,11},{10,9},{12,15},{14,13},{16,19},{18,... | collective-permute-start | bytes 786440 | tf_op jit(solution)/shard_map/ppermute | solution.py:360
  75.2 7.8 %collective-permute-start.26 = (bf16[128,512]{1,0:T(8,128)(2,1)S(1)}, bf16[128,512]{1,0:T(8,128)(2,1)S(1)}, u32[]{:S(2)}, u32[]{:S(2)}) collective-permute-start(bf16[128,512]{1,0:T(8,128)(2,1)S(1)} %get-tuple-element.33.refs_0_), channel_id=1, source_target_pairs={{0,2},{2,0},{1,3},{3,1},{4,6},{6,4},{5,7},{7,5},{8,10},{10,8},{9,1... | collective-permute-start | bytes 393224 | tf_op jit(solution)/shard_map/ppermute | solution.py:273
  75.8 8.2 %collective-permute-start.28 = (bf16[128,512]{1,0:T(8,128)(2,1)S(1)}, bf16[128,512]{1,0:T(8,128)(2,1)S(1)}, u32[]{:S(2)}, u32[]{:S(2)}) collective-permute-start(bf16[128,512]{1,0:T(8,128)(2,1)S(1)} %get-tuple-element.34), channel_id=1, source_target_pairs={{1,17},{5,21},{9,25},{13,29},{17,1},{21,5},{25,9},{29,13},{3,19},{... | collective-permute-start | bytes 393224 | tf_op jit(solution)/shard_map/ppermute | solution.py:277
  83.3 2.2 %collective-permute-start.27 = (bf16[128,512]{1,0:T(8,128)(2,1)S(1)}, bf16[128,512]{1,0:T(8,128)(2,1)S(1)}, u32[]{:S(2)}, u32[]{:S(2)}) collective-permute-start(bf16[128,512]{1,0:T(8,128)(2,1)S(1)} %shard_map.62), channel_id=1, source_target_pairs={{1,17},{5,21},{9,25},{13,29},{17,1},{21,5},{25,9},{29,13},{3,19},{... | collective-permute-start | bytes 393224 | tf_op jit(solution)/shard_map/ppermute | solution.py:277
  84.0 5.0 %collective-permute-start.29 = (bf16[128,512]{1,0:T(8,128)(2,1)S(1)}, bf16[128,512]{1,0:T(8,128)(2,1)S(1)}, u32[]{:S(2)}, u32[]{:S(2)}) collective-permute-start(bf16[128,512]{1,0:T(8,128)(2,1)S(1)} %collective-permute-done.28.own_ref), channel_id=1, source_target_pairs={{0,2},{2,0},{1,3},{3,1},{4,6},{6,4},{5,7},{7,5},{8,10},{10,8},{9,1... | collective-permute-start | bytes 393224 | tf_op jit(solution)/shard_map/ppermute | solution.py:273

commit v3 on v2

--- a/solution.py
+++ b/solution.py
@@ -233,32 +233,57 @@
     )(own, peer, out_own, out_peer, in_weight)
 
 
-def finish_kernel(weight_ref, first_ref, first_home_ref, near_ref, home_ref, own_ref, peer_ref, out_ref):
+def finish_kernel(weight_ref, first_ref, first_home_ref, near_ref, home_ref, own_ref, peer_ref, out_ref, lower_ref, sems):
     section = lax.axis_index("section")
     sequence, _ = position()
     rows = home_ref.shape[0]
+    block = near_ref.shape[0]
+
+    def run(copies):
+        for copy in copies:
+            copy.start()
+        return copies
 
     @pl.when(section == 0)
     def _():
-        out_ref[0, sequence] = first_ref[...]
-        out_ref[0, 1 - sequence] = first_home_ref[...]
+        copies = run(
+            [
+                pltpu.make_async_copy(first_ref, out_ref.at[0, sequence], sems.at[0]),
+                pltpu.make_async_copy(first_home_ref, out_ref.at[0, 1 - sequence], sems.at[1]),
+            ]
+        )
+        for copy in copies:
+            copy.wait()
 
     @pl.when(section == 1)
     def _():
-        out_ref[0, 1 - sequence, :rows] = home_ref[...]
-        out_ref[0, 1 - sequence, rows:] = product([own_ref], [peer_ref], weight_ref).astype(jnp.bfloat16)
-        out_ref[0, sequence] = near_ref[...]
+        copies = run(
+            [
+                pltpu.make_async_copy(near_ref, out_ref.at[0, sequence], sems.at[0]),
+                pltpu.make_async_copy(home_ref, out_ref.at[0, 1 - sequence, pl.ds(0, rows), :], sems.at[1]),
+            ]
+        )
+        lower_ref[...] = product([own_ref], [peer_ref], weight_ref).astype(jnp.bfloat16)
+        copies += run(
+            [pltpu.make_async_copy(lower_ref, out_ref.at[0, 1 - sequence, pl.ds(rows, block - rows), :], sems.at[2])]
+        )
+        for copy in copies:
+            copy.wait()
 
 
 def finish(weight, first, first_home, near, home, own, peer):
     block, local = first.shape
-    return call(
+    return pl.pallas_call(
         finish_kernel,
-        shape(1, MB, block, local),
-        [VMEM] * 7,
-        block * weight.size,
-        weight.size * 2 + 12 * first.size,
-        out_spec=pl.BlockSpec(),
+        out_shape=shape(1, MB, block, local),
+        in_specs=[VMEM] * 7,
+        out_specs=pl.BlockSpec(memory_space=pltpu.HBM),
+        scratch_shapes=[pltpu.VMEM(own.shape, jnp.bfloat16), pltpu.SemaphoreType.DMA((3,))],
+        name="finish",
+        cost_estimate=pl.CostEstimate(
+            flops=block * weight.size, bytes_accessed=weight.size * 2 + 12 * first.size, transcendentals=0
+        ),
+        compiler_params=pltpu.CompilerParams(vmem_limit_bytes=12 << 20),
     )(weight, first, first_home, near, home, own, peer)
 
 
@@ -271,6 +296,9 @@
 
     def swap(value, axis):
         return lax.ppermute(value, axis, [(0, 1), (1, 0)])
+
+    def swap_in(value, at):
+        return lax.ppermute(value, ("chan", "section"), [(at, 2 + at), (2 + at, at)])
 
     def across(value, from_section, to_section):
         pairs = [(2 * i + from_section, 2 * ((i + half) % count) + to_section) for i in range(count)]
@@ -351,14 +379,14 @@
     gated_home = across(gated, 1, 0)
     first, signal, gating = step(gated, gated_peer, out_first, out_peer, in_last)
     sources = gathered(signal)
-    home_peer = swap(gated_home, "chan")
+    home_peer = swap_in(gated_home, 0)
     (first_home,) = project([gated_home], [home_peer], out_first, 1)
     gated, upper, lower = mixed(1, sources, gating, two_parts(block, HOMING))
 
     upper_peer = swap(upper, "chan")
     lower_home = across(lower, 1, 1)
     near_peer = lax.ppermute(gated, ("chan", "section"), [(0, 3), (2, 1)])
-    near_own = lax.ppermute(gated, "section", [(0, 1)])
+    near_own = swap(gated, "section")
     (second_upper,) = project([upper], [upper_peer], out_last, 1)
     upper_home = across(second_upper, 1, 1)
     (second_near,) = project([near_own], [near_peer], out_last, 1)

time: 90.2 us -> 90.2 us (level)
  waiting for transfers between devices: 27.1 us -> 25.2 us
  starting transfers between devices: 43.3 us -> 45.1 us
    ppermute x18, waiting for transfers between devices: 18.1 us -> 16.3 us  [swap(): return lax.ppermute(value, axis, [(0, 1), (1, 0)])]
    ppermute x1, starting transfers between devices: 2.39 us -> 3.5 us  [both_layers(): near_peer = lax.ppermute(gated, ('chan', 'section'), [(0, 3), (2, 1)])]
where the time goes in v3:
time: 90.2 us; the launch traced here: 89.8 us
  starting transfers between devices  45.1 us (50%)
  waiting for transfers between devices  25.2 us (28%)
  Pallas kernels  11.7 us (13%)
  other arithmetic  5.29 us (6%)
  local copies, waits for them, and re-layouts  2.16 us (2%)
    ppermute x18, starting transfers between devices, swap(): return lax.ppermute(value, axis, [(0, 1), (1, 0)])  28.8 us
    ppermute x18, waiting for transfers between devices, swap(): return lax.ppermute(value, axis, [(0, 1), (1, 0)])  16.3 us
    ppermute x6, waiting for transfers between devices, gathered(): lax.ppermute(signal, 'seq', [(i, i ^ apart) for i in range(count)])  8.91 us
    ppermute x6, starting transfers between devices, gathered(): lax.ppermute(signal, 'seq', [(i, i ^ apart) for i in range(count)])  7.04 us
    select_n x5, other arithmetic, pick(): return jnp.where(section == 0, zero, one)  5.29 us
    pallas_call x2, Pallas kernels, toeplitz(): pl.pallas_call(functools.partial(toeplitz_kernel, block, groups, layer),...  3.83 us
    ppermute x1, starting transfers between devices, both_layers(): near_peer = lax.ppermute(gated, ('chan', 'section'), [(0, 3), (2, 1)])  3.5 us
    ppermute x4, starting transfers between devices, across(): return lax.ppermute(value, ('seq', 'section'), pairs)  3.28 us
  transfers between devices with their start and end apart: 30, of which 8 were waited for; matrix products, arithmetic and copies ran while one was open for 6% of the time, Pallas kernels for 10%

profile of v3, /device:TPU:0, one launch (start us, length us, event | category | flops | bytes accessed | tf_op | source)
XLA Modules:
  0.0 89.8 jit_solution(11249487411794351440)
XLA Ops:
  0.0 2.1 %copy.6 = bf16[128,8,2,512]{3,1,2,0:T(8,128)(2,1)S(1)} copy(bf16[128,8,2,512]{3,2,1,0:T(2,128)(2,1)} %bitcast.14) | data formatting | bytes 4194304
  2.2 0.6 collective-permute-start.2
  2.7 0.1 collective-permute-start
  2.8 1.0 %take.1 = (bf16[256,512]{1,0:T(8,128)(2,1)S(1)}, bf16[256,512]{1,0:T(8,128)(2,1)S(1)}) custom-call(bf16[2,256,512]{2,1,0:T(8,128)(2,1)} %tokens_ref.1), custom_call_target="tpu_custom_call" | custom-call | bytes 1048576 | tf_op jit(solution)/shard_map/take/pallas_call | solution.py:119
  3.8 0.7 collective-permute-start.3
  4.6 3.0 %collective-permute-start.4 = (bf16[256,512]{1,0:T(8,128)(2,1)S(1)}, bf16[256,512]{1,0:T(8,128)(2,1)S(1)}, u32[]{:S(2)}, u32[]{:S(2)}) collective-permute-start(bf16[256,512]{1,0:T(8,128)(2,1)S(1)} %broadcast_select_fusion.4.refs_0_), channel_id=1, source_target_pairs={{0,2},{2,0},{1,3},{3,1},{4,6},{6,4},{5,7},{7,5},{8,10},{10,8},{9,1... | collective-permute-start | bytes 786440 | tf_op jit(solution)/shard_map/ppermute | solution.py:298
  7.6 0.6 collective-permute-done
  8.1 1.3 %slice_select_fusion = bf16[512,512]{1,0:T(8,128)(2,1)S(1)} fusion(bf16[1024,512]{1,0:T(8,128)(2,1)} %collective-permute-done, bf16[1,1024,512]{2,1,0:T(8,128)(2,1)} %param.8, pred[]{:T(512)S(6)} %eq.2), kind=kLoop, calls=%fused_computation.5 | loop fusion | flops 262144 | bytes 1572865 | tf_op jit(solution)/shard_map/jit(_where)/select_n | solution.py:308
  9.4 1.9 %broadcast_select_fusion = (bf16[1024,1024]{1,0:T(8,128)(2,1)S(1)}, bf16[1024,1024]{1,0:T(8,128)(2,1)S(1)}) fusion(bf16[1024,1024]{1,0:T(8,128)(2,1)} %collective-permute-done.2, bf16[1024,1024]{1,0:T(8,128)(2,1)S(1)} %bitcast.13, pred[]{:T(512)S(6)} %eq.2), kind=kLoop, calls=%fused_computation | loop fusion | flops 2097152 | bytes 8388609 | tf_op jit(solution)/shard_map/jit(_where)/select_n | solution.py:308
  11.3 0.0 copy-start
  11.3 0.0 copy-start.1
  11.3 0.6 collective-permute-done.4.refs_1_
  11.9 0.7 shard_map.55
  12.6 2.3 %collective-permute-start.13 = (bf16[512,512]{1,0:T(8,128)(2,1)S(1)}, bf16[512,512]{1,0:T(8,128)(2,1)S(1)}, u32[]{:S(2)}, u32[]{:S(2)}) collective-permute-start(bf16[512,512]{1,0:T(8,128)(2,1)S(1)} %slice_select_fusion), channel_id=1, source_target_pairs={{0,2},{2,0},{1,3},{3,1},{4,6},{6,4},{5,7},{7,5},{8,10},{10,8},{9,1... | collective-permute-start | bytes 1572872 | tf_op jit(solution)/shard_map/ppermute | solution.py:298
  14.9 1.6 %collective-permute-start.10 = (bf16[256,512]{1,0:T(8,128)(2,1)S(1)}, bf16[256,512]{1,0:T(8,128)(2,1)S(1)}, u32[]{:S(2)}, u32[]{:S(2)}) collective-permute-start(bf16[256,512]{1,0:T(8,128)(2,1)S(1)} %get-tuple-element.23.refs_0_), channel_id=1, source_target_pairs={{0,8},{4,12},{8,0},{12,4},{16,24},{20,28},{24,16},{28,20},{1,9},{5... | collective-permute-start | bytes 786440 | tf_op jit(solution)/shard_map/ppermute | solution.py:355
  16.5 1.5 %collective-permute-start.8 = (bf16[256,512]{1,0:T(8,128)(2,1)S(1)}, bf16[256,512]{1,0:T(8,128)(2,1)S(1)}, u32[]{:S(2)}, u32[]{:S(2)}) collective-permute-start(bf16[256,512]{1,0:T(8,128)(2,1)S(1)} %get-tuple-element.23.refs_0_), channel_id=1, source_target_pairs={{0,4},{4,0},{8,12},{12,8},{16,20},{20,16},{24,28},{28,24},{1,5},{5... | collective-permute-start | bytes 786440 | tf_op jit(solution)/shard_map/ppermute | solution.py:355
  18.0 0.4 collective-permute-start.5
  18.4 10.8 %collective-permute-start.1 = (bf16[4,2304]{1,0:T(4,128)(2,1)S(1)}, bf16[4,2304]{1,0:T(4,128)(2,1)S(1)}, u32[]{:S(2)}, u32[]{:S(2)}) collective-permute-start(bf16[4,2304]{1,0:T(4,128)(2,1)S(1)} %bitcast.9), channel_id=1, source_target_pairs={{0,1},{1,0},{2,3},{3,2},{4,5},{5,4},{6,7},{7,6},{8,9},{9,8},{10,11... | collective-permute-start | bytes 55304 | tf_op jit(solution)/shard_map/ppermute | solution.py:298
  29.2 0.8 collective-permute-done.1.far_ref
  30.1 0.3 collective-permute-start.7
  30.4 0.0 collective-permute-done.10.refs_4_
  30.4 1.4 %collective-permute-start.11 = (bf16[256,512]{1,0:T(8,128)(2,1)S(1)}, bf16[256,512]{1,0:T(8,128)(2,1)S(1)}, u32[]{:S(2)}, u32[]{:S(2)}) collective-permute-start(bf16[256,512]{1,0:T(8,128)(2,1)S(1)} %collective-permute-done.10.refs_4_), channel_id=1, source_target_pairs={{0,1},{1,0},{2,3},{3,2},{4,5},{5,4},{6,7},{7,6},{8,9},{9,8},{10,11... | collective-permute-start | bytes 786440 | tf_op jit(solution)/shard_map/ppermute | solution.py:298
  31.8 0.0 collective-permute-done.8.refs_2_
  31.8 2.8 %collective-permute-start.9 = (bf16[256,512]{1,0:T(8,128)(2,1)S(1)}, bf16[256,512]{1,0:T(8,128)(2,1)S(1)}, u32[]{:S(2)}, u32[]{:S(2)}) collective-permute-start(bf16[256,512]{1,0:T(8,128)(2,1)S(1)} %collective-permute-done.8.refs_2_), channel_id=1, source_target_pairs={{0,1},{1,0},{2,3},{3,2},{4,5},{5,4},{6,7},{7,6},{8,9},{9,8},{10,11... | collective-permute-start | bytes 786440 | tf_op jit(solution)/shard_map/ppermute | solution.py:298
  34.6 0.0 collective-permute-done.5.refs_0_
  34.6 0.9 %collective-permute-start.6 = (bf16[256,512]{1,0:T(8,128)(2,1)S(1)}, bf16[256,512]{1,0:T(8,128)(2,1)S(1)}, u32[]{:S(2)}, u32[]{:S(2)}) collective-permute-start(bf16[256,512]{1,0:T(8,128)(2,1)S(1)} %collective-permute-done.5.refs_0_), channel_id=1, source_target_pairs={{0,1},{1,0},{2,3},{3,2},{4,5},{5,4},{6,7},{7,6},{8,9},{9,8},{10,11... | collective-permute-start | bytes 786440 | tf_op jit(solution)/shard_map/ppermute | solution.py:298
  35.6 0.0 collective-permute-done.13
  35.6 0.0 collective-permute-start.14
  35.6 1.9 %toeplitz.2 = (bf16[4,256,1536]{2,1,0:T(8,128)(2,1)S(1)}, bf16[4,256,512]{2,1,0:T(8,128)(2,1)S(1)}) custom-call(s32[2]{0:T(128)S(1)} %copy-done.1, bf16[4,2304]{1,0:T(4,128)(2,1)S(1)} %bitcast.10, bf16[4,2304]{1,0:T(4,128)(2,1)S(1)} %collective-permute-done.1.far_ref), custom_call_target="tpu_custom_call" | custom-call | flops 83886080 | bytes 4194304 | tf_op jit(solution)/shard_map/toeplitz/pallas_call | solution.py:86
  37.5 0.0 collective-permute-done.7.refs_1_
  37.5 1.0 %shard_map.56.refs_3_ = f32[256,512]{1,0:T(8,128)S(1)} custom-call(bf16[4,256,1536]{2,1,0:T(8,128)(2,1)S(1)} %get-tuple-element.25.toeplitz_ref, bf16[256,512]{1,0:T(8,128)(2,1)S(1)} %get-tuple-element.23.refs_0_, bf16[256,512]{1,0:T(8,128)(2,1)S(1)} %collective-permute-done.7.refs_1_, bf16[256,512]{1,0:T(8,128)(2,1)S(1)} %collective-permute-done.8.refs_2_, ...), custom_call_target="tpu_custom_call" | custom-call | flops 402653184 | bytes 5767168 | tf_op jit(solution)/shard_map/pallas_call | solution.py:160
  38.5 0.4 shard_map.57.own_ref
  38.9 0.6 collective-permute-start.12
  39.5 1.7 %broadcast_select_fusion.2 = (bf16[1024,512]{1,0:T(8,128)(2,1)S(1)}, bf16[1024,512]{1,0:T(8,128)(2,1)S(1)}) fusion(bf16[1024,512]{1,0:T(8,128)(2,1)} %collective-permute-done, pred[]{:T(512)S(6)} %eq.2, bf16[1,1024,512]{2,1,0:T(8,128)(2,1)} %param.8), kind=kLoop, calls=%fused_computation.3 | loop fusion | flops 1048576 | bytes 4194305 | tf_op jit(solution)/shard_map/jit(_where)/select_n | solution.py:308
  41.2 0.5 maximum_select_fusion.out_peer_ref
  41.7 6.0 %collective-permute-done.12.peer_ref = bf16[256,512]{1,0:T(8,128)(2,1)S(1)} collective-permute-done((bf16[256,512]{1,0:T(8,128)(2,1)S(1)}, bf16[256,512]{1,0:T(8,128)(2,1)S(1)}, u32[]{:S(2)}, u32[]{:S(2)}) %collective-permute-start.12) | collective-permute-done | bytes 262176 | tf_op jit(solution)/shard_map/ppermute | solution.py:298
  47.7 1.4 %step.1 = (bf16[256,512]{1,0:T(8,128)(2,1)S(1)}, bf16[256,512]{1,0:T(8,128)(2,1)S(1)}, bf16[256,512]{1,0:T(8,128)(2,1)S(1)}) custom-call(bf16[256,512]{1,0:T(8,128)(2,1)S(1)} %shard_map.57.own_ref, bf16[256,512]{1,0:T(8,128)(2,1)S(1)} %collective-permute-done.12.peer_ref, bf16[1024,512]{1,0:T(8,128)(2,1)S(1)} %get-tuple-element.37.out_own_ref.weight_ref, ...), custom_call_target="tpu_custom_call" | custom-call | flops 1073741824 | bytes 5505024 | tf_op jit(solution)/shard_map/step/pallas_call | solution.py:222
  49.1 1.4 %collective-permute-start.20 = (bf16[256,512]{1,0:T(8,128)(2,1)S(1)}, bf16[256,512]{1,0:T(8,128)(2,1)S(1)}, u32[]{:S(2)}, u32[]{:S(2)}) collective-permute-start(bf16[256,512]{1,0:T(8,128)(2,1)S(1)} %get-tuple-element.29.refs_0_), channel_id=1, source_target_pairs={{0,4},{4,0},{8,12},{12,8},{16,20},{20,16},{24,28},{28,24},{1,5},{5... | collective-permute-start | bytes 786440 | tf_op jit(solution)/shard_map/ppermute | solution.py:355
  50.5 1.1 %collective-permute-start.22 = (bf16[256,512]{1,0:T(8,128)(2,1)S(1)}, bf16[256,512]{1,0:T(8,128)(2,1)S(1)}, u32[]{:S(2)}, u32[]{:S(2)}) collective-permute-start(bf16[256,512]{1,0:T(8,128)(2,1)S(1)} %get-tuple-element.29.refs_0_), channel_id=1, source_target_pairs={{0,8},{4,12},{8,0},{12,4},{16,24},{20,28},{24,16},{28,20},{1,9},{5... | collective-permute-start | bytes 786440 | tf_op jit(solution)/shard_map/ppermute | solution.py:355
  51.6 1.1 %collective-permute-start.17 = (bf16[256,512]{1,0:T(8,128)(2,1)S(1)}, bf16[256,512]{1,0:T(8,128)(2,1)S(1)}, u32[]{:S(2)}, u32[]{:S(2)}) collective-permute-start(bf16[256,512]{1,0:T(8,128)(2,1)S(1)} %get-tuple-element.29.refs_0_), channel_id=1, source_target_pairs={{0,12},{4,8},{8,4},{12,0},{16,28},{20,24},{24,20},{28,16},{1,13},{... | collective-permute-start | bytes 786440 | tf_op jit(solution)/shard_map/ppermute | solution.py:355
  52.7 1.3 %collective-permute-start.15 = (bf16[256,512]{1,0:T(8,128)(2,1)S(1)}, bf16[256,512]{1,0:T(8,128)(2,1)S(1)}, u32[]{:S(2)}, u32[]{:S(2)}) collective-permute-start(bf16[256,512]{1,0:T(8,128)(2,1)S(1)} %shard_map.57.own_ref), channel_id=1, source_target_pairs={{1,16},{5,20},{9,24},{13,28},{17,0},{21,4},{25,8},{29,12},{3,18},{... | collective-permute-start | bytes 786440 | tf_op jit(solution)/shard_map/ppermute | solution.py:305
  53.9 3.7 %collective-permute-start.19 = (bf16[256,512]{1,0:T(8,128)(2,1)S(1)}, bf16[256,512]{1,0:T(8,128)(2,1)S(1)}, u32[]{:S(2)}, u32[]{:S(2)}) collective-permute-start(bf16[256,512]{1,0:T(8,128)(2,1)S(1)} %get-tuple-element.29.refs_0_), channel_id=1, source_target_pairs={{0,1},{1,0},{2,3},{3,2},{4,5},{5,4},{6,7},{7,6},{8,9},{9,8},{10,11... | collective-permute-start | bytes 786440 | tf_op jit(solution)/shard_map/ppermute | solution.py:298
  57.7 0.1 collective-permute-start.21
  57.7 4.7 %collective-permute-done.22.refs_4_ = bf16[256,512]{1,0:T(8,128)(2,1)S(1)} collective-permute-done((bf16[256,512]{1,0:T(8,128)(2,1)S(1)}, bf16[256,512]{1,0:T(8,128)(2,1)S(1)}, u32[]{:S(2)}, u32[]{:S(2)}) %collective-permute-start.22) | collective-permute-done | bytes 262176 | tf_op jit(solution)/shard_map/ppermute | solution.py:355
  62.5 4.1 %collective-permute-done.17.refs_0_ = bf16[256,512]{1,0:T(8,128)(2,1)S(1)} collective-permute-done((bf16[256,512]{1,0:T(8,128)(2,1)S(1)}, bf16[256,512]{1,0:T(8,128)(2,1)S(1)}, u32[]{:S(2)}, u32[]{:S(2)}) %collective-permute-start.17) | collective-permute-done | bytes 262176 | tf_op jit(solution)/shard_map/ppermute | solution.py:355
  66.6 0.0 collective-permute-start.18
  66.6 1.9 %toeplitz.3 = (bf16[4,256,1536]{2,1,0:T(8,128)(2,1)S(1)}, bf16[4,256,512]{2,1,0:T(8,128)(2,1)S(1)}) custom-call(s32[2]{0:T(128)S(1)} %copy-done.1, bf16[4,2304]{1,0:T(4,128)(2,1)S(1)} %bitcast.11, bf16[4,2304]{1,0:T(4,128)(2,1)S(1)} %collective-permute-done.1.far_ref), custom_call_target="tpu_custom_call" | custom-call | flops 83886080 | bytes 4194304 | tf_op jit(solution)/shard_map/toeplitz/pallas_call | solution.py:86
  68.6 0.0 collective-permute-done.15.refs_0_
  68.6 2.4 %collective-permute-start.16 = (bf16[256,512]{1,0:T(8,128)(2,1)S(1)}, bf16[256,512]{1,0:T(8,128)(2,1)S(1)}, u32[]{:S(2)}, u32[]{:S(2)}) collective-permute-start(bf16[256,512]{1,0:T(8,128)(2,1)S(1)} %collective-permute-done.15.refs_0_), channel_id=1, source_target_pairs={{0,2},{2,0},{4,6},{6,4},{8,10},{10,8},{12,14},{14,12},{16,18},{18,... | collective-permute-start | bytes 786440 | tf_op jit(solution)/shard_map/ppermute | solution.py:301
  71.0 0.0 collective-permute-done.21.refs_3_
  71.1 1.0 %shard_map.59.refs_3_ = f32[256,512]{1,0:T(8,128)S(1)} custom-call(bf16[4,256,1536]{2,1,0:T(8,128)(2,1)S(1)} %get-tuple-element.31.toeplitz_ref, bf16[256,512]{1,0:T(8,128)(2,1)S(1)} %get-tuple-element.29.refs_0_, bf16[256,512]{1,0:T(8,128)(2,1)S(1)} %collective-permute-done.19.refs_1_, bf16[256,512]{1,0:T(8,128)(2,1)S(1)} %collective-permute-done.20.refs_2_, ...), custom_call_target="tpu_custom_call" | custom-call | flops 402653184 | bytes 5767168 | tf_op jit(solution)/shard_map/pallas_call | solution.py:160
  72.0 0.4 shard_map.60
  72.5 0.1 collective-permute-start.24
  72.6 3.5 %collective-permute-start.25 = (bf16[256,512]{1,0:T(8,128)(2,1)S(1)}, bf16[256,512]{1,0:T(8,128)(2,1)S(1)}, u32[]{:S(2)}, u32[]{:S(2)}) collective-permute-start(bf16[256,512]{1,0:T(8,128)(2,1)S(1)} %get-tuple-element.32), channel_id=1, source_target_pairs={{0,3},{2,1},{4,7},{6,5},{8,11},{10,9},{12,15},{14,13},{16,19},{18,... | collective-permute-start | bytes 786440 | tf_op jit(solution)/shard_map/ppermute | solution.py:388
  76.1 0.6 collective-permute-start.26
  76.7 0.7 collective-permute-start.28
  77.3 5.3 %collective-permute-done.26.refs_1_ = bf16[128,512]{1,0:T(8,128)(2,1)S(1)} collective-permute-done((bf16[128,512]{1,0:T(8,128)(2,1)S(1)}, bf16[128,512]{1,0:T(8,128)(2,1)S(1)}, u32[]{:S(2)}, u32[]{:S(2)}) %collective-permute-start.26) | collective-permute-done | bytes 131104 | tf_op jit(solution)/shard_map/ppermute | solution.py:298
  82.6 0.3 shard_map.62
  82.9 0.7 collective-permute-start.27
  83.6 1.5 %collective-permute-start.29 = (bf16[128,512]{1,0:T(8,128)(2,1)S(1)}, bf16[128,512]{1,0:T(8,128)(2,1)S(1)}, u32[]{:S(2)}, u32[]{:S(2)}) collective-permute-start(bf16[128,512]{1,0:T(8,128)(2,1)S(1)} %collective-permute-done.28.own_ref), channel_id=1, source_target_pairs={{0,2},{2,0},{1,3},{3,1},{4,6},{6,4},{5,7},{7,5},{8,10},{10,8},{9,1... | collective-permute-start | bytes 393224 | tf_op jit(solution)/shard_map/ppermute | solution.py:298
  85.2 0.4 shard_map.58.first_home_ref
  85.6 0.4 shard_map.61.near_ref
  86.1 2.9 %collective-permute-done.29.peer_ref = bf16[128,512]{1,0:T(8,128)(2,1)S(1)} collective-permute-done((bf16[128,512]{1,0:T(8,128)(2,1)S(1)}, bf16[128,512]{1,0:T(8,128)(2,1)S(1)}, u32[]{:S(2)}, u32[]{:S(2)}) %collective-permute-start.29) | collective-permute-done | bytes 131104 | tf_op jit(solution)/shard_map/ppermute | solution.py:298
  89.0 0.8 finish.1
  (19 shorter events, 0.1 us)
Async XLA Ops:
  2.2 7.2 %collective-permute-start.2 = (bf16[1024,1024]{1,0:T(8,128)(2,1)S(1)}, bf16[1024,1024]{1,0:T(8,128)(2,1)}, u32[]{:S(2)}, u32[]{:S(2)}) collective-permute-start(bf16[1024,1024]{1,0:T(8,128)(2,1)S(1)} %bitcast.12), channel_id=1, source_target_pairs={{0,1},{1,0},{2,3},{3,2},{4,5},{5,4},{6,7},{7,6},{8,9},{9,8},{10,11... | collective-permute-start | bytes 6291464 | tf_op jit(solution)/shard_map/ppermute | solution.py:298
  2.7 5.4 %collective-permute-start = (bf16[1024,512]{1,0:T(8,128)(2,1)}, bf16[1024,512]{1,0:T(8,128)(2,1)}, u32[]{:S(2)}, u32[]{:S(2)}) collective-permute-start(bf16[1024,512]{1,0:T(8,128)(2,1)} %bitcast), channel_id=1, source_target_pairs={{0,1},{1,0},{2,3},{3,2},{4,5},{5,4},{6,7},{7,6},{8,9},{9,8},{10,11... | collective-permute-start | bytes 3145736 | tf_op jit(solution)/shard_map/ppermute | solution.py:298
  3.8 0.7 collective-permute-start.3
  4.6 7.3 %collective-permute-start.4 = (bf16[256,512]{1,0:T(8,128)(2,1)S(1)}, bf16[256,512]{1,0:T(8,128)(2,1)S(1)}, u32[]{:S(2)}, u32[]{:S(2)}) collective-permute-start(bf16[256,512]{1,0:T(8,128)(2,1)S(1)} %broadcast_select_fusion.4.refs_0_), channel_id=1, source_target_pairs={{0,2},{2,0},{1,3},{3,1},{4,6},{6,4},{5,7},{7,5},{8,10},{10,8},{9,1... | collective-permute-start | bytes 786440 | tf_op jit(solution)/shard_map/ppermute | solution.py:298
  11.3 7.2 %copy-start = (bf16[1,4,2304]{2,1,0:T(4,128)(2,1)S(1)}, bf16[1,4,2304]{2,1,0:T(4,128)(2,1)}, u32[]{:S(2)}) copy-start(bf16[1,4,2304]{2,1,0:T(4,128)(2,1)} %param.7) | copy-start | bytes 55300
  11.3 24.3 %copy-start.1 = (s32[2]{0:T(128)S(1)}, s32[2]{0:T(128)}, u32[]{:S(2)}) copy-start(s32[2]{0:T(128)} %widths_ref.3) | copy-start | bytes 28
  12.6 22.9 %collective-permute-start.13 = (bf16[512,512]{1,0:T(8,128)(2,1)S(1)}, bf16[512,512]{1,0:T(8,128)(2,1)S(1)}, u32[]{:S(2)}, u32[]{:S(2)}) collective-permute-start(bf16[512,512]{1,0:T(8,128)(2,1)S(1)} %slice_select_fusion), channel_id=1, source_target_pairs={{0,2},{2,0},{1,3},{3,1},{4,6},{6,4},{5,7},{7,5},{8,10},{10,8},{9,1... | collective-permute-start | bytes 1572872 | tf_op jit(solution)/shard_map/ppermute | solution.py:298
  14.9 15.5 %collective-permute-start.10 = (bf16[256,512]{1,0:T(8,128)(2,1)S(1)}, bf16[256,512]{1,0:T(8,128)(2,1)S(1)}, u32[]{:S(2)}, u32[]{:S(2)}) collective-permute-start(bf16[256,512]{1,0:T(8,128)(2,1)S(1)} %get-tuple-element.23.refs_0_), channel_id=1, source_target_pairs={{0,8},{4,12},{8,0},{12,4},{16,24},{20,28},{24,16},{28,20},{1,9},{5... | collective-permute-start | bytes 786440 | tf_op jit(solution)/shard_map/ppermute | solution.py:355
  16.5 15.3 %collective-permute-start.8 = (bf16[256,512]{1,0:T(8,128)(2,1)S(1)}, bf16[256,512]{1,0:T(8,128)(2,1)S(1)}, u32[]{:S(2)}, u32[]{:S(2)}) collective-permute-start(bf16[256,512]{1,0:T(8,128)(2,1)S(1)} %get-tuple-element.23.refs_0_), channel_id=1, source_target_pairs={{0,4},{4,0},{8,12},{12,8},{16,20},{20,16},{24,28},{28,24},{1,5},{5... | collective-permute-start | bytes 786440 | tf_op jit(solution)/shard_map/ppermute | solution.py:355
  18.0 16.6 %collective-permute-start.5 = (bf16[256,512]{1,0:T(8,128)(2,1)S(1)}, bf16[256,512]{1,0:T(8,128)(2,1)S(1)}, u32[]{:S(2)}, u32[]{:S(2)}) collective-permute-start(bf16[256,512]{1,0:T(8,128)(2,1)S(1)} %get-tuple-element.23.refs_0_), channel_id=1, source_target_pairs={{0,12},{4,8},{8,4},{12,0},{16,28},{20,24},{24,20},{28,16},{1,13},{... | collective-permute-start | bytes 786440 | tf_op jit(solution)/shard_map/ppermute | solution.py:355
  18.4 11.6 %collective-permute-start.1 = (bf16[4,2304]{1,0:T(4,128)(2,1)S(1)}, bf16[4,2304]{1,0:T(4,128)(2,1)S(1)}, u32[]{:S(2)}, u32[]{:S(2)}) collective-permute-start(bf16[4,2304]{1,0:T(4,128)(2,1)S(1)} %bitcast.9), channel_id=1, source_target_pairs={{0,1},{1,0},{2,3},{3,2},{4,5},{5,4},{6,7},{7,6},{8,9},{9,8},{10,11... | collective-permute-start | bytes 55304 | tf_op jit(solution)/shard_map/ppermute | solution.py:298
  30.1 7.4 %collective-permute-start.7 = (bf16[256,512]{1,0:T(8,128)(2,1)S(1)}, bf16[256,512]{1,0:T(8,128)(2,1)S(1)}, u32[]{:S(2)}, u32[]{:S(2)}) collective-permute-start(bf16[256,512]{1,0:T(8,128)(2,1)S(1)} %get-tuple-element.23.refs_0_), channel_id=1, source_target_pairs={{0,1},{1,0},{2,3},{3,2},{4,5},{5,4},{6,7},{7,6},{8,9},{9,8},{10,11... | collective-permute-start | bytes 786440 | tf_op jit(solution)/shard_map/ppermute | solution.py:298
  30.4 7.1 %collective-permute-start.11 = (bf16[256,512]{1,0:T(8,128)(2,1)S(1)}, bf16[256,512]{1,0:T(8,128)(2,1)S(1)}, u32[]{:S(2)}, u32[]{:S(2)}) collective-permute-start(bf16[256,512]{1,0:T(8,128)(2,1)S(1)} %collective-permute-done.10.refs_4_), channel_id=1, source_target_pairs={{0,1},{1,0},{2,3},{3,2},{4,5},{5,4},{6,7},{7,6},{8,9},{9,8},{10,11... | collective-permute-start | bytes 786440 | tf_op jit(solution)/shard_map/ppermute | solution.py:298
  31.8 5.7 %collective-permute-start.9 = (bf16[256,512]{1,0:T(8,128)(2,1)S(1)}, bf16[256,512]{1,0:T(8,128)(2,1)S(1)}, u32[]{:S(2)}, u32[]{:S(2)}) collective-permute-start(bf16[256,512]{1,0:T(8,128)(2,1)S(1)} %collective-permute-done.8.refs_2_), channel_id=1, source_target_pairs={{0,1},{1,0},{2,3},{3,2},{4,5},{5,4},{6,7},{7,6},{8,9},{9,8},{10,11... | collective-permute-start | bytes 786440 | tf_op jit(solution)/shard_map/ppermute | solution.py:298
  34.6 3.9 %collective-permute-start.6 = (bf16[256,512]{1,0:T(8,128)(2,1)S(1)}, bf16[256,512]{1,0:T(8,128)(2,1)S(1)}, u32[]{:S(2)}, u32[]{:S(2)}) collective-permute-start(bf16[256,512]{1,0:T(8,128)(2,1)S(1)} %collective-permute-done.5.refs_0_), channel_id=1, source_target_pairs={{0,1},{1,0},{2,3},{3,2},{4,5},{5,4},{6,7},{7,6},{8,9},{9,8},{10,11... | collective-permute-start | bytes 786440 | tf_op jit(solution)/shard_map/ppermute | solution.py:298
  35.6 5.7 %collective-permute-start.14 = (bf16[512,512]{1,0:T(8,128)(2,1)S(1)}, bf16[512,512]{1,0:T(8,128)(2,1)S(1)}, u32[]{:S(2)}, u32[]{:S(2)}) collective-permute-start(bf16[512,512]{1,0:T(8,128)(2,1)S(1)} %collective-permute-done.13), channel_id=1, source_target_pairs={{0,1},{1,0},{2,3},{3,2},{4,5},{5,4},{6,7},{7,6},{8,9},{9,8},{10,11... | collective-permute-start | bytes 1572872 | tf_op jit(solution)/shard_map/ppermute | solution.py:298
  38.9 8.8 %collective-permute-start.12 = (bf16[256,512]{1,0:T(8,128)(2,1)S(1)}, bf16[256,512]{1,0:T(8,128)(2,1)S(1)}, u32[]{:S(2)}, u32[]{:S(2)}) collective-permute-start(bf16[256,512]{1,0:T(8,128)(2,1)S(1)} %shard_map.57.own_ref), channel_id=1, source_target_pairs={{0,2},{2,0},{1,3},{3,1},{4,6},{6,4},{5,7},{7,5},{8,10},{10,8},{9,1... | collective-permute-start | bytes 786440 | tf_op jit(solution)/shard_map/ppermute | solution.py:298
  49.1 8.6 %collective-permute-start.20 = (bf16[256,512]{1,0:T(8,128)(2,1)S(1)}, bf16[256,512]{1,0:T(8,128)(2,1)S(1)}, u32[]{:S(2)}, u32[]{:S(2)}) collective-permute-start(bf16[256,512]{1,0:T(8,128)(2,1)S(1)} %get-tuple-element.29.refs_0_), channel_id=1, source_target_pairs={{0,4},{4,0},{8,12},{12,8},{16,20},{20,16},{24,28},{28,24},{1,5},{5... | collective-permute-start | bytes 786440 | tf_op jit(solution)/shard_map/ppermute | solution.py:355
  50.5 12.0 %collective-permute-start.22 = (bf16[256,512]{1,0:T(8,128)(2,1)S(1)}, bf16[256,512]{1,0:T(8,128)(2,1)S(1)}, u32[]{:S(2)}, u32[]{:S(2)}) collective-permute-start(bf16[256,512]{1,0:T(8,128)(2,1)S(1)} %get-tuple-element.29.refs_0_), channel_id=1, source_target_pairs={{0,8},{4,12},{8,0},{12,4},{16,24},{20,28},{24,16},{28,20},{1,9},{5... | collective-permute-start | bytes 786440 | tf_op jit(solution)/shard_map/ppermute | solution.py:355
  51.6 15.1 %collective-permute-start.17 = (bf16[256,512]{1,0:T(8,128)(2,1)S(1)}, bf16[256,512]{1,0:T(8,128)(2,1)S(1)}, u32[]{:S(2)}, u32[]{:S(2)}) collective-permute-start(bf16[256,512]{1,0:T(8,128)(2,1)S(1)} %get-tuple-element.29.refs_0_), channel_id=1, source_target_pairs={{0,12},{4,8},{8,4},{12,0},{16,28},{20,24},{24,20},{28,16},{1,13},{... | collective-permute-start | bytes 786440 | tf_op jit(solution)/shard_map/ppermute | solution.py:355
  52.7 15.9 %collective-permute-start.15 = (bf16[256,512]{1,0:T(8,128)(2,1)S(1)}, bf16[256,512]{1,0:T(8,128)(2,1)S(1)}, u32[]{:S(2)}, u32[]{:S(2)}) collective-permute-start(bf16[256,512]{1,0:T(8,128)(2,1)S(1)} %shard_map.57.own_ref), channel_id=1, source_target_pairs={{1,16},{5,20},{9,24},{13,28},{17,0},{21,4},{25,8},{29,12},{3,18},{... | collective-permute-start | bytes 786440 | tf_op jit(solution)/shard_map/ppermute | solution.py:305
  53.9 17.1 %collective-permute-start.19 = (bf16[256,512]{1,0:T(8,128)(2,1)S(1)}, bf16[256,512]{1,0:T(8,128)(2,1)S(1)}, u32[]{:S(2)}, u32[]{:S(2)}) collective-permute-start(bf16[256,512]{1,0:T(8,128)(2,1)S(1)} %get-tuple-element.29.refs_0_), channel_id=1, source_target_pairs={{0,1},{1,0},{2,3},{3,2},{4,5},{5,4},{6,7},{7,6},{8,9},{9,8},{10,11... | collective-permute-start | bytes 786440 | tf_op jit(solution)/shard_map/ppermute | solution.py:298
  57.7 13.4 %collective-permute-start.21 = (bf16[256,512]{1,0:T(8,128)(2,1)S(1)}, bf16[256,512]{1,0:T(8,128)(2,1)S(1)}, u32[]{:S(2)}, u32[]{:S(2)}) collective-permute-start(bf16[256,512]{1,0:T(8,128)(2,1)S(1)} %collective-permute-done.20.refs_2_), channel_id=1, source_target_pairs={{0,1},{1,0},{2,3},{3,2},{4,5},{5,4},{6,7},{7,6},{8,9},{9,8},{10,11... | collective-permute-start | bytes 786440 | tf_op jit(solution)/shard_map/ppermute | solution.py:298
  62.5 8.6 %collective-permute-start.23 = (bf16[256,512]{1,0:T(8,128)(2,1)S(1)}, bf16[256,512]{1,0:T(8,128)(2,1)S(1)}, u32[]{:S(2)}, u32[]{:S(2)}) collective-permute-start(bf16[256,512]{1,0:T(8,128)(2,1)S(1)} %collective-permute-done.22.refs_4_), channel_id=1, source_target_pairs={{0,1},{1,0},{2,3},{3,2},{4,5},{5,4},{6,7},{7,6},{8,9},{9,8},{10,11... | collective-permute-start | bytes 786440 | tf_op jit(solution)/shard_map/ppermute | solution.py:298
  66.6 5.4 %collective-permute-start.18 = (bf16[256,512]{1,0:T(8,128)(2,1)S(1)}, bf16[256,512]{1,0:T(8,128)(2,1)S(1)}, u32[]{:S(2)}, u32[]{:S(2)}) collective-permute-start(bf16[256,512]{1,0:T(8,128)(2,1)S(1)} %collective-permute-done.17.refs_0_), channel_id=1, source_target_pairs={{0,1},{1,0},{2,3},{3,2},{4,5},{5,4},{6,7},{7,6},{8,9},{9,8},{10,11... | collective-permute-start | bytes 786440 | tf_op jit(solution)/shard_map/ppermute | solution.py:298
  68.6 16.6 %collective-permute-start.16 = (bf16[256,512]{1,0:T(8,128)(2,1)S(1)}, bf16[256,512]{1,0:T(8,128)(2,1)S(1)}, u32[]{:S(2)}, u32[]{:S(2)}) collective-permute-start(bf16[256,512]{1,0:T(8,128)(2,1)S(1)} %collective-permute-done.15.refs_0_), channel_id=1, source_target_pairs={{0,2},{2,0},{4,6},{6,4},{8,10},{10,8},{12,14},{14,12},{16,18},{18,... | collective-permute-start | bytes 786440 | tf_op jit(solution)/shard_map/ppermute | solution.py:301
  72.5 13.1 %collective-permute-start.24 = (bf16[256,512]{1,0:T(8,128)(2,1)S(1)}, bf16[256,512]{1,0:T(8,128)(2,1)S(1)}, u32[]{:S(2)}, u32[]{:S(2)}) collective-permute-start(bf16[256,512]{1,0:T(8,128)(2,1)S(1)} %get-tuple-element.32), channel_id=1, source_target_pairs={{0,1},{1,0},{2,3},{3,2},{4,5},{5,4},{6,7},{7,6},{8,9},{9,8},{10,11... | collective-permute-start | bytes 786440 | tf_op jit(solution)/shard_map/ppermute | solution.py:298
  72.6 13.1 %collective-permute-start.25 = (bf16[256,512]{1,0:T(8,128)(2,1)S(1)}, bf16[256,512]{1,0:T(8,128)(2,1)S(1)}, u32[]{:S(2)}, u32[]{:S(2)}) collective-permute-start(bf16[256,512]{1,0:T(8,128)(2,1)S(1)} %get-tuple-element.32), channel_id=1, source_target_pairs={{0,3},{2,1},{4,7},{6,5},{8,11},{10,9},{12,15},{14,13},{16,19},{18,... | collective-permute-start | bytes 786440 | tf_op jit(solution)/shard_map/ppermute | solution.py:388
  76.1 6.6 %collective-permute-start.26 = (bf16[128,512]{1,0:T(8,128)(2,1)S(1)}, bf16[128,512]{1,0:T(8,128)(2,1)S(1)}, u32[]{:S(2)}, u32[]{:S(2)}) collective-permute-start(bf16[128,512]{1,0:T(8,128)(2,1)S(1)} %get-tuple-element.33.refs_0_), channel_id=1, source_target_pairs={{0,2},{2,0},{1,3},{3,1},{4,6},{6,4},{5,7},{7,5},{8,10},{10,8},{9,1... | collective-permute-start | bytes 393224 | tf_op jit(solution)/shard_map/ppermute | solution.py:298
  76.7 6.9 %collective-permute-start.28 = (bf16[128,512]{1,0:T(8,128)(2,1)S(1)}, bf16[128,512]{1,0:T(8,128)(2,1)S(1)}, u32[]{:S(2)}, u32[]{:S(2)}) collective-permute-start(bf16[128,512]{1,0:T(8,128)(2,1)S(1)} %get-tuple-element.34), channel_id=1, source_target_pairs={{1,17},{5,21},{9,25},{13,29},{17,1},{21,5},{25,9},{29,13},{3,19},{... | collective-permute-start | bytes 393224 | tf_op jit(solution)/shard_map/ppermute | solution.py:305
  82.9 3.2 %collective-permute-start.27 = (bf16[128,512]{1,0:T(8,128)(2,1)S(1)}, bf16[128,512]{1,0:T(8,128)(2,1)S(1)}, u32[]{:S(2)}, u32[]{:S(2)}) collective-permute-start(bf16[128,512]{1,0:T(8,128)(2,1)S(1)} %shard_map.62), channel_id=1, source_target_pairs={{1,17},{5,21},{9,25},{13,29},{17,1},{21,5},{25,9},{29,13},{3,19},{... | collective-permute-start | bytes 393224 | tf_op jit(solution)/shard_map/ppermute | solution.py:305
  83.6 5.4 %collective-permute-start.29 = (bf16[128,512]{1,0:T(8,128)(2,1)S(1)}, bf16[128,512]{1,0:T(8,128)(2,1)S(1)}, u32[]{:S(2)}, u32[]{:S(2)}) collective-permute-start(bf16[128,512]{1,0:T(8,128)(2,1)S(1)} %collective-permute-done.28.own_ref), channel_id=1, source_target_pairs={{0,2},{2,0},{1,3},{3,1},{4,6},{6,4},{5,7},{7,5},{8,10},{10,8},{9,1... | collective-permute-start | bytes 393224 | tf_op jit(solution)/shard_map/ppermute | solution.py:298
